TPU v7x, 256 devices: a whole 4x4x8 slice. The times are simulated.
256 devices in a mesh: row: 64 (over y, z, core), col: 4 (over x).
Axes of the slice: x: 4, y: 4, z: 8, core: 2. Of those that a mesh axis runs over, the one named last changes fastest.
Arguments:
- features: bfloat16 [65536, 256], P('row', 'col'), may hold values from -600 to 600
- tile_vals: bfloat16 [10240, 128, 128], P('row'), may hold values from -0.125 to 0.125
- tile_rows: int32 [64, 160], P('row'), may hold values from 0 to 7
- tile_srcs: int32 [64, 160], P('row'), may hold values from 0 to 135, as said below
- tile_count: int32 [64], P('row'), may hold values from 20 to 160, as said below
- needed: int32 [64, 64, 2], P('row'), may hold values from 0 to 7, as said below
- hop_noise: float32 [2, 65536, 256], P(None, 'row', 'col'), may hold values from -0.24 to 0.24
- enc_weight: bfloat16 [3, 256, 256], replicated, may hold values from -3.59375 to 3.59375
Outputs:
- encoded: bfloat16 [65536, 256], P('row', 'col')
Inputs may be any that keep to these rules, and one draw needn't show every extreme that they name: `tile_count`: some row index has exactly 160 live slots; slots at or beyond a row index's count are ignored. `tile_srcs`: A value s below 8 names the row index's own block s; otherwise s = 8 + o * 2 + c names entry c of needed for owner o, and o is never the row index itself. needed[d, o, :] are 2 distinct block indices among owner o's 8 blocks.
All inputs are finite; a program needn't handle non-finite values.
Results may differ from a plain program's by a relative error of at most 0.0053.
Values may be sent and summed in bfloat16 or wider, within the bound.
No kernel may reach another device: no remote copies, remote signals or barrier semaphores. Data moves between devices by JAX's collectives and lax.ppermute only.
A program may use at most 64 MiB of HBM per device.

v0:
```python
import functools

import jax
import jax.numpy as jnp
import numpy as np
from jax import lax
from jax.experimental import pallas as pl
from jax.experimental.pallas import tpu as pltpu
from jax.sharding import Mesh, PartitionSpec as P

BLK = 128
BPD = 8
TPD = 160
PAIRS = BPD // 2
HOPS = 2
NY, NZ, NC, NX = 4, 8, 2, 4
WIDTH = 64
GROUP = 4
BUCKETS = 2 * BPD
MAXG = TPD // GROUP + BUCKETS
SLOTS = MAXG * GROUP
SHIFTS = (0, 2, 1, 3)
DEPTH = 4
FULL = 63 << 20
MOST = 65_300_000
ROOM = 63_600_000
EPS = 1e-06
bf16 = jnp.bfloat16
f32 = jnp.float32
VMEM = pltpu.VMEM
SMEM = pltpu.SMEM
HBM = pltpu.HBM
DMA = pltpu.SemaphoreType.DMA


def lane_low(shape):
    return lax.broadcasted_iota(jnp.int32, shape, len(shape) - 1) < WIDTH


def pair_squares(pair_values):
    total = jnp.zeros((BPD, BLK), f32)
    row = lax.broadcasted_iota(jnp.int32, (BPD, BLK), 0)
    half = lax.broadcasted_iota(jnp.int32, (BPD, BLK), 1) // WIDTH
    for p in range(PAIRS):
        v = pair_values[p]
        pick = jnp.where(row == 2 * p + half, 1.0, 0.0).astype(f32)
        total = total + lax.dot_general(
            pick, v * v, (((1,), (1,)), ((), ())),
            precision=lax.Precision.HIGHEST, preferred_element_type=f32,
        )
    return total


def row_scale(total):
    return (1.0 / jnp.sqrt(total + EPS)).T


def pair_scale(columns, p):
    return jnp.where(
        lane_low((BLK, BLK)),
        jnp.broadcast_to(columns[:, 2 * p : 2 * p + 1], (BLK, BLK)),
        jnp.broadcast_to(columns[:, 2 * p + 1 : 2 * p + 2], (BLK, BLK)),
    )


def swap_halves(v):
    return pltpu.roll(v, WIDTH, 1)


def stacked_pair(ref, p):
    first = ref[:, (2 * p) * BLK : (2 * p + 1) * BLK].astype(f32)
    second = ref[:, (2 * p + 1) * BLK : (2 * p + 2) * BLK].astype(f32)
    return jnp.concatenate([first, second], axis=0)


def pack_kernel(feat_ref, out_ref, sq_ref):
    rows = []
    for p in range(PAIRS):
        stacked = stacked_pair(feat_ref, p)
        out_ref[p] = stacked.T.astype(bf16)
        squares = stacked * stacked
        rows.append(jnp.sum(squares[:WIDTH], axis=0, keepdims=True))
        rows.append(jnp.sum(squares[WIDTH:], axis=0, keepdims=True))
    sq_ref[...] = jnp.concatenate(rows, axis=0)


def norm_kernel(hop, raw_ref, sq_ref, *rest):
    columns = row_scale(sq_ref[...])
    before_ref = rest[0] if hop else None
    out_ref, own_ref, buf, sem = rest[-4:]
    copies = []
    for p in range(PAIRS):
        v = (raw_ref[p].astype(f32) * pair_scale(columns, p)).astype(bf16)
        buf[p] = v
        own_ref[hop, p] = v
    for z in range(NZ):
        copy = pltpu.make_async_copy(buf, out_ref.at[z], sem.at[z])
        copy.start()
        copies.append(copy)
    if hop:
        own_ref[0:hop] = before_ref[...]
    for copy in copies:
        copy.wait()


def pick_kernel(me_ref, idx_ref, z_ref, out_ref, slots, buf, sem):
    for z in range(NZ):
        for p in range(PAIRS):
            v = z_ref[z, p]
            slots[z * BPD + p] = v
            slots[z * BPD + PAIRS + p] = jnp.concatenate([v[:, WIDTH:], v[:, :WIDTH]], axis=1)
    mask = lane_low((BLK, BLK))
    mine = me_ref[0] * NC + me_ref[2]
    copies = []
    for dest in range(NY * NC):
        for z in range(NZ):
            i = dest * NZ + z
            buf[i] = jnp.where(mask, slots[idx_ref[2 * i]], slots[idx_ref[2 * i + 1]])

        @pl.when(mine == dest)
        def _():
            buf[dest * NZ + me_ref[1]] = jnp.zeros((BLK, BLK), bf16)

        copy = pltpu.make_async_copy(
            buf.at[pl.ds(dest * NZ, NZ)], out_ref.at[pl.ds(dest * NZ, NZ)], sem.at[dest]
        )
        copy.start()
        copies.append(copy)
    for copy in copies:
        copy.wait()


def order_kernel(me_ref, rows_ref, srcs_ref, count_ref, tile_ref, slab_ref, into_ref, groups_ref, fill, begin):
    count = count_ref[0]
    empty = (me_ref[0] * NC + me_ref[2]) * NZ + me_ref[1]

    @pl.loop(0, SLOTS // 8)
    def _(i):
        for j in range(8):
            tile_ref[i * 8 + j] = 0
            tile_ref[SLOTS + i * 8 + j] = 0
            slab_ref[i * 8 + j] = PAIRS
            slab_ref[SLOTS + i * 8 + j] = empty

    @pl.loop(0, 2 * MAXG)
    def _(i):
        into_ref[i] = 0

    for b in range(2 * BUCKETS):
        fill[b] = 0

    def bucket_of(t):
        s = srcs_ref[t]
        return jnp.where(s < BPD, 0, BUCKETS) + rows_ref[t] * 2 + s % 2

    @pl.loop(0, count)
    def _(t):
        b = bucket_of(t)
        fill[b] = fill[b] + 1

    for kind in range(2):
        def place(b, group):
            size = (fill[kind * BUCKETS + b] + GROUP - 1) // GROUP
            begin[kind * BUCKETS + b] = (kind * MAXG + group) * GROUP

            @pl.loop(0, size)
            def _(i):
                into_ref[kind * MAXG + group + i] = b

            return group + size

        groups_ref[kind] = lax.fori_loop(0, BUCKETS, place, jnp.int32(0))

    @pl.loop(0, count)
    def _(t):
        b = bucket_of(t)
        at = begin[b]
        begin[b] = at + 1
        s = srcs_ref[t]
        o = (s - BPD) // 2
        y = o // (NZ * NC)
        z = (o // NC) % NZ
        k = o % NC
        tile_ref[at] = t
        slab_ref[at] = jnp.where(s < BPD, s // 2, (y * NC + k) * NZ + z)


def add_groups(kind, tile_ref, slab_ref, into_ref, groups_ref, tiles_ref, src, acc, ring, sem):
    steps = (groups_ref[kind] + 1) // 2

    def copies(step):
        slot = step % DEPTH
        first = (kind * MAXG + 2 * step) * GROUP
        return [
            pltpu.make_async_copy(tiles_ref.at[tile_ref[first + j]], ring.at[slot, j], sem.at[slot, j])
            for j in range(2 * GROUP)
        ]

    def begin(step):
        @pl.when(step < steps)
        def _():
            for copy in copies(step):
                copy.start()

    def run(step, carry):
        slot = step % DEPTH
        group = kind * MAXG + 2 * step
        for copy in copies(step):
            copy.wait()
        parts = []
        for h in range(2):
            left = jnp.concatenate([ring[slot, h * GROUP + j] for j in range(GROUP)], axis=1)
            right = jnp.concatenate([src[slab_ref[(group + h) * GROUP + j]] for j in range(GROUP)], axis=0)
            parts.append(jnp.dot(left, right, preferred_element_type=f32))
        for h in range(2):
            acc[into_ref[group + h]] += parts[h]
        begin(step + DEPTH)
        return carry

    return begin, lambda: lax.fori_loop(0, steps, run, 0)


def own_kernel(hop, tile_ref, slab_ref, into_ref, groups_ref, tiles_ref, own_ref, acc_ref, src, ring, sem):
    begin, run = add_groups(0, tile_ref, slab_ref, into_ref, groups_ref, tiles_ref, src, acc_ref, ring, sem)
    for step in range(DEPTH):
        begin(step)
    acc_ref[...] = jnp.zeros_like(acc_ref)
    src[0:PAIRS] = own_ref[hop]
    src[PAIRS] = jnp.zeros((BLK, BLK), bf16)
    run()


def far_kernel(hop, tile_ref, slab_ref, into_ref, groups_ref, tiles_ref, got_ref, part_ref, noise_ref, *rest):
    last = hop == HOPS - 1
    if last:
        out_ref, acc, noise, ring, sem, load = rest
    else:
        out_ref, sq_ref, acc, noise, ring, sem, load = rest
    begin, run = add_groups(1, tile_ref, slab_ref, into_ref, groups_ref, tiles_ref, got_ref, acc, ring, sem)
    for step in range(DEPTH):
        begin(step)
    noise_copy = pltpu.make_async_copy(noise_ref.at[hop], noise, load)
    noise_copy.start()
    acc[...] = part_ref[...]
    run()
    noise_copy.wait()
    mask = lane_low((BLK, BLK))
    pairs = []
    for p in range(PAIRS):
        u = stacked_pair(noise, p).T + jnp.where(
            mask,
            acc[4 * p] + swap_halves(acc[4 * p + 1]),
            swap_halves(acc[4 * p + 2]) + acc[4 * p + 3],
        )
        pairs.append(u)
        if last:
            out_ref[p * BLK : (p + 1) * BLK] = u.astype(bf16)
        else:
            out_ref[p] = u
    total = pair_squares(pairs)
    if last:
        hi = total.astype(bf16).astype(f32)
        mid = (total - hi).astype(bf16).astype(f32)
        lo = total - hi - mid
        out_ref[PAIRS * BLK : PAIRS * BLK + 16] = jnp.concatenate([hi, mid], axis=0).astype(bf16)
        out_ref[PAIRS * BLK + 16 : PAIRS * BLK + 32] = jnp.concatenate([lo, jnp.zeros_like(lo)], axis=0).astype(bf16)
    else:
        sq_ref[...] = total


def early_kernel(x_ref, w_ref, *refs):
    h_refs, out_ref = refs[:-1], refs[-1]
    for p in range(PAIRS):
        total = jnp.zeros((BLK, BLK), f32)
        for k in range(HOPS):
            for j, shift in enumerate(SHIFTS):
                source = (x_ref[0] + NX - shift) % NX
                total = total + jnp.dot(h_refs[j][k, p], w_ref[k, source], preferred_element_type=f32)
        out_ref[p] = total


def final_kernel(x_ref, w_ref, early_ref, *refs):
    got_refs, out_ref = refs[:-1], refs[-1]
    total = jnp.zeros((BPD, BLK), f32)
    for got_ref in got_refs:
        a = got_ref[PAIRS * BLK : PAIRS * BLK + 16].astype(f32)
        b = got_ref[PAIRS * BLK + 16 : PAIRS * BLK + 32].astype(f32)
        total = total + (a[:BPD] + a[BPD:] + b[:BPD])
    columns = row_scale(total)
    for p in range(PAIRS):
        raw = jnp.zeros((BLK, BLK), f32)
        for j, shift in enumerate(SHIFTS):
            source = (x_ref[0] + NX - shift) % NX
            raw = raw + jnp.dot(got_refs[j][p * BLK : (p + 1) * BLK], w_ref[HOPS, source], preferred_element_type=f32)
        v = (early_ref[p] + raw * pair_scale(columns, p)).T
        out_ref[:, (2 * p) * BLK : (2 * p + 1) * BLK] = v[:WIDTH].astype(bf16)
        out_ref[:, (2 * p + 1) * BLK : (2 * p + 2) * BLK] = v[WIDTH:].astype(bf16)


def whole(space=VMEM):
    return pl.BlockSpec(memory_space=space)


def call(kernel, name, in_specs, outs, scratch=(), limit=24 << 20, flops=1 << 20, moved=1 << 20):
    shapes = [jax.ShapeDtypeStruct(dims, kind) for dims, kind, _ in outs]
    specs = [whole(space) for _, _, space in outs]
    single = len(outs) == 1
    return pl.pallas_call(
        kernel,
        name=name,
        out_shape=shapes[0] if single else shapes,
        in_specs=in_specs,
        out_specs=specs[0] if single else specs,
        scratch_shapes=list(scratch),
        compiler_params=pltpu.CompilerParams(vmem_limit_bytes=limit),
        cost_estimate=pl.CostEstimate(flops=flops, bytes_accessed=moved, transcendentals=0),
    )


def shift_by(value, axis, shift):
    size = lax.axis_size(axis)
    return lax.ppermute(value, axis, [(i, (i + shift) % size) for i in range(size)])


def shards(features, tile_vals, tile_rows, tile_srcs, tile_count, needed, hop_noise, enc_weight):
    me = jnp.stack([lax.axis_index("y"), lax.axis_index("z"), lax.axis_index("core")]).astype(jnp.int32)
    x_index = lax.axis_index("x").astype(jnp.int32)
    x_only = x_index.reshape(1)
    noise = hop_noise.transpose(0, 2, 1)

    packed, squares = call(
        pack_kernel, "pack", [whole()],
        [((PAIRS, BLK, BLK), bf16, VMEM), ((BPD, BLK), f32, VMEM)],
    )(features.T)
    packed, squares, needed, rows, srcs, count, enc_weight, tile_vals = lax.optimization_barrier(
        (packed, squares, needed.reshape(-1), tile_rows.reshape(-1), tile_srcs.reshape(-1), tile_count, enc_weight, tile_vals)
    )

    weights = lax.dynamic_slice_in_dim(enc_weight, x_index * WIDTH, WIDTH, axis=2).reshape(HOPS + 1, NX, WIDTH, WIDTH)
    nothing = jnp.zeros_like(weights)
    weights = jnp.concatenate(
        [jnp.concatenate([weights, nothing], axis=-1), jnp.concatenate([nothing, weights], axis=-1)], axis=-2
    )
    lists = call(
        order_kernel, "order", [whole(SMEM)] * 4,
        [((2 * SLOTS,), jnp.int32, SMEM), ((2 * SLOTS,), jnp.int32, SMEM), ((2 * MAXG,), jnp.int32, SMEM), ((2,), jnp.int32, SMEM)],
        [SMEM((2 * BUCKETS,), jnp.int32), SMEM((2 * BUCKETS,), jnp.int32)],
    )(me, rows, srcs, count)
    table = None
    for hop in range(HOPS):
        last = hop == HOPS - 1
        total = lax.psum(squares, "x")
        before = [owned] if hop else []
        packed, owned = call(
            functools.partial(norm_kernel, hop), "norm", [whole()] * (2 + hop),
            [((NZ, PAIRS, BLK, BLK), bf16, HBM), ((hop + 1, PAIRS, BLK, BLK), bf16, VMEM)],
            [VMEM((PAIRS, BLK, BLK), bf16), DMA((NZ,))],
            limit=MOST,
        )(packed, total, *before)
        if last:
            spread = [owned] + [shift_by(owned, "x", shift) for shift in SHIFTS[1:]]
        along = lax.all_to_all(packed, "z", 0, 0, tiled=True)
        if table is None:
            needed, owned = lax.optimization_barrier((needed, owned))
            asked = lax.all_gather(needed, ("y", "core"), axis=0).reshape(NY * NC, NY, NZ, NC, 2)
            asked = lax.dynamic_slice(asked, (0, me[0], 0, me[2], 0), (NY * NC, 1, NZ, 1, 2)).reshape(NY * NC, NZ, 2)
            odd = (asked % 2) ^ jnp.arange(2, dtype=jnp.int32)
            table = (jnp.arange(NZ, dtype=jnp.int32)[:, None] * BPD + asked // 2 + PAIRS * odd).reshape(-1)
        picked = call(
            pick_kernel, "pick", [whole(SMEM)] * 2 + [whole()],
            [((NY * NC * NZ, BLK, BLK), bf16, HBM)],
            [VMEM((NZ * BPD, BLK, BLK), bf16), VMEM((NY * NC * NZ, BLK, BLK), bf16), DMA((NY * NC,))],
            limit=MOST,
        )(me, table, along)
        got = lax.all_to_all(picked, ("y", "core"), 0, 0, tiled=True)
        ring = [VMEM((DEPTH, 2 * GROUP, BLK, BLK), bf16), DMA((DEPTH, 2 * GROUP))]
        part = call(
            functools.partial(own_kernel, hop), "own", [whole(SMEM)] * 4 + [whole(HBM), whole()], [((BUCKETS, BLK, BLK), f32, VMEM)],
            [VMEM((PAIRS + 1, BLK, BLK), bf16)] + ring,
            limit=FULL, flops=TPD * 2 * BLK**3, moved=4 << 20,
        )(*lists, tile_vals, owned)
        if last:
            early = call(
                early_kernel, "early", [whole(SMEM)] + [whole()] * (1 + NX), [((PAIRS, BLK, BLK), f32, VMEM)]
            )(x_only, weights, *spread)
        if last:
            outs = [((PAIRS * BLK + 32, BLK), bf16, VMEM)]
        else:
            outs = [((PAIRS, BLK, BLK), f32, VMEM), ((BPD, BLK), f32, VMEM)]
        result = call(
            functools.partial(far_kernel, hop), "far", [whole(SMEM)] * 4 + [whole(HBM), whole(), whole(), whole(HBM)], outs,
            [
                VMEM((BUCKETS, BLK, BLK), f32),
                VMEM((WIDTH, BPD * BLK), f32),
            ] + ring + [DMA(())],
            limit=ROOM, flops=TPD * 2 * BLK**3, moved=8 << 20,
        )(*lists, tile_vals, got, part, noise)
        if not last:
            packed, squares = result
    tails = [result] + [shift_by(result, "x", shift) for shift in SHIFTS[1:]]
    return call(
        final_kernel, "final", [whole(SMEM)] + [whole()] * (2 + NX), [((WIDTH, BPD * BLK), bf16, VMEM)]
    )(x_only, weights, early, *tails).T


def solution(mesh):
    grid = Mesh(np.array(mesh.devices).reshape(NY, NZ, NC, NX), ("y", "z", "core", "x"))
    row = ("y", "z", "core")
    in_specs = (
        P(row, "x"),
        P(row, None, None),
        P(row, None),
        P(row, None),
        P(row),
        P(row, None, None),
        P(None, row, "x"),
        P(),
    )
    return jax.shard_map(shards, mesh=grid, in_specs=in_specs, out_specs=P(row, "x"), check_vma=False)
```

profile of v0, /device:TPU:1, one launch (start us, length us, event | category | flops | bytes accessed | tf_op | source)
XLA Modules:
  0.0 190.9 jit_solution(14751460321229875646)
XLA Ops:
  0.0 1.0 copy-done.4
  1.7 0.8 copy.14
  2.6 9.9 %psum.14.sq_ref = f32[8,128]{1,0:T(8,128)} all-reduce(f32[8,128]{1,0:T(8,128)S(1)} %get-tuple-element.40), channel_id=1, replica_groups=mesh['y'=4,'z'=8,'core'=2,'x'=4] {'x'}, use_global_device_ids=true, to_apply=%region_0.0 | all-reduce | flops 1024 | bytes 8192 | tf_op jit(solution)/shard_map/psum | solution.py:352
  12.5 3.0 %norm.2 = (bf16[8,4,128,128]{3,2,1,0:T(8,128)(2,1)}, bf16[1,4,128,128]{3,2,1,0:T(8,128)(2,1)}) custom-call(bf16[4,128,128]{2,1,0:T(8,128)(2,1)} %copy-done.5, f32[8,128]{1,0:T(8,128)} %psum.14.sq_ref), custom_call_target="tpu_custom_call" | custom-call | flops 1048576 | bytes 1048576 | tf_op jit(solution)/shard_map/norm/pallas_call | solution.py:354
  15.5 8.2 %all-to-all-start = ((bf16[8,4,128,128]{3,2,1,0:T(8,128)(2,1)}), bf16[8,4,128,128]{3,2,1,0:T(8,128)(2,1)S(1)}, u32[]{:S(2)}, u32[]{:S(2)}) async-start(bf16[8,4,128,128]{3,2,1,0:T(8,128)(2,1)} %get-tuple-element.43), calls=%async_computation | async-start | bytes 2097152 | tf_op jit(solution)/shard_map/all_to_all | solution.py:362
  23.9 13.6 %all-gather.1 = s32[8,1,128]{2,1,0:T(1,128)S(1)} all-gather(s32[1,1,128]{2,1,0:T(1,128)S(1)} %bitcast.23), channel_id=2, replica_groups=mesh['y'=4,'z'=8,'core'=2,'x'=4] {'y','core'}, dimensions={0}, use_global_device_ids=true | all-gather | bytes 4608 | tf_op jit(solution)/shard_map/all_gather | solution.py:365
  39.3 11.5 %all-to-all-done.z_ref = bf16[8,4,128,128]{3,2,1,0:T(8,128)(2,1)S(1)} async-done(((bf16[8,4,128,128]{3,2,1,0:T(8,128)(2,1)}), bf16[8,4,128,128]{3,2,1,0:T(8,128)(2,1)S(1)}, u32[]{:S(2)}, u32[]{:S(2)}) %all-to-all-start) | async-done | bytes 1048608 | tf_op jit(solution)/shard_map/all_to_all | solution.py:362
  50.7 1.0 copy-done.13
  51.7 3.1 %pick.2 = bf16[64,128,128]{2,1,0:T(8,128)(2,1)} custom-call(s32[3]{0:T(128)} %pad_add_fusion.me_ref, s32[128]{0:T(128)} %multiply_add_fusion.idx_ref, bf16[8,4,128,128]{3,2,1,0:T(8,128)(2,1)} %copy-done.13), custom_call_target="tpu_custom_call" | custom-call | flops 1048576 | bytes 1048576 | tf_op jit(solution)/shard_map/pick/pallas_call | solution.py:369
  54.9 7.2 %all-to-all-start.1 = ((bf16[64,128,128]{2,1,0:T(8,128)(2,1)}), bf16[64,128,128]{2,1,0:T(8,128)(2,1)}, u32[]{:S(2)}, u32[]{:S(2)}) async-start(bf16[64,128,128]{2,1,0:T(8,128)(2,1)} %pick.2), calls=%async_computation.1 | async-start | bytes 4194304 | tf_op jit(solution)/shard_map/all_to_all | solution.py:375
  62.7 5.1 %order.1 = (s32[448]{0:T(512)S(1)}, s32[448]{0:T(512)S(1)}, s32[112]{0:T(128)S(1)}, s32[2]{0:T(128)S(1)}) custom-call(s32[3]{0:T(128)S(1)} %copy-done.10, s32[160]{0:T(256)S(1)} %bitcast.17, s32[160]{0:T(256)S(1)} %bitcast.18, s32[1]{0:T(128)S(6)} %copy.17.count_ref), custom_call_target="tpu_custom_call" | custom-call | flops 1048576 | bytes 1048576 | tf_op jit(solution)/shard_map/order/pallas_call | solution.py:344
  70.2 4.1 %own.2.part_ref = f32[16,128,128]{2,1,0:T(8,128)} custom-call(s32[448]{0:T(512)} %copy-done.6, s32[448]{0:T(512)} %copy-done.7, s32[112]{0:T(128)} %copy-done.8, s32[2]{0:T(128)} %copy-done.9, bf16[160,128,128]{2,1,0:T(8,128)(2,1)} %tiles_ref.3, bf16[1,4,128,128]{3,2,1,0:T(8,128)(2,1)} %get-tuple-element.44.own_ref.rest_0_), custom_call_target="tpu_custom_call" | custom-call | flops 671088640 | bytes 4194304 | tf_op jit(solution)/shard_map/own/pallas_call | solution.py:377
  74.3 14.0 %all-to-all-done.1.got_ref = bf16[64,128,128]{2,1,0:T(8,128)(2,1)} async-done(((bf16[64,128,128]{2,1,0:T(8,128)(2,1)}), bf16[64,128,128]{2,1,0:T(8,128)(2,1)}, u32[]{:S(2)}, u32[]{:S(2)}) %all-to-all-start.1) | async-done | bytes 2097184 | tf_op jit(solution)/shard_map/all_to_all | solution.py:375
  88.4 6.6 %far.2 = (f32[4,128,128]{2,1,0:T(8,128)}, f32[8,128]{1,0:T(8,128)}) custom-call(s32[448]{0:T(512)} %copy-done.6, s32[448]{0:T(512)} %copy-done.7, s32[112]{0:T(128)} %copy-done.8, s32[2]{0:T(128)} %copy-done.9, bf16[160,128,128]{2,1,0:T(8,128)(2,1)} %tiles_ref.3, bf16[64,128,128]{2,1,0:T(8,128)(2,1)} %all-to-all-done.1.got_ref, ...), custom_call_target="tpu_custom_call" | custom-call | flops 671088640 | bytes 8388608 | tf_op jit(solution)/shard_map/far/pallas_call | solution.py:390
  94.9 6.7 %psum.15.sq_ref = f32[8,128]{1,0:T(8,128)} all-reduce(f32[8,128]{1,0:T(8,128)} %get-tuple-element.46), channel_id=1, replica_groups=mesh['y'=4,'z'=8,'core'=2,'x'=4] {'x'}, use_global_device_ids=true, to_apply=%region_1.2 | all-reduce | flops 1024 | bytes 8192 | tf_op jit(solution)/shard_map/psum | solution.py:352
  101.7 3.1 %norm.3 = (bf16[8,4,128,128]{3,2,1,0:T(8,128)(2,1)}, bf16[2,4,128,128]{3,2,1,0:T(8,128)(2,1)}) custom-call(f32[4,128,128]{2,1,0:T(8,128)} %get-tuple-element.45.raw_ref, f32[8,128]{1,0:T(8,128)} %psum.15.sq_ref, bf16[1,4,128,128]{3,2,1,0:T(8,128)(2,1)} %get-tuple-element.44.own_ref.rest_0_), custom_call_target="tpu_custom_call" | custom-call | flops 1048576 | bytes 1048576 | tf_op jit(solution)/shard_map/norm/pallas_call | solution.py:354
  104.8 30.7 %all_to_all.20.z_ref = bf16[8,4,128,128]{3,2,1,0:T(8,128)(2,1)} all-to-all(bf16[8,4,128,128]{3,2,1,0:T(8,128)(2,1)} %get-tuple-element.48), channel_id=1, replica_groups=mesh['y'=4,'z'=8,'core'=2,'x'=4] {'z'}, dimensions={0} | all-to-all | bytes 2097152 | tf_op jit(solution)/shard_map/all_to_all | solution.py:362
  135.5 3.1 %pick.3 = bf16[64,128,128]{2,1,0:T(8,128)(2,1)} custom-call(s32[3]{0:T(128)} %pad_add_fusion.me_ref, s32[128]{0:T(128)} %multiply_add_fusion.idx_ref, bf16[8,4,128,128]{3,2,1,0:T(8,128)(2,1)} %all_to_all.20.z_ref), custom_call_target="tpu_custom_call" | custom-call | flops 1048576 | bytes 1048576 | tf_op jit(solution)/shard_map/pick/pallas_call | solution.py:369
  138.7 7.7 %all-to-all-start.3 = ((bf16[64,128,128]{2,1,0:T(8,128)(2,1)}), bf16[64,128,128]{2,1,0:T(8,128)(2,1)}, u32[]{:S(2)}, u32[]{:S(2)}) async-start(bf16[64,128,128]{2,1,0:T(8,128)(2,1)} %pick.3), calls=%async_computation.3 | async-start | bytes 4194304 | tf_op jit(solution)/shard_map/all_to_all | solution.py:375
  146.3 0.9 collective-permute-start
  147.2 1.1 collective-permute-start.1
  148.3 1.8 collective-permute-start.2
  150.1 4.2 %own.3.part_ref = f32[16,128,128]{2,1,0:T(8,128)} custom-call(s32[448]{0:T(512)} %copy-done.6, s32[448]{0:T(512)} %copy-done.7, s32[112]{0:T(128)} %copy-done.8, s32[2]{0:T(128)} %copy-done.9, bf16[160,128,128]{2,1,0:T(8,128)(2,1)} %tiles_ref.3, bf16[2,4,128,128]{3,2,1,0:T(8,128)(2,1)} %get-tuple-element.47.refs_0_.own_ref), custom_call_target="tpu_custom_call" | custom-call | flops 671088640 | bytes 4194304 | tf_op jit(solution)/shard_map/own/pallas_call | solution.py:377
  154.3 18.3 %all-to-all-done.3.got_ref = bf16[64,128,128]{2,1,0:T(8,128)(2,1)} async-done(((bf16[64,128,128]{2,1,0:T(8,128)(2,1)}), bf16[64,128,128]{2,1,0:T(8,128)(2,1)}, u32[]{:S(2)}, u32[]{:S(2)}) %all-to-all-start.3) | async-done | bytes 2097184 | tf_op jit(solution)/shard_map/all_to_all | solution.py:375
  172.6 6.6 %far.3.refs_0_ = bf16[544,128]{1,0:T(8,128)(2,1)} custom-call(s32[448]{0:T(512)} %copy-done.6, s32[448]{0:T(512)} %copy-done.7, s32[112]{0:T(128)} %copy-done.8, s32[2]{0:T(128)} %copy-done.9, bf16[160,128,128]{2,1,0:T(8,128)(2,1)} %tiles_ref.3, bf16[64,128,128]{2,1,0:T(8,128)(2,1)} %all-to-all-done.3.got_ref, f32[16,128,128]{2,1,0:T(8,128)} %own.3.part_ref, ...), custom_call_target="tpu_custom_call" | custom-call | flops 671088640 | bytes 8388608 | tf_op jit(solution)/shard_map/far/pallas_call | solution.py:390
  179.3 1.0 collective-permute-start.3
  180.2 1.1 collective-permute-start.4
  181.3 1.8 collective-permute-start.5
  183.5 1.5 early.1.early_ref
  184.9 1.6 collective-permute-done.3.refs_1_
  186.5 3.2 %collective-permute-done.4.refs_2_ = bf16[544,128]{1,0:T(8,128)(2,1)S(1)} collective-permute-done((bf16[544,128]{1,0:T(8,128)(2,1)}, bf16[544,128]{1,0:T(8,128)(2,1)S(1)}, u32[]{:S(2)}, u32[]{:S(2)}) %collective-permute-start.4) | collective-permute-done | bytes 139296 | tf_op jit(solution)/shard_map/ppermute | solution.py:322
  189.7 1.2 final.1
  (45 shorter events, 5.4 us)
Async XLA Ops:
  0.0 183.2 %copy-start = (bf16[3,256,256]{2,1,0:T(8,128)(2,1)S(1)}, bf16[3,256,256]{2,1,0:T(8,128)(2,1)}, u32[]{:S(2)}) copy-start(bf16[3,256,256]{2,1,0:T(8,128)(2,1)} %param.15) | copy-start | bytes 1179652
  0.0 1.0 copy-start.4
  1.1 0.7 copy-start.5
  15.5 35.2 %all-to-all-start = ((bf16[8,4,128,128]{3,2,1,0:T(8,128)(2,1)}), bf16[8,4,128,128]{3,2,1,0:T(8,128)(2,1)S(1)}, u32[]{:S(2)}, u32[]{:S(2)}) async-start(bf16[8,4,128,128]{3,2,1,0:T(8,128)(2,1)} %get-tuple-element.43), calls=%async_computation | async-start | bytes 2097152 | tf_op jit(solution)/shard_map/all_to_all | solution.py:362
  50.7 1.0 copy-start.13
  54.8 7.9 %copy-start.10 = (s32[3]{0:T(128)S(1)}, s32[3]{0:T(128)}, u32[]{:S(2)}) copy-start(s32[3]{0:T(128)} %pad_add_fusion.me_ref) | copy-start | bytes 40
  54.9 7.9 %copy-start.11 = (s32[1,160]{1,0:T(1,128)S(1)}, s32[1,160]{1,0:T(1,128)}, u32[]{:S(2)}) copy-start(s32[1,160]{1,0:T(1,128)} %param.10) | copy-start | bytes 1924
  54.9 7.9 %copy-start.12 = (s32[1,160]{1,0:T(1,128)S(1)}, s32[1,160]{1,0:T(1,128)}, u32[]{:S(2)}) copy-start(s32[1,160]{1,0:T(1,128)} %param.11) | copy-start | bytes 1924
  54.9 33.5 %all-to-all-start.1 = ((bf16[64,128,128]{2,1,0:T(8,128)(2,1)}), bf16[64,128,128]{2,1,0:T(8,128)(2,1)}, u32[]{:S(2)}, u32[]{:S(2)}) async-start(bf16[64,128,128]{2,1,0:T(8,128)(2,1)} %pick.2), calls=%async_computation.1 | async-start | bytes 4194304 | tf_op jit(solution)/shard_map/all_to_all | solution.py:375
  67.9 0.6 copy-start.6
  68.5 0.6 copy-start.7
  69.0 0.6 copy-start.8
  69.6 0.6 copy-start.9
  138.6 7.7 %copy-start.1 = (bf16[2,4,128,128]{3,2,1,0:T(8,128)(2,1)S(1)}, bf16[2,4,128,128]{3,2,1,0:T(8,128)(2,1)}, u32[]{:S(2)}) copy-start(bf16[2,4,128,128]{3,2,1,0:T(8,128)(2,1)} %get-tuple-element.47.refs_0_.own_ref) | copy-start | bytes 786436
  138.7 34.0 %all-to-all-start.3 = ((bf16[64,128,128]{2,1,0:T(8,128)(2,1)}), bf16[64,128,128]{2,1,0:T(8,128)(2,1)}, u32[]{:S(2)}, u32[]{:S(2)}) async-start(bf16[64,128,128]{2,1,0:T(8,128)(2,1)} %pick.3), calls=%async_computation.3 | async-start | bytes 4194304 | tf_op jit(solution)/shard_map/all_to_all | solution.py:375
  146.3 35.0 %collective-permute-start = (bf16[2,4,128,128]{3,2,1,0:T(8,128)(2,1)S(1)}, bf16[2,4,128,128]{3,2,1,0:T(8,128)(2,1)S(1)}, u32[]{:S(2)}, u32[]{:S(2)}) collective-permute-start(bf16[2,4,128,128]{3,2,1,0:T(8,128)(2,1)S(1)} %copy-done.1), channel_id=1, source_target_pairs={{0,2},{1,3},{2,0},{3,1},{4,6},{5,7},{6,4},{7,5},{8,10},{9,11},{10,... | collective-permute-start | bytes 786440 | tf_op jit(solution)/shard_map/ppermute | solution.py:322
  147.2 36.2 %collective-permute-start.1 = (bf16[2,4,128,128]{3,2,1,0:T(8,128)(2,1)S(1)}, bf16[2,4,128,128]{3,2,1,0:T(8,128)(2,1)}, u32[]{:S(2)}, u32[]{:S(2)}) collective-permute-start(bf16[2,4,128,128]{3,2,1,0:T(8,128)(2,1)S(1)} %copy-done.1), channel_id=1, source_target_pairs={{0,1},{1,2},{2,3},{3,0},{4,5},{5,6},{6,7},{7,4},{8,9},{9,10},{10,1... | collective-permute-start | bytes 786440 | tf_op jit(solution)/shard_map/ppermute | solution.py:322
  148.3 35.1 %collective-permute-start.2 = (bf16[2,4,128,128]{3,2,1,0:T(8,128)(2,1)S(1)}, bf16[2,4,128,128]{3,2,1,0:T(8,128)(2,1)}, u32[]{:S(2)}, u32[]{:S(2)}) collective-permute-start(bf16[2,4,128,128]{3,2,1,0:T(8,128)(2,1)S(1)} %copy-done.1), channel_id=1, source_target_pairs={{0,3},{1,0},{2,1},{3,2},{4,7},{5,4},{6,5},{7,6},{8,11},{9,8},{10,9... | collective-permute-start | bytes 786440 | tf_op jit(solution)/shard_map/ppermute | solution.py:322
  154.3 29.1 %copy-start.2 = (bf16[2,4,128,128]{3,2,1,0:T(8,128)(2,1)S(1)}, bf16[2,4,128,128]{3,2,1,0:T(8,128)(2,1)}, u32[]{:S(2)}) copy-start(bf16[2,4,128,128]{3,2,1,0:T(8,128)(2,1)} %get-tuple-element.47.refs_0_.own_ref) | copy-start | bytes 786436
  179.3 10.5 %copy-start.3 = (bf16[544,128]{1,0:T(8,128)(2,1)S(1)}, bf16[544,128]{1,0:T(8,128)(2,1)}, u32[]{:S(2)}) copy-start(bf16[544,128]{1,0:T(8,128)(2,1)} %far.3.refs_0_) | copy-start | bytes 417796
  179.3 7.2 %collective-permute-start.3 = (bf16[544,128]{1,0:T(8,128)(2,1)}, bf16[544,128]{1,0:T(8,128)(2,1)S(1)}, u32[]{:S(2)}, u32[]{:S(2)}) collective-permute-start(bf16[544,128]{1,0:T(8,128)(2,1)} %far.3.refs_0_), channel_id=1, source_target_pairs={{0,2},{1,3},{2,0},{3,1},{4,6},{5,7},{6,4},{7,5},{8,10},{9,11},{10,... | collective-permute-start | bytes 417800 | tf_op jit(solution)/shard_map/ppermute | solution.py:322
  180.2 9.5 %collective-permute-start.4 = (bf16[544,128]{1,0:T(8,128)(2,1)}, bf16[544,128]{1,0:T(8,128)(2,1)S(1)}, u32[]{:S(2)}, u32[]{:S(2)}) collective-permute-start(bf16[544,128]{1,0:T(8,128)(2,1)} %far.3.refs_0_), channel_id=1, source_target_pairs={{0,1},{1,2},{2,3},{3,0},{4,5},{5,6},{6,7},{7,4},{8,9},{9,10},{10,1... | collective-permute-start | bytes 417800 | tf_op jit(solution)/shard_map/ppermute | solution.py:322
  181.3 8.4 %collective-permute-start.5 = (bf16[544,128]{1,0:T(8,128)(2,1)}, bf16[544,128]{1,0:T(8,128)(2,1)S(1)}, u32[]{:S(2)}, u32[]{:S(2)}) collective-permute-start(bf16[544,128]{1,0:T(8,128)(2,1)} %far.3.refs_0_), channel_id=1, source_target_pairs={{0,3},{1,0},{2,1},{3,2},{4,7},{5,4},{6,5},{7,6},{8,11},{9,8},{10,9... | collective-permute-start | bytes 417800 | tf_op jit(solution)/shard_map/ppermute | solution.py:322
where the time goes:
time: 192 us; the launch traced here: 191 us
  blocking collectives  61 us (32%)
  waiting for transfers between devices  48.7 us (25%)
  Pallas kernels  41.7 us (22%)
  starting transfers between devices  30.7 us (16%)
  local copies, waits for them, and re-layouts  6.69 us (3%)
    all_to_all x2, waiting for transfers between devices, shards(): got = lax.all_to_all(picked, ('y', 'core'), 0, 0, tiled=True)  32.4 us
    all_to_all x1, blocking collectives, shards(): along = lax.all_to_all(packed, 'z', 0, 0, tiled=True)  30.7 us
    psum x2, blocking collectives, shards(): total = lax.psum(squares, 'x')  16.6 us
    all_to_all x2, starting transfers between devices, shards(): got = lax.all_to_all(picked, ('y', 'core'), 0, 0, tiled=True)  14.9 us
    all_gather x1, blocking collectives, shards(): lax.all_gather(needed, ('y', 'core'), axis=0)  13.6 us
    pallas_call x2, Pallas kernels, shards(): call(functools.partial(far_kernel, hop), 'far', [whole(SMEM)] * 4 + [whol...  13.2 us
    all_to_all x1, waiting for transfers between devices, shards(): along = lax.all_to_all(packed, 'z', 0, 0, tiled=True)  11.5 us
    pallas_call x2, Pallas kernels, shards(): call(functools.partial(own_kernel, hop), 'own', [whole(SMEM)] * 4 + [whol...  8.3 us
  transfers between devices with their start and end apart: 9, of which 5 were waited for; matrix products, arithmetic and copies ran while one was open for 1% of the time, Pallas kernels for 11%

commit v1 on v0

--- a/solution.py
+++ b/solution.py
@@ -20,9 +20,11 @@
 MAXG = TPD // GROUP + BUCKETS
 SLOTS = MAXG * GROUP
 SHIFTS = (0, 2, 1, 3)
-DEPTH = 4
+ZSHIFTS = (0, 4, 3, 5, 2, 6, 1, 7)
+HALF = BLK // 2
+DEPTH = 10
 FULL = 63 << 20
-MOST = 65_300_000
+MOST = 66_200_000
 ROOM = 63_600_000
 EPS = 1e-06
 bf16 = jnp.bfloat16
@@ -87,11 +89,12 @@
 def norm_kernel(hop, raw_ref, sq_ref, *rest):
     columns = row_scale(sq_ref[...])
     before_ref = rest[0] if hop else None
-    out_ref, own_ref, buf, sem = rest[-4:]
+    out_ref, second_ref, own_ref, buf, sem = rest[-5:]
     copies = []
     for p in range(PAIRS):
         v = (raw_ref[p].astype(f32) * pair_scale(columns, p)).astype(bf16)
-        buf[p] = v
+        buf[p] = v[:HALF]
+        second_ref[p] = v[HALF:]
         own_ref[hop, p] = v
     for z in range(NZ):
         copy = pltpu.make_async_copy(buf, out_ref.at[z], sem.at[z])
@@ -103,13 +106,16 @@
         copy.wait()
 
 
-def pick_kernel(me_ref, idx_ref, z_ref, out_ref, slots, buf, sem):
-    for z in range(NZ):
+def pick_kernel(direct, me_ref, idx_ref, *refs):
+    z_refs = refs[: NZ if direct else 1]
+    out_ref, slots, buf, sem = refs[len(z_refs) :]
+    for j in range(NZ):
+        z = (me_ref[1] + NZ - ZSHIFTS[j]) % NZ if direct else j
         for p in range(PAIRS):
-            v = z_ref[z, p]
+            v = z_refs[j][p] if direct else z_refs[0][j, p]
             slots[z * BPD + p] = v
             slots[z * BPD + PAIRS + p] = jnp.concatenate([v[:, WIDTH:], v[:, :WIDTH]], axis=1)
-    mask = lane_low((BLK, BLK))
+    mask = lane_low((HALF, BLK))
     mine = me_ref[0] * NC + me_ref[2]
     copies = []
     for dest in range(NY * NC):
@@ -119,7 +125,7 @@
 
         @pl.when(mine == dest)
         def _():
-            buf[dest * NZ + me_ref[1]] = jnp.zeros((BLK, BLK), bf16)
+            buf[dest * NZ + me_ref[1]] = jnp.zeros((HALF, BLK), bf16)
 
         copy = pltpu.make_async_copy(
             buf.at[pl.ds(dest * NZ, NZ)], out_ref.at[pl.ds(dest * NZ, NZ)], sem.at[dest]
@@ -185,7 +191,7 @@
         slab_ref[at] = jnp.where(s < BPD, s // 2, (y * NC + k) * NZ + z)
 
 
-def add_groups(kind, tile_ref, slab_ref, into_ref, groups_ref, tiles_ref, src, acc, ring, sem):
+def add_groups(kind, tile_ref, slab_ref, into_ref, groups_ref, tiles_ref, srcs, acc, ring, sem):
     steps = (groups_ref[kind] + 1) // 2
 
     def copies(step):
@@ -210,7 +216,7 @@
         parts = []
         for h in range(2):
             left = jnp.concatenate([ring[slot, h * GROUP + j] for j in range(GROUP)], axis=1)
-            right = jnp.concatenate([src[slab_ref[(group + h) * GROUP + j]] for j in range(GROUP)], axis=0)
+            right = jnp.concatenate([src[slab_ref[(group + h) * GROUP + j]] for j in range(GROUP) for src in srcs], axis=0)
             parts.append(jnp.dot(left, right, preferred_element_type=f32))
         for h in range(2):
             acc[into_ref[group + h]] += parts[h]
@@ -221,7 +227,7 @@
 
 
 def own_kernel(hop, tile_ref, slab_ref, into_ref, groups_ref, tiles_ref, own_ref, acc_ref, src, ring, sem):
-    begin, run = add_groups(0, tile_ref, slab_ref, into_ref, groups_ref, tiles_ref, src, acc_ref, ring, sem)
+    begin, run = add_groups(0, tile_ref, slab_ref, into_ref, groups_ref, tiles_ref, (src,), acc_ref, ring, sem)
     for step in range(DEPTH):
         begin(step)
     acc_ref[...] = jnp.zeros_like(acc_ref)
@@ -230,13 +236,13 @@
     run()
 
 
-def far_kernel(hop, tile_ref, slab_ref, into_ref, groups_ref, tiles_ref, got_ref, part_ref, noise_ref, *rest):
+def far_kernel(hop, tile_ref, slab_ref, into_ref, groups_ref, tiles_ref, first_ref, second_ref, part_ref, noise_ref, *rest):
     last = hop == HOPS - 1
     if last:
         out_ref, acc, noise, ring, sem, load = rest
     else:
         out_ref, sq_ref, acc, noise, ring, sem, load = rest
-    begin, run = add_groups(1, tile_ref, slab_ref, into_ref, groups_ref, tiles_ref, got_ref, acc, ring, sem)
+    begin, run = add_groups(1, tile_ref, slab_ref, into_ref, groups_ref, tiles_ref, (first_ref, second_ref), acc, ring, sem)
     for step in range(DEPTH):
         begin(step)
     noise_copy = pltpu.make_async_copy(noise_ref.at[hop], noise, load)
@@ -351,28 +357,37 @@
         last = hop == HOPS - 1
         total = lax.psum(squares, "x")
         before = [owned] if hop else []
-        packed, owned = call(
+        first, second, owned = call(
             functools.partial(norm_kernel, hop), "norm", [whole()] * (2 + hop),
-            [((NZ, PAIRS, BLK, BLK), bf16, HBM), ((hop + 1, PAIRS, BLK, BLK), bf16, VMEM)],
-            [VMEM((PAIRS, BLK, BLK), bf16), DMA((NZ,))],
+            [
+                ((NZ, PAIRS, HALF, BLK), bf16, HBM),
+                ((PAIRS, HALF, BLK), bf16, VMEM),
+                ((hop + 1, PAIRS, BLK, BLK), bf16, VMEM),
+            ],
+            [VMEM((PAIRS, HALF, BLK), bf16), DMA((NZ,))],
             limit=MOST,
         )(packed, total, *before)
         if last:
             spread = [owned] + [shift_by(owned, "x", shift) for shift in SHIFTS[1:]]
-        along = lax.all_to_all(packed, "z", 0, 0, tiled=True)
+        along = [lax.all_to_all(first, "z", 0, 0, tiled=True)]
+        direct = [second] + [shift_by(second, "z", shift) for shift in ZSHIFTS[1:]]
         if table is None:
             needed, owned = lax.optimization_barrier((needed, owned))
             asked = lax.all_gather(needed, ("y", "core"), axis=0).reshape(NY * NC, NY, NZ, NC, 2)
             asked = lax.dynamic_slice(asked, (0, me[0], 0, me[2], 0), (NY * NC, 1, NZ, 1, 2)).reshape(NY * NC, NZ, 2)
             odd = (asked % 2) ^ jnp.arange(2, dtype=jnp.int32)
             table = (jnp.arange(NZ, dtype=jnp.int32)[:, None] * BPD + asked // 2 + PAIRS * odd).reshape(-1)
-        picked = call(
-            pick_kernel, "pick", [whole(SMEM)] * 2 + [whole()],
-            [((NY * NC * NZ, BLK, BLK), bf16, HBM)],
-            [VMEM((NZ * BPD, BLK, BLK), bf16), VMEM((NY * NC * NZ, BLK, BLK), bf16), DMA((NY * NC,))],
-            limit=MOST,
-        )(me, table, along)
-        got = lax.all_to_all(picked, ("y", "core"), 0, 0, tiled=True)
+        got = []
+        at = me
+        for inputs in (along, direct):
+            picked = call(
+                functools.partial(pick_kernel, inputs is direct), "pick", [whole(SMEM)] * 2 + [whole()] * len(inputs),
+                [((NY * NC * NZ, HALF, BLK), bf16, HBM)],
+                [VMEM((NZ * BPD, HALF, BLK), bf16), VMEM((NY * NC * NZ, HALF, BLK), bf16), DMA((NY * NC,))],
+                limit=MOST,
+            )(at, table, *inputs)
+            picked, at = lax.optimization_barrier((picked, at))
+            got.append(lax.all_to_all(picked, ("y", "core"), 0, 0, tiled=True))
         ring = [VMEM((DEPTH, 2 * GROUP, BLK, BLK), bf16), DMA((DEPTH, 2 * GROUP))]
         part = call(
             functools.partial(own_kernel, hop), "own", [whole(SMEM)] * 4 + [whole(HBM), whole()], [((BUCKETS, BLK, BLK), f32, VMEM)],
@@ -383,18 +398,19 @@
             early = call(
                 early_kernel, "early", [whole(SMEM)] + [whole()] * (1 + NX), [((PAIRS, BLK, BLK), f32, VMEM)]
             )(x_only, weights, *spread)
+            early, part = lax.optimization_barrier((early, part))
         if last:
             outs = [((PAIRS * BLK + 32, BLK), bf16, VMEM)]
         else:
             outs = [((PAIRS, BLK, BLK), f32, VMEM), ((BPD, BLK), f32, VMEM)]
         result = call(
-            functools.partial(far_kernel, hop), "far", [whole(SMEM)] * 4 + [whole(HBM), whole(), whole(), whole(HBM)], outs,
+            functools.partial(far_kernel, hop), "far", [whole(SMEM)] * 4 + [whole(HBM), whole(), whole(), whole(), whole(HBM)], outs,
             [
                 VMEM((BUCKETS, BLK, BLK), f32),
                 VMEM((WIDTH, BPD * BLK), f32),
             ] + ring + [DMA(())],
             limit=ROOM, flops=TPD * 2 * BLK**3, moved=8 << 20,
-        )(*lists, tile_vals, got, part, noise)
+        )(*lists, tile_vals, *got, part, noise)
         if not last:
             packed, squares = result
     tails = [result] + [shift_by(result, "x", shift) for shift in SHIFTS[1:]]

time: 192 us -> 207 us (1.078); the launches traced: 191 us -> 203 us
  starting transfers between devices: 30.7 us -> 67.2 us
  waiting for transfers between devices: 48.7 us -> 29.3 us
  blocking collectives: 61 us -> 54.8 us
    all_to_all x3 -> x5, waiting for transfers between devices: 43.8 us -> 3.7 us  [the longest x4 3.7 us: shards(): got.append(lax.all_to_all(picked, ('y', 'core'), 0, 0, tiled=True))]
    ppermute x6 -> x20, waiting for transfers between devices: 4.82 us -> 25.6 us  [shift_by(): lax.ppermute(value, axis, [(i, (i + shift) % size) for i in range(size)])]
    all_to_all x3 -> x5, starting transfers between devices: 23.1 us -> 43.2 us  [the longest x4 35.1 us: shards(): got.append(lax.all_to_all(picked, ('y', 'core'), 0, 0, tiled=True))]
    ppermute x6 -> x20, starting transfers between devices: 7.65 us -> 23.9 us  [shift_by(): lax.ppermute(value, axis, [(i, (i + shift) % size) for i in range(size)])]
    all_to_all x1, blocking collectives: 30.7 us -> 24.6 us  [shards(): along = [lax.all_to_all(first, 'z', 0, 0, tiled=True)]]
    pallas_call x2 -> x4, Pallas kernels: 6.22 us -> 9.58 us  [shards(): call(functools.partial(pick_kernel, inputs is direct), 'pick', [whole(SME...]
    unnamed x29 -> x47, local copies, waits for them, and re-layouts: 5.71 us -> 5.51 us
  transfers between devices with their start and end apart: 9 -> 25, of which waited for: 5 -> 10; matrix products, arithmetic and copies ran while one was open for 1% -> 1% of each run, Pallas kernels for 11% -> 9%
where the time goes in v1:
time: 207 us; the launch traced here: 203 us
  starting transfers between devices  67.2 us (32%)
  blocking collectives  54.8 us (26%)
  Pallas kernels  43.3 us (21%)
  waiting for transfers between devices  29.3 us (14%)
  local copies, waits for them, and re-layouts  6.49 us (3%)
    all_to_all x4, starting transfers between devices, shards(): got.append(lax.all_to_all(picked, ('y', 'core'), 0, 0, tiled=True))  35.1 us
    ppermute x20, waiting for transfers between devices, shift_by(): lax.ppermute(value, axis, [(i, (i + shift) % size) for i in range(size)])  25.6 us
    all_to_all x1, blocking collectives, shards(): along = [lax.all_to_all(first, 'z', 0, 0, tiled=True)]  24.6 us
    ppermute x20, starting transfers between devices, shift_by(): lax.ppermute(value, axis, [(i, (i + shift) % size) for i in range(size)])  23.9 us
    psum x2, blocking collectives, shards(): total = lax.psum(squares, 'x')  16.6 us
    all_gather x1, blocking collectives, shards(): lax.all_gather(needed, ('y', 'core'), axis=0)  13.6 us
    pallas_call x2, Pallas kernels, shards(): call(functools.partial(far_kernel, hop), 'far', [whole(SMEM)] * 4 + [whol...  12.3 us
    pallas_call x4, Pallas kernels, shards(): call(functools.partial(pick_kernel, inputs is direct), 'pick', [whole(SME...  9.58 us
  transfers between devices with their start and end apart: 25, of which 10 were waited for; matrix products, arithmetic and copies ran while one was open for 1% of the time, Pallas kernels for 9%

profile of v1, /device:TPU:1, one launch (start us, length us, event | category | flops | bytes accessed | tf_op | source)
XLA Modules:
  0.0 203.5 jit_solution(10819177779261551411)
XLA Ops:
  2.6 9.8 %psum.14.sq_ref = f32[8,128]{1,0:T(8,128)} all-reduce(f32[8,128]{1,0:T(8,128)S(1)} %get-tuple-element.50), channel_id=1, replica_groups=mesh['y'=4,'z'=8,'core'=2,'x'=4] {'x'}, use_global_device_ids=true, to_apply=%region_0.0 | all-reduce | flops 1024 | bytes 8192 | tf_op jit(solution)/shard_map/psum | solution.py:358
  12.5 2.8 %norm.2 = (bf16[8,4,64,128]{3,2,1,0:T(8,128)(2,1)}, bf16[4,64,128]{2,1,0:T(8,128)(2,1)}, bf16[1,4,128,128]{3,2,1,0:T(8,128)(2,1)}) custom-call(bf16[4,128,128]{2,1,0:T(8,128)(2,1)} %copy-done.3, f32[8,128]{1,0:T(8,128)} %psum.14.sq_ref), custom_call_target="tpu_custom_call" | custom-call | flops 1048576 | bytes 1048576 | tf_op jit(solution)/shard_map/norm/pallas_call | solution.py:360
  15.3 8.2 %all-to-all-start = ((bf16[8,4,64,128]{3,2,1,0:T(8,128)(2,1)}), bf16[8,4,64,128]{3,2,1,0:T(8,128)(2,1)}, u32[]{:S(2)}, u32[]{:S(2)}) async-start(bf16[8,4,64,128]{3,2,1,0:T(8,128)(2,1)} %get-tuple-element.53), calls=%async_computation | async-start | bytes 1048576 | tf_op jit(solution)/shard_map/all_to_all | solution.py:372
  23.8 13.6 %all-gather.1 = s32[8,1,128]{2,1,0:T(1,128)S(1)} all-gather(s32[1,1,128]{2,1,0:T(1,128)S(1)} %bitcast.23), channel_id=2, replica_groups=mesh['y'=4,'z'=8,'core'=2,'x'=4] {'y','core'}, dimensions={0}, use_global_device_ids=true | all-gather | bytes 4608 | tf_op jit(solution)/shard_map/all_gather | solution.py:376
  39.0 2.4 %pick.4 = bf16[64,64,128]{2,1,0:T(8,128)(2,1)} custom-call(s32[3]{0:T(128)} %pad_add_fusion.me_ref, s32[128]{0:T(128)} %multiply_add_fusion.idx_ref, bf16[8,4,64,128]{3,2,1,0:T(8,128)(2,1)} %all-to-all-done.refs_0_), custom_call_target="tpu_custom_call" | custom-call | flops 1048576 | bytes 1048576 | tf_op jit(solution)/shard_map/pick/pallas_call | solution.py:383
  41.4 7.5 %all-to-all-start.1 = ((bf16[64,64,128]{2,1,0:T(8,128)(2,1)}), bf16[64,64,128]{2,1,0:T(8,128)(2,1)}, u32[]{:S(2)}, u32[]{:S(2)}) async-start(bf16[64,64,128]{2,1,0:T(8,128)(2,1)} %pick.4), calls=%async_computation.1 | async-start | bytes 2097152 | tf_op jit(solution)/shard_map/all_to_all | solution.py:390
  56.0 2.5 %collective-permute-start = (bf16[4,64,128]{2,1,0:T(8,128)(2,1)}, bf16[4,64,128]{2,1,0:T(8,128)(2,1)}, u32[]{:S(2)}, u32[]{:S(2)}) collective-permute-start(bf16[4,64,128]{2,1,0:T(8,128)(2,1)} %get-tuple-element.56.refs_0_), channel_id=1, source_target_pairs={{0,32},{8,40},{16,48},{24,56},{32,0},{40,8},{48,16},{56,24},{1,33}... | collective-permute-start | bytes 196616 | tf_op jit(solution)/shard_map/ppermute | solution.py:328
  58.5 2.6 %collective-permute-done.1.refs_2_ = bf16[4,64,128]{2,1,0:T(8,128)(2,1)S(1)} collective-permute-done((bf16[4,64,128]{2,1,0:T(8,128)(2,1)}, bf16[4,64,128]{2,1,0:T(8,128)(2,1)S(1)}, u32[]{:S(2)}, u32[]{:S(2)}) %collective-permute-start.1) | collective-permute-done | bytes 65568 | tf_op jit(solution)/shard_map/ppermute | solution.py:328
  61.1 2.3 %collective-permute-done.refs_1_ = bf16[4,64,128]{2,1,0:T(8,128)(2,1)} collective-permute-done((bf16[4,64,128]{2,1,0:T(8,128)(2,1)}, bf16[4,64,128]{2,1,0:T(8,128)(2,1)}, u32[]{:S(2)}, u32[]{:S(2)}) %collective-permute-start) | collective-permute-done | bytes 65568 | tf_op jit(solution)/shard_map/ppermute | solution.py:328
  63.5 2.4 %pick.5 = bf16[64,64,128]{2,1,0:T(8,128)(2,1)} custom-call(s32[3]{0:T(128)} %pad_add_fusion.me_ref, s32[128]{0:T(128)} %multiply_add_fusion.idx_ref, bf16[4,64,128]{2,1,0:T(8,128)(2,1)} %get-tuple-element.56.refs_0_, bf16[4,64,128]{2,1,0:T(8,128)(2,1)} %collective-permute-done.refs_1_, bf16[4,64,128]{2,1,0:T(8,128)(2,1)} %copy-done.22, ...), custom_call_target="tpu_custom_call" | custom-call | flops 1048576 | bytes 1048576 | tf_op jit(solution)/shard_map/pick/pallas_call | solution.py:383
  65.9 8.1 %all-to-all-start.2 = ((bf16[64,64,128]{2,1,0:T(8,128)(2,1)}), bf16[64,64,128]{2,1,0:T(8,128)(2,1)}, u32[]{:S(2)}, u32[]{:S(2)}) async-start(bf16[64,64,128]{2,1,0:T(8,128)(2,1)} %pick.5), calls=%async_computation.2 | async-start | bytes 2097152 | tf_op jit(solution)/shard_map/all_to_all | solution.py:390
  74.7 4.2 %order.1 = (s32[448]{0:T(512)S(1)}, s32[448]{0:T(512)S(1)}, s32[112]{0:T(128)S(1)}, s32[2]{0:T(128)S(1)}) custom-call(s32[3]{0:T(128)S(1)} %copy-done.6, s32[160]{0:T(256)S(1)} %bitcast.17, s32[160]{0:T(256)S(1)} %bitcast.18, s32[1]{0:T(128)S(6)} %copy.17.count_ref), custom_call_target="tpu_custom_call" | custom-call | flops 1048576 | bytes 1048576 | tf_op jit(solution)/shard_map/order/pallas_call | solution.py:350
  81.1 4.3 %own.2.part_ref = f32[16,128,128]{2,1,0:T(8,128)} custom-call(s32[448]{0:T(512)} %copy-done.4, s32[448]{0:T(512)} %copy-done.5, s32[112]{0:T(128)} %copy-done.7, s32[2]{0:T(128)} %copy-done.8, bf16[160,128,128]{2,1,0:T(8,128)(2,1)} %tiles_ref.3, bf16[1,4,128,128]{3,2,1,0:T(8,128)(2,1)} %get-tuple-element.58.own_ref.rest_0_), custom_call_target="tpu_custom_call" | custom-call | flops 671088640 | bytes 4194304 | tf_op jit(solution)/shard_map/own/pallas_call | solution.py:392
  85.4 3.7 %all-to-all-done.2.second_ref = bf16[64,64,128]{2,1,0:T(8,128)(2,1)} async-done(((bf16[64,64,128]{2,1,0:T(8,128)(2,1)}), bf16[64,64,128]{2,1,0:T(8,128)(2,1)}, u32[]{:S(2)}, u32[]{:S(2)}) %all-to-all-start.2) | async-done | bytes 1048608 | tf_op jit(solution)/shard_map/all_to_all | solution.py:390
  89.1 6.1 %far.2 = (f32[4,128,128]{2,1,0:T(8,128)}, f32[8,128]{1,0:T(8,128)}) custom-call(s32[448]{0:T(512)} %copy-done.4, s32[448]{0:T(512)} %copy-done.5, s32[112]{0:T(128)} %copy-done.7, s32[2]{0:T(128)} %copy-done.8, bf16[160,128,128]{2,1,0:T(8,128)(2,1)} %tiles_ref.3, bf16[64,64,128]{2,1,0:T(8,128)(2,1)} %all-to-all-done.1.first_ref, ...), custom_call_target="tpu_custom_call" | custom-call | flops 671088640 | bytes 8388608 | tf_op jit(solution)/shard_map/far/pallas_call | solution.py:406
  95.2 6.7 %psum.15.sq_ref = f32[8,128]{1,0:T(8,128)} all-reduce(f32[8,128]{1,0:T(8,128)} %get-tuple-element.60), channel_id=1, replica_groups=mesh['y'=4,'z'=8,'core'=2,'x'=4] {'x'}, use_global_device_ids=true, to_apply=%region_1.2 | all-reduce | flops 1024 | bytes 8192 | tf_op jit(solution)/shard_map/psum | solution.py:358
  101.9 2.9 %norm.3 = (bf16[8,4,64,128]{3,2,1,0:T(8,128)(2,1)}, bf16[4,64,128]{2,1,0:T(8,128)(2,1)}, bf16[2,4,128,128]{3,2,1,0:T(8,128)(2,1)}) custom-call(f32[4,128,128]{2,1,0:T(8,128)} %get-tuple-element.59.raw_ref, f32[8,128]{1,0:T(8,128)} %psum.15.sq_ref, bf16[1,4,128,128]{3,2,1,0:T(8,128)(2,1)} %get-tuple-element.58.own_ref.rest_0_), custom_call_target="tpu_custom_call" | custom-call | flops 1048576 | bytes 1048576 | tf_op jit(solution)/shard_map/norm/pallas_call | solution.py:360
  104.8 24.6 %all_to_all.30.refs_0_ = bf16[8,4,64,128]{3,2,1,0:T(8,128)(2,1)} all-to-all(bf16[8,4,64,128]{3,2,1,0:T(8,128)(2,1)} %get-tuple-element.63), channel_id=1, replica_groups=mesh['y'=4,'z'=8,'core'=2,'x'=4] {'z'}, dimensions={0} | all-to-all | bytes 1048576 | tf_op jit(solution)/shard_map/all_to_all | solution.py:372
  129.5 2.4 %pick.6 = bf16[64,64,128]{2,1,0:T(8,128)(2,1)} custom-call(s32[3]{0:T(128)} %pad_add_fusion.me_ref, s32[128]{0:T(128)} %multiply_add_fusion.idx_ref, bf16[8,4,64,128]{3,2,1,0:T(8,128)(2,1)} %all_to_all.30.refs_0_), custom_call_target="tpu_custom_call" | custom-call | flops 1048576 | bytes 1048576 | tf_op jit(solution)/shard_map/pick/pallas_call | solution.py:383
  131.9 11.4 %all-to-all-start.4 = ((bf16[64,64,128]{2,1,0:T(8,128)(2,1)}), bf16[64,64,128]{2,1,0:T(8,128)(2,1)}, u32[]{:S(2)}, u32[]{:S(2)}) async-start(bf16[64,64,128]{2,1,0:T(8,128)(2,1)} %pick.6), calls=%async_computation.4 | async-start | bytes 2097152 | tf_op jit(solution)/shard_map/all_to_all | solution.py:390
  144.8 2.3 %collective-permute-start.13 = (bf16[4,64,128]{2,1,0:T(8,128)(2,1)}, bf16[4,64,128]{2,1,0:T(8,128)(2,1)S(1)}, u32[]{:S(2)}, u32[]{:S(2)}) collective-permute-start(bf16[4,64,128]{2,1,0:T(8,128)(2,1)} %get-tuple-element.66.refs_0_), channel_id=1, source_target_pairs={{0,16},{8,24},{16,32},{24,40},{32,48},{40,56},{48,0},{56,8},{1,17}... | collective-permute-start | bytes 196616 | tf_op jit(solution)/shard_map/ppermute | solution.py:328
  148.3 2.1 %collective-permute-start.11 = (bf16[4,64,128]{2,1,0:T(8,128)(2,1)}, bf16[4,64,128]{2,1,0:T(8,128)(2,1)S(1)}, u32[]{:S(2)}, u32[]{:S(2)}) collective-permute-start(bf16[4,64,128]{2,1,0:T(8,128)(2,1)} %get-tuple-element.66.refs_0_), channel_id=1, source_target_pairs={{0,24},{8,32},{16,40},{24,48},{32,56},{40,0},{48,8},{56,16},{1,25}... | collective-permute-start | bytes 196616 | tf_op jit(solution)/shard_map/ppermute | solution.py:328
  150.4 2.2 %collective-permute-start.10 = (bf16[4,64,128]{2,1,0:T(8,128)(2,1)}, bf16[4,64,128]{2,1,0:T(8,128)(2,1)}, u32[]{:S(2)}, u32[]{:S(2)}) collective-permute-start(bf16[4,64,128]{2,1,0:T(8,128)(2,1)} %get-tuple-element.66.refs_0_), channel_id=1, source_target_pairs={{0,32},{8,40},{16,48},{24,56},{32,0},{40,8},{48,16},{56,24},{1,33}... | collective-permute-start | bytes 196616 | tf_op jit(solution)/shard_map/ppermute | solution.py:328
  152.7 2.5 %collective-permute-done.11.refs_2_ = bf16[4,64,128]{2,1,0:T(8,128)(2,1)S(1)} collective-permute-done((bf16[4,64,128]{2,1,0:T(8,128)(2,1)}, bf16[4,64,128]{2,1,0:T(8,128)(2,1)S(1)}, u32[]{:S(2)}, u32[]{:S(2)}) %collective-permute-start.11) | collective-permute-done | bytes 65568 | tf_op jit(solution)/shard_map/ppermute | solution.py:328
  155.2 3.2 %collective-permute-done.10.refs_1_ = bf16[4,64,128]{2,1,0:T(8,128)(2,1)} collective-permute-done((bf16[4,64,128]{2,1,0:T(8,128)(2,1)}, bf16[4,64,128]{2,1,0:T(8,128)(2,1)}, u32[]{:S(2)}, u32[]{:S(2)}) %collective-permute-start.10) | collective-permute-done | bytes 65568 | tf_op jit(solution)/shard_map/ppermute | solution.py:328
  158.4 2.4 %pick.7 = bf16[64,64,128]{2,1,0:T(8,128)(2,1)} custom-call(s32[3]{0:T(128)} %pad_add_fusion.me_ref, s32[128]{0:T(128)} %multiply_add_fusion.idx_ref, bf16[4,64,128]{2,1,0:T(8,128)(2,1)} %get-tuple-element.66.refs_0_, bf16[4,64,128]{2,1,0:T(8,128)(2,1)} %collective-permute-done.10.refs_1_, bf16[4,64,128]{2,1,0:T(8,128)(2,1)} %copy-done.21, ...), custom_call_target="tpu_custom_call" | custom-call | flops 1048576 | bytes 1048576 | tf_op jit(solution)/shard_map/pick/pallas_call | solution.py:383
  160.9 8.0 %all-to-all-start.5 = ((bf16[64,64,128]{2,1,0:T(8,128)(2,1)}), bf16[64,64,128]{2,1,0:T(8,128)(2,1)}, u32[]{:S(2)}, u32[]{:S(2)}) async-start(bf16[64,64,128]{2,1,0:T(8,128)(2,1)} %pick.7), calls=%async_computation.5 | async-start | bytes 2097152 | tf_op jit(solution)/shard_map/all_to_all | solution.py:390
  171.9 4.4 %own.3.part_ref = f32[16,128,128]{2,1,0:T(8,128)} custom-call(s32[448]{0:T(512)} %copy-done.4, s32[448]{0:T(512)} %copy-done.5, s32[112]{0:T(128)} %copy-done.7, s32[2]{0:T(128)} %copy-done.8, bf16[160,128,128]{2,1,0:T(8,128)(2,1)} %tiles_ref.3, bf16[2,4,128,128]{3,2,1,0:T(8,128)(2,1)} %get-tuple-element.61.refs_0_.own_ref), custom_call_target="tpu_custom_call" | custom-call | flops 671088640 | bytes 4194304 | tf_op jit(solution)/shard_map/own/pallas_call | solution.py:392
  177.1 7.5 %collective-permute-done.8.refs_2_ = bf16[2,4,128,128]{3,2,1,0:T(8,128)(2,1)} collective-permute-done((bf16[2,4,128,128]{3,2,1,0:T(8,128)(2,1)}, bf16[2,4,128,128]{3,2,1,0:T(8,128)(2,1)}, u32[]{:S(2)}, u32[]{:S(2)}) %collective-permute-start.8) | collective-permute-done | bytes 262176 | tf_op jit(solution)/shard_map/ppermute | solution.py:328
  186.3 6.2 %far.3.refs_0_ = bf16[544,128]{1,0:T(8,128)(2,1)} custom-call(s32[448]{0:T(512)} %copy-done.4, s32[448]{0:T(512)} %copy-done.5, s32[112]{0:T(128)} %copy-done.7, s32[2]{0:T(128)} %copy-done.8, bf16[160,128,128]{2,1,0:T(8,128)(2,1)} %tiles_ref.3, bf16[64,64,128]{2,1,0:T(8,128)(2,1)} %all-to-all-done.4.first_ref, ...), custom_call_target="tpu_custom_call" | custom-call | flops 671088640 | bytes 8388608 | tf_op jit(solution)/shard_map/far/pallas_call | solution.py:406
  194.7 1.9 collective-permute-done.19.refs_3_
  198.5 2.9 %collective-permute-done.17.refs_1_ = bf16[544,128]{1,0:T(8,128)(2,1)S(1)} collective-permute-done((bf16[544,128]{1,0:T(8,128)(2,1)}, bf16[544,128]{1,0:T(8,128)(2,1)S(1)}, u32[]{:S(2)}, u32[]{:S(2)}) %collective-permute-start.17) | collective-permute-done | bytes 139296 | tf_op jit(solution)/shard_map/ppermute | solution.py:328
  (97 shorter events, 28.2 us)
Async XLA Ops:
  0.0 171.7 %copy-start = (bf16[3,256,256]{2,1,0:T(8,128)(2,1)S(1)}, bf16[3,256,256]{2,1,0:T(8,128)(2,1)}, u32[]{:S(2)}) copy-start(bf16[3,256,256]{2,1,0:T(8,128)(2,1)} %param.15) | copy-start | bytes 1179652
  0.0 74.7 %copy-start.10 = (s32[1,160]{1,0:T(1,128)S(1)}, s32[1,160]{1,0:T(1,128)}, u32[]{:S(2)}) copy-start(s32[1,160]{1,0:T(1,128)} %param.11) | copy-start | bytes 1924
  0.0 74.7 %copy-start.9 = (s32[1,160]{1,0:T(1,128)S(1)}, s32[1,160]{1,0:T(1,128)}, u32[]{:S(2)}) copy-start(s32[1,160]{1,0:T(1,128)} %param.10) | copy-start | bytes 1924
  15.3 23.7 %all-to-all-start = ((bf16[8,4,64,128]{3,2,1,0:T(8,128)(2,1)}), bf16[8,4,64,128]{3,2,1,0:T(8,128)(2,1)}, u32[]{:S(2)}, u32[]{:S(2)}) async-start(bf16[8,4,64,128]{3,2,1,0:T(8,128)(2,1)} %get-tuple-element.53), calls=%async_computation | async-start | bytes 1048576 | tf_op jit(solution)/shard_map/all_to_all | solution.py:372
  38.5 36.2 %copy-start.6 = (s32[3]{0:T(128)S(1)}, s32[3]{0:T(128)}, u32[]{:S(2)}) copy-start(s32[3]{0:T(128)} %pad_add_fusion.me_ref) | copy-start | bytes 40
  41.4 24.5 %all-to-all-start.1 = ((bf16[64,64,128]{2,1,0:T(8,128)(2,1)}), bf16[64,64,128]{2,1,0:T(8,128)(2,1)}, u32[]{:S(2)}, u32[]{:S(2)}) async-start(bf16[64,64,128]{2,1,0:T(8,128)(2,1)} %pick.4), calls=%async_computation.1 | async-start | bytes 2097152 | tf_op jit(solution)/shard_map/all_to_all | solution.py:390
  48.9 5.4 %collective-permute-start.6 = (bf16[4,64,128]{2,1,0:T(8,128)(2,1)}, bf16[4,64,128]{2,1,0:T(8,128)(2,1)S(1)}, u32[]{:S(2)}, u32[]{:S(2)}) collective-permute-start(bf16[4,64,128]{2,1,0:T(8,128)(2,1)} %get-tuple-element.56.refs_0_), channel_id=1, source_target_pairs={{0,56},{8,0},{16,8},{24,16},{32,24},{40,32},{48,40},{56,48},{1,57}... | collective-permute-start | bytes 196616 | tf_op jit(solution)/shard_map/ppermute | solution.py:328
  48.9 7.1 %collective-permute-start.5 = (bf16[4,64,128]{2,1,0:T(8,128)(2,1)}, bf16[4,64,128]{2,1,0:T(8,128)(2,1)S(1)}, u32[]{:S(2)}, u32[]{:S(2)}) collective-permute-start(bf16[4,64,128]{2,1,0:T(8,128)(2,1)} %get-tuple-element.56.refs_0_), channel_id=1, source_target_pairs={{0,8},{8,16},{16,24},{24,32},{32,40},{40,48},{48,56},{56,0},{1,9},... | collective-permute-start | bytes 196616 | tf_op jit(solution)/shard_map/ppermute | solution.py:328
  50.4 8.1 %collective-permute-start.4 = (bf16[4,64,128]{2,1,0:T(8,128)(2,1)}, bf16[4,64,128]{2,1,0:T(8,128)(2,1)S(1)}, u32[]{:S(2)}, u32[]{:S(2)}) collective-permute-start(bf16[4,64,128]{2,1,0:T(8,128)(2,1)} %get-tuple-element.56.refs_0_), channel_id=1, source_target_pairs={{0,48},{8,56},{16,0},{24,8},{32,16},{40,24},{48,32},{56,40},{1,49}... | collective-permute-start | bytes 196616 | tf_op jit(solution)/shard_map/ppermute | solution.py:328
  51.0 7.4 %collective-permute-start.3 = (bf16[4,64,128]{2,1,0:T(8,128)(2,1)}, bf16[4,64,128]{2,1,0:T(8,128)(2,1)S(1)}, u32[]{:S(2)}, u32[]{:S(2)}) collective-permute-start(bf16[4,64,128]{2,1,0:T(8,128)(2,1)} %get-tuple-element.56.refs_0_), channel_id=1, source_target_pairs={{0,16},{8,24},{16,32},{24,40},{32,48},{40,56},{48,0},{56,8},{1,17}... | collective-permute-start | bytes 196616 | tf_op jit(solution)/shard_map/ppermute | solution.py:328
  52.7 5.8 %collective-permute-start.2 = (bf16[4,64,128]{2,1,0:T(8,128)(2,1)}, bf16[4,64,128]{2,1,0:T(8,128)(2,1)S(1)}, u32[]{:S(2)}, u32[]{:S(2)}) collective-permute-start(bf16[4,64,128]{2,1,0:T(8,128)(2,1)} %get-tuple-element.56.refs_0_), channel_id=1, source_target_pairs={{0,40},{8,48},{16,56},{24,0},{32,8},{40,16},{48,24},{56,32},{1,41}... | collective-permute-start | bytes 196616 | tf_op jit(solution)/shard_map/ppermute | solution.py:328
  54.3 9.1 %copy-start.12 = (bf16[4,64,128]{2,1,0:T(8,128)(2,1)}, bf16[4,64,128]{2,1,0:T(8,128)(2,1)S(1)}, u32[]{:S(2)}) copy-start(bf16[4,64,128]{2,1,0:T(8,128)(2,1)S(1)} %collective-permute-done.6.refs_7_) | copy-start | bytes 196612
  54.3 6.8 %collective-permute-start.1 = (bf16[4,64,128]{2,1,0:T(8,128)(2,1)}, bf16[4,64,128]{2,1,0:T(8,128)(2,1)S(1)}, u32[]{:S(2)}, u32[]{:S(2)}) collective-permute-start(bf16[4,64,128]{2,1,0:T(8,128)(2,1)} %get-tuple-element.56.refs_0_), channel_id=1, source_target_pairs={{0,24},{8,32},{16,40},{24,48},{32,56},{40,0},{48,8},{56,16},{1,25}... | collective-permute-start | bytes 196616 | tf_op jit(solution)/shard_map/ppermute | solution.py:328
  56.0 7.4 %collective-permute-start = (bf16[4,64,128]{2,1,0:T(8,128)(2,1)}, bf16[4,64,128]{2,1,0:T(8,128)(2,1)}, u32[]{:S(2)}, u32[]{:S(2)}) collective-permute-start(bf16[4,64,128]{2,1,0:T(8,128)(2,1)} %get-tuple-element.56.refs_0_), channel_id=1, source_target_pairs={{0,32},{8,40},{16,48},{24,56},{32,0},{40,8},{48,16},{56,24},{1,33}... | collective-permute-start | bytes 196616 | tf_op jit(solution)/shard_map/ppermute | solution.py:328
  65.9 23.2 %all-to-all-start.2 = ((bf16[64,64,128]{2,1,0:T(8,128)(2,1)}), bf16[64,64,128]{2,1,0:T(8,128)(2,1)}, u32[]{:S(2)}, u32[]{:S(2)}) async-start(bf16[64,64,128]{2,1,0:T(8,128)(2,1)} %pick.5), calls=%async_computation.2 | async-start | bytes 2097152 | tf_op jit(solution)/shard_map/all_to_all | solution.py:390
  131.9 29.0 %all-to-all-start.4 = ((bf16[64,64,128]{2,1,0:T(8,128)(2,1)}), bf16[64,64,128]{2,1,0:T(8,128)(2,1)}, u32[]{:S(2)}, u32[]{:S(2)}) async-start(bf16[64,64,128]{2,1,0:T(8,128)(2,1)} %pick.6), calls=%async_computation.4 | async-start | bytes 2097152 | tf_op jit(solution)/shard_map/all_to_all | solution.py:390
  143.3 5.0 %collective-permute-start.16 = (bf16[4,64,128]{2,1,0:T(8,128)(2,1)}, bf16[4,64,128]{2,1,0:T(8,128)(2,1)S(1)}, u32[]{:S(2)}, u32[]{:S(2)}) collective-permute-start(bf16[4,64,128]{2,1,0:T(8,128)(2,1)} %get-tuple-element.66.refs_0_), channel_id=1, source_target_pairs={{0,56},{8,0},{16,8},{24,16},{32,24},{40,32},{48,40},{56,48},{1,57}... | collective-permute-start | bytes 196616 | tf_op jit(solution)/shard_map/ppermute | solution.py:328
  143.3 7.1 %collective-permute-start.15 = (bf16[4,64,128]{2,1,0:T(8,128)(2,1)}, bf16[4,64,128]{2,1,0:T(8,128)(2,1)S(1)}, u32[]{:S(2)}, u32[]{:S(2)}) collective-permute-start(bf16[4,64,128]{2,1,0:T(8,128)(2,1)} %get-tuple-element.66.refs_0_), channel_id=1, source_target_pairs={{0,8},{8,16},{16,24},{24,32},{32,40},{40,48},{48,56},{56,0},{1,9},... | collective-permute-start | bytes 196616 | tf_op jit(solution)/shard_map/ppermute | solution.py:328
  144.7 7.9 %collective-permute-start.14 = (bf16[4,64,128]{2,1,0:T(8,128)(2,1)}, bf16[4,64,128]{2,1,0:T(8,128)(2,1)S(1)}, u32[]{:S(2)}, u32[]{:S(2)}) collective-permute-start(bf16[4,64,128]{2,1,0:T(8,128)(2,1)} %get-tuple-element.66.refs_0_), channel_id=1, source_target_pairs={{0,48},{8,56},{16,0},{24,8},{32,16},{40,24},{48,32},{56,40},{1,49}... | collective-permute-start | bytes 196616 | tf_op jit(solution)/shard_map/ppermute | solution.py:328
  144.8 7.8 %collective-permute-start.13 = (bf16[4,64,128]{2,1,0:T(8,128)(2,1)}, bf16[4,64,128]{2,1,0:T(8,128)(2,1)S(1)}, u32[]{:S(2)}, u32[]{:S(2)}) collective-permute-start(bf16[4,64,128]{2,1,0:T(8,128)(2,1)} %get-tuple-element.66.refs_0_), channel_id=1, source_target_pairs={{0,16},{8,24},{16,32},{24,40},{32,48},{40,56},{48,0},{56,8},{1,17}... | collective-permute-start | bytes 196616 | tf_op jit(solution)/shard_map/ppermute | solution.py:328
  147.1 5.5 %collective-permute-start.12 = (bf16[4,64,128]{2,1,0:T(8,128)(2,1)}, bf16[4,64,128]{2,1,0:T(8,128)(2,1)S(1)}, u32[]{:S(2)}, u32[]{:S(2)}) collective-permute-start(bf16[4,64,128]{2,1,0:T(8,128)(2,1)} %get-tuple-element.66.refs_0_), channel_id=1, source_target_pairs={{0,40},{8,48},{16,56},{24,0},{32,8},{40,16},{48,24},{56,32},{1,41}... | collective-permute-start | bytes 196616 | tf_op jit(solution)/shard_map/ppermute | solution.py:328
  148.3 10.1 %copy-start.11 = (bf16[4,64,128]{2,1,0:T(8,128)(2,1)}, bf16[4,64,128]{2,1,0:T(8,128)(2,1)S(1)}, u32[]{:S(2)}) copy-start(bf16[4,64,128]{2,1,0:T(8,128)(2,1)S(1)} %collective-permute-done.16.refs_7_) | copy-start | bytes 196612
  148.3 6.9 %collective-permute-start.11 = (bf16[4,64,128]{2,1,0:T(8,128)(2,1)}, bf16[4,64,128]{2,1,0:T(8,128)(2,1)S(1)}, u32[]{:S(2)}, u32[]{:S(2)}) collective-permute-start(bf16[4,64,128]{2,1,0:T(8,128)(2,1)} %get-tuple-element.66.refs_0_), channel_id=1, source_target_pairs={{0,24},{8,32},{16,40},{24,48},{32,56},{40,0},{48,8},{56,16},{1,25}... | collective-permute-start | bytes 196616 | tf_op jit(solution)/shard_map/ppermute | solution.py:328
  150.4 8.0 %copy-start.13 = (bf16[4,64,128]{2,1,0:T(8,128)(2,1)}, bf16[4,64,128]{2,1,0:T(8,128)(2,1)S(1)}, u32[]{:S(2)}) copy-start(bf16[4,64,128]{2,1,0:T(8,128)(2,1)S(1)} %collective-permute-done.15.refs_6_) | copy-start | bytes 196612
  150.4 8.0 %collective-permute-start.10 = (bf16[4,64,128]{2,1,0:T(8,128)(2,1)}, bf16[4,64,128]{2,1,0:T(8,128)(2,1)}, u32[]{:S(2)}, u32[]{:S(2)}) collective-permute-start(bf16[4,64,128]{2,1,0:T(8,128)(2,1)} %get-tuple-element.66.refs_0_), channel_id=1, source_target_pairs={{0,32},{8,40},{16,48},{24,56},{32,0},{40,8},{48,16},{56,24},{1,33}... | collective-permute-start | bytes 196616 | tf_op jit(solution)/shard_map/ppermute | solution.py:328
  160.9 25.4 %all-to-all-start.5 = ((bf16[64,64,128]{2,1,0:T(8,128)(2,1)}), bf16[64,64,128]{2,1,0:T(8,128)(2,1)}, u32[]{:S(2)}, u32[]{:S(2)}) async-start(bf16[64,64,128]{2,1,0:T(8,128)(2,1)} %pick.7), calls=%async_computation.5 | async-start | bytes 2097152 | tf_op jit(solution)/shard_map/all_to_all | solution.py:390
  168.9 8.2 %collective-permute-start.9 = (bf16[2,4,128,128]{3,2,1,0:T(8,128)(2,1)}, bf16[2,4,128,128]{3,2,1,0:T(8,128)(2,1)}, u32[]{:S(2)}, u32[]{:S(2)}) collective-permute-start(bf16[2,4,128,128]{3,2,1,0:T(8,128)(2,1)} %get-tuple-element.61.refs_0_.own_ref), channel_id=1, source_target_pairs={{0,3},{1,0},{2,1},{3,2},{4,7},{5,4},{6,5},{7,6},{8,11},{9,8},{10,9... | collective-permute-start | bytes 786440 | tf_op jit(solution)/shard_map/ppermute | solution.py:328
  169.9 14.7 %collective-permute-start.8 = (bf16[2,4,128,128]{3,2,1,0:T(8,128)(2,1)}, bf16[2,4,128,128]{3,2,1,0:T(8,128)(2,1)}, u32[]{:S(2)}, u32[]{:S(2)}) collective-permute-start(bf16[2,4,128,128]{3,2,1,0:T(8,128)(2,1)} %get-tuple-element.61.refs_0_.own_ref), channel_id=1, source_target_pairs={{0,1},{1,2},{2,3},{3,0},{4,5},{5,6},{6,7},{7,4},{8,9},{9,10},{10,1... | collective-permute-start | bytes 786440 | tf_op jit(solution)/shard_map/ppermute | solution.py:328
  170.4 14.2 %collective-permute-start.7 = (bf16[2,4,128,128]{3,2,1,0:T(8,128)(2,1)}, bf16[2,4,128,128]{3,2,1,0:T(8,128)(2,1)}, u32[]{:S(2)}, u32[]{:S(2)}) collective-permute-start(bf16[2,4,128,128]{3,2,1,0:T(8,128)(2,1)} %get-tuple-element.61.refs_0_.own_ref), channel_id=1, source_target_pairs={{0,2},{1,3},{2,0},{3,1},{4,6},{5,7},{6,4},{7,5},{8,10},{9,11},{10,... | collective-permute-start | bytes 786440 | tf_op jit(solution)/shard_map/ppermute | solution.py:328
  192.4 4.2 %collective-permute-start.19 = (bf16[544,128]{1,0:T(8,128)(2,1)}, bf16[544,128]{1,0:T(8,128)(2,1)S(1)}, u32[]{:S(2)}, u32[]{:S(2)}) collective-permute-start(bf16[544,128]{1,0:T(8,128)(2,1)} %far.3.refs_0_), channel_id=1, source_target_pairs={{0,3},{1,0},{2,1},{3,2},{4,7},{5,4},{6,5},{7,6},{8,11},{9,8},{10,9... | collective-permute-start | bytes 417800 | tf_op jit(solution)/shard_map/ppermute | solution.py:328
  193.0 5.5 %collective-permute-start.18 = (bf16[544,128]{1,0:T(8,128)(2,1)}, bf16[544,128]{1,0:T(8,128)(2,1)S(1)}, u32[]{:S(2)}, u32[]{:S(2)}) collective-permute-start(bf16[544,128]{1,0:T(8,128)(2,1)} %far.3.refs_0_), channel_id=1, source_target_pairs={{0,1},{1,2},{2,3},{3,0},{4,5},{5,6},{6,7},{7,4},{8,9},{9,10},{10,1... | collective-permute-start | bytes 417800 | tf_op jit(solution)/shard_map/ppermute | solution.py:328
  194.0 7.4 %collective-permute-start.17 = (bf16[544,128]{1,0:T(8,128)(2,1)}, bf16[544,128]{1,0:T(8,128)(2,1)S(1)}, u32[]{:S(2)}, u32[]{:S(2)}) collective-permute-start(bf16[544,128]{1,0:T(8,128)(2,1)} %far.3.refs_0_), channel_id=1, source_target_pairs={{0,2},{1,3},{2,0},{3,1},{4,6},{5,7},{6,4},{7,5},{8,10},{9,11},{10,... | collective-permute-start | bytes 417800 | tf_op jit(solution)/shard_map/ppermute | solution.py:328
  (16 other events, 49.9 us)

commit v2 on v0

--- a/solution.py
+++ b/solution.py
@@ -16,13 +16,16 @@
 NY, NZ, NC, NX = 4, 8, 2, 4
 WIDTH = 64
 GROUP = 4
+STEP = 4
 BUCKETS = 2 * BPD
 MAXG = TPD // GROUP + BUCKETS
 SLOTS = MAXG * GROUP
 SHIFTS = (0, 2, 1, 3)
+ZSHIFTS = (0, 4, 3, 5, 2, 6, 1, 7)
 DEPTH = 4
 FULL = 63 << 20
-MOST = 65_300_000
+MOST = 65_000_000
+TIGHT = 66_200_000
 ROOM = 63_600_000
 EPS = 1e-06
 bf16 = jnp.bfloat16
@@ -84,29 +87,39 @@
     sq_ref[...] = jnp.concatenate(rows, axis=0)
 
 
-def norm_kernel(hop, raw_ref, sq_ref, *rest):
+def norm_kernel(raw_ref, sq_ref, out_ref, own_ref, buf, sem):
     columns = row_scale(sq_ref[...])
-    before_ref = rest[0] if hop else None
-    out_ref, own_ref, buf, sem = rest[-4:]
     copies = []
     for p in range(PAIRS):
         v = (raw_ref[p].astype(f32) * pair_scale(columns, p)).astype(bf16)
         buf[p] = v
-        own_ref[hop, p] = v
+        own_ref[0, p] = v
     for z in range(NZ):
         copy = pltpu.make_async_copy(buf, out_ref.at[z], sem.at[z])
         copy.start()
         copies.append(copy)
-    if hop:
-        own_ref[0:hop] = before_ref[...]
     for copy in copies:
         copy.wait()
 
 
-def pick_kernel(me_ref, idx_ref, z_ref, out_ref, slots, buf, sem):
-    for z in range(NZ):
+def pick_kernel(raw, me_ref, idx_ref, z_ref, *refs):
+    out_ref, slots, buf, sem = refs[0], *refs[-3:]
+    if raw:
+        u_ref, before_ref = refs[0], refs[1]
+        sum_refs = refs[2 : 2 + NZ]
+        out_ref, own_ref = refs[2 + NZ], refs[3 + NZ]
+        columns = row_scale(sum_refs[0][...])
+        for p in range(PAIRS):
+            own_ref[1, p] = (u_ref[p] * pair_scale(columns, p)).astype(bf16)
+        own_ref[0] = before_ref[0]
+    for j in range(NZ):
+        z = (me_ref[1] + NZ - ZSHIFTS[j]) % NZ if raw else j
+        if raw:
+            columns = row_scale(sum_refs[j][...])
         for p in range(PAIRS):
             v = z_ref[z, p]
+            if raw:
+                v = (v.astype(f32) * pair_scale(columns, p)).astype(bf16)
             slots[z * BPD + p] = v
             slots[z * BPD + PAIRS + p] = jnp.concatenate([v[:, WIDTH:], v[:, :WIDTH]], axis=1)
     mask = lane_low((BLK, BLK))
@@ -186,14 +199,14 @@
 
 
 def add_groups(kind, tile_ref, slab_ref, into_ref, groups_ref, tiles_ref, src, acc, ring, sem):
-    steps = (groups_ref[kind] + 1) // 2
+    steps = (groups_ref[kind] + STEP - 1) // STEP
 
     def copies(step):
         slot = step % DEPTH
-        first = (kind * MAXG + 2 * step) * GROUP
+        first = (kind * MAXG + STEP * step) * GROUP
         return [
             pltpu.make_async_copy(tiles_ref.at[tile_ref[first + j]], ring.at[slot, j], sem.at[slot, j])
-            for j in range(2 * GROUP)
+            for j in range(STEP * GROUP)
         ]
 
     def begin(step):
@@ -204,15 +217,15 @@
 
     def run(step, carry):
         slot = step % DEPTH
-        group = kind * MAXG + 2 * step
+        group = kind * MAXG + STEP * step
         for copy in copies(step):
             copy.wait()
         parts = []
-        for h in range(2):
+        for h in range(STEP):
             left = jnp.concatenate([ring[slot, h * GROUP + j] for j in range(GROUP)], axis=1)
             right = jnp.concatenate([src[slab_ref[(group + h) * GROUP + j]] for j in range(GROUP)], axis=0)
             parts.append(jnp.dot(left, right, preferred_element_type=f32))
-        for h in range(2):
+        for h in range(STEP):
             acc[into_ref[group + h]] += parts[h]
         begin(step + DEPTH)
         return carry
@@ -220,43 +233,53 @@
     return begin, lambda: lax.fori_loop(0, steps, run, 0)
 
 
-def own_kernel(hop, tile_ref, slab_ref, into_ref, groups_ref, tiles_ref, own_ref, acc_ref, src, ring, sem):
-    begin, run = add_groups(0, tile_ref, slab_ref, into_ref, groups_ref, tiles_ref, src, acc_ref, ring, sem)
-    for step in range(DEPTH):
-        begin(step)
-    acc_ref[...] = jnp.zeros_like(acc_ref)
-    src[0:PAIRS] = own_ref[hop]
-    src[PAIRS] = jnp.zeros((BLK, BLK), bf16)
-    run()
-
-
-def far_kernel(hop, tile_ref, slab_ref, into_ref, groups_ref, tiles_ref, got_ref, part_ref, noise_ref, *rest):
-    last = hop == HOPS - 1
-    if last:
-        out_ref, acc, noise, ring, sem, load = rest
-    else:
-        out_ref, sq_ref, acc, noise, ring, sem, load = rest
-    begin, run = add_groups(1, tile_ref, slab_ref, into_ref, groups_ref, tiles_ref, got_ref, acc, ring, sem)
+def fold(acc, p):
+    return jnp.where(
+        lane_low((BLK, BLK)),
+        acc[4 * p] + swap_halves(acc[4 * p + 1]),
+        swap_halves(acc[4 * p + 2]) + acc[4 * p + 3],
+    )
+
+
+def own_kernel(hop, tile_ref, slab_ref, into_ref, groups_ref, tiles_ref, own_ref, noise_ref, part_ref, acc, src, noise, ring, sem, load):
+    begin, run = add_groups(0, tile_ref, slab_ref, into_ref, groups_ref, tiles_ref, src, acc, ring, sem)
     for step in range(DEPTH):
         begin(step)
     noise_copy = pltpu.make_async_copy(noise_ref.at[hop], noise, load)
     noise_copy.start()
-    acc[...] = part_ref[...]
+    acc[...] = jnp.zeros_like(acc)
+    src[0:PAIRS] = own_ref[hop]
+    src[PAIRS] = jnp.zeros((BLK, BLK), bf16)
     run()
     noise_copy.wait()
-    mask = lane_low((BLK, BLK))
+    for p in range(PAIRS):
+        part_ref[p] = stacked_pair(noise, p).T + fold(acc, p)
+
+
+def far_kernel(hop, tile_ref, slab_ref, into_ref, groups_ref, tiles_ref, got_ref, part_ref, *rest):
+    last = hop == HOPS - 1
+    if last:
+        out_ref, acc, ring, sem = rest
+    else:
+        out_ref, u_ref, sq_ref, acc, ring, sem, buf, out_sem = rest
+    begin, run = add_groups(1, tile_ref, slab_ref, into_ref, groups_ref, tiles_ref, got_ref, acc, ring, sem)
+    for step in range(DEPTH):
+        begin(step)
+    acc[...] = jnp.zeros_like(acc)
+    run()
     pairs = []
     for p in range(PAIRS):
-        u = stacked_pair(noise, p).T + jnp.where(
-            mask,
-            acc[4 * p] + swap_halves(acc[4 * p + 1]),
-            swap_halves(acc[4 * p + 2]) + acc[4 * p + 3],
-        )
+        u = part_ref[p] + fold(acc, p)
         pairs.append(u)
         if last:
             out_ref[p * BLK : (p + 1) * BLK] = u.astype(bf16)
         else:
-            out_ref[p] = u
+            buf[p] = u.astype(bf16)
+            u_ref[p] = u
+    if not last:
+        copies = [pltpu.make_async_copy(buf, out_ref.at[z], out_sem.at[z]) for z in range(NZ)]
+        for copy in copies:
+            copy.start()
     total = pair_squares(pairs)
     if last:
         hi = total.astype(bf16).astype(f32)
@@ -266,6 +289,8 @@
         out_ref[PAIRS * BLK + 16 : PAIRS * BLK + 32] = jnp.concatenate([lo, jnp.zeros_like(lo)], axis=0).astype(bf16)
     else:
         sq_ref[...] = total
+        for copy in copies:
+            copy.wait()
 
 
 def early_kernel(x_ref, w_ref, *refs):
@@ -350,15 +375,13 @@
     for hop in range(HOPS):
         last = hop == HOPS - 1
         total = lax.psum(squares, "x")
-        before = [owned] if hop else []
-        packed, owned = call(
-            functools.partial(norm_kernel, hop), "norm", [whole()] * (2 + hop),
-            [((NZ, PAIRS, BLK, BLK), bf16, HBM), ((hop + 1, PAIRS, BLK, BLK), bf16, VMEM)],
-            [VMEM((PAIRS, BLK, BLK), bf16), DMA((NZ,))],
-            limit=MOST,
-        )(packed, total, *before)
-        if last:
-            spread = [owned] + [shift_by(owned, "x", shift) for shift in SHIFTS[1:]]
+        if not hop:
+            packed, owned = call(
+                norm_kernel, "norm", [whole()] * 2,
+                [((NZ, PAIRS, BLK, BLK), bf16, HBM), ((1, PAIRS, BLK, BLK), bf16, VMEM)],
+                [VMEM((PAIRS, BLK, BLK), bf16), DMA((NZ,))],
+                limit=TIGHT,
+            )(packed, total)
         along = lax.all_to_all(packed, "z", 0, 0, tiled=True)
         if table is None:
             needed, owned = lax.optimization_barrier((needed, owned))
@@ -366,37 +389,45 @@
             asked = lax.dynamic_slice(asked, (0, me[0], 0, me[2], 0), (NY * NC, 1, NZ, 1, 2)).reshape(NY * NC, NZ, 2)
             odd = (asked % 2) ^ jnp.arange(2, dtype=jnp.int32)
             table = (jnp.arange(NZ, dtype=jnp.int32)[:, None] * BPD + asked // 2 + PAIRS * odd).reshape(-1)
-        picked = call(
-            pick_kernel, "pick", [whole(SMEM)] * 2 + [whole()],
-            [((NY * NC * NZ, BLK, BLK), bf16, HBM)],
-            [VMEM((NZ * BPD, BLK, BLK), bf16), VMEM((NY * NC * NZ, BLK, BLK), bf16), DMA((NY * NC,))],
-            limit=MOST,
-        )(me, table, along)
+        scratch = [VMEM((NZ * BPD, BLK, BLK), bf16), VMEM((NY * NC * NZ, BLK, BLK), bf16), DMA((NY * NC,))]
+        outs = [((NY * NC * NZ, BLK, BLK), bf16, HBM)]
+        if hop:
+            totals = [total] + [shift_by(total, "z", shift) for shift in ZSHIFTS[1:]]
+            picked, owned = call(
+                functools.partial(pick_kernel, True), "pick", [whole(SMEM)] * 2 + [whole()] * (3 + NZ),
+                outs + [((2, PAIRS, BLK, BLK), bf16, VMEM)], scratch, limit=MOST,
+            )(me, table, along, values, owned, *totals)
+            spread = [owned] + [shift_by(owned, "x", shift) for shift in SHIFTS[1:]]
+        else:
+            picked = call(
+                functools.partial(pick_kernel, False), "pick", [whole(SMEM)] * 2 + [whole()], outs, scratch, limit=MOST
+            )(me, table, along)
         got = lax.all_to_all(picked, ("y", "core"), 0, 0, tiled=True)
-        ring = [VMEM((DEPTH, 2 * GROUP, BLK, BLK), bf16), DMA((DEPTH, 2 * GROUP))]
+        ring = [VMEM((DEPTH, STEP * GROUP, BLK, BLK), bf16), DMA((DEPTH, STEP * GROUP))]
         part = call(
-            functools.partial(own_kernel, hop), "own", [whole(SMEM)] * 4 + [whole(HBM), whole()], [((BUCKETS, BLK, BLK), f32, VMEM)],
-            [VMEM((PAIRS + 1, BLK, BLK), bf16)] + ring,
+            functools.partial(own_kernel, hop), "own", [whole(SMEM)] * 4 + [whole(HBM), whole(), whole(HBM)],
+            [((PAIRS, BLK, BLK), f32, VMEM)],
+            [VMEM((BUCKETS, BLK, BLK), f32), VMEM((PAIRS + 1, BLK, BLK), bf16), VMEM((WIDTH, BPD * BLK), f32)] + ring + [DMA(())],
             limit=FULL, flops=TPD * 2 * BLK**3, moved=4 << 20,
-        )(*lists, tile_vals, owned)
+        )(*lists, tile_vals, owned, noise)
         if last:
             early = call(
                 early_kernel, "early", [whole(SMEM)] + [whole()] * (1 + NX), [((PAIRS, BLK, BLK), f32, VMEM)]
             )(x_only, weights, *spread)
+            early, part = lax.optimization_barrier((early, part))
         if last:
             outs = [((PAIRS * BLK + 32, BLK), bf16, VMEM)]
+            more = []
         else:
-            outs = [((PAIRS, BLK, BLK), f32, VMEM), ((BPD, BLK), f32, VMEM)]
+            outs = [((NZ, PAIRS, BLK, BLK), bf16, HBM), ((PAIRS, BLK, BLK), f32, VMEM), ((BPD, BLK), f32, VMEM)]
+            more = [VMEM((PAIRS, BLK, BLK), bf16), DMA((NZ,))]
         result = call(
-            functools.partial(far_kernel, hop), "far", [whole(SMEM)] * 4 + [whole(HBM), whole(), whole(), whole(HBM)], outs,
-            [
-                VMEM((BUCKETS, BLK, BLK), f32),
-                VMEM((WIDTH, BPD * BLK), f32),
-            ] + ring + [DMA(())],
+            functools.partial(far_kernel, hop), "far", [whole(SMEM)] * 4 + [whole(HBM), whole(), whole()], outs,
+            [VMEM((BUCKETS, BLK, BLK), f32)] + ring + more,
             limit=ROOM, flops=TPD * 2 * BLK**3, moved=8 << 20,
-        )(*lists, tile_vals, got, part, noise)
+        )(*lists, tile_vals, got, part)
         if not last:
-            packed, squares = result
+            packed, values, squares = result
     tails = [result] + [shift_by(result, "x", shift) for shift in SHIFTS[1:]]
     return call(
         final_kernel, "final", [whole(SMEM)] + [whole()] * (2 + NX), [((WIDTH, BPD * BLK), bf16, VMEM)]

time: 192 us -> 195 us (1.016)
  blocking collectives: 61 us -> 29.5 us
  starting transfers between devices: 30.7 us -> 49.2 us
  waiting for transfers between devices: 48.7 us -> 55.4 us
  Pallas kernels: 41.7 us -> 47.5 us
    all_to_all x1 -> x0, blocking collectives: 30.7 us -> none  [shards(): along = lax.all_to_all(packed, 'z', 0, 0, tiled=True)]
    ppermute x6 -> x13, waiting for transfers between devices: 4.82 us -> 22 us  [shift_by(): lax.ppermute(value, axis, [(i, (i + shift) % size) for i in range(size)])]
    ppermute x6 -> x13, starting transfers between devices: 7.65 us -> 18.3 us  [shift_by(): lax.ppermute(value, axis, [(i, (i + shift) % size) for i in range(size)])]
    all_to_all x2, waiting for transfers between devices: 32.4 us -> 21.9 us  [shards(): got = lax.all_to_all(picked, ('y', 'core'), 0, 0, tiled=True)]
    all_to_all x2, starting transfers between devices: 14.9 us -> 19.1 us  [shards(): got = lax.all_to_all(picked, ('y', 'core'), 0, 0, tiled=True)]
    all_to_all x1 -> x2, starting transfers between devices: 8.2 us -> 11.8 us  [shards(): along = lax.all_to_all(packed, 'z', 0, 0, tiled=True)]
    pallas_call x2, Pallas kernels: 8.3 us -> 10.4 us  [shards(): call(functools.partial(own_kernel, hop), 'own', [whole(SMEM)] * 4 + [whol...]
    unnamed x29 -> x45, local copies, waits for them, and re-layouts: 5.71 us -> 7.52 us
  transfers between devices with their start and end apart: 9 -> 17, of which waited for: 5 -> 12; matrix products, arithmetic and copies ran while one was open for 1% -> 1% of each run, Pallas kernels for 11% -> 10%
where the time goes in v2:
time: 195 us; the launch traced here: 192 us
  waiting for transfers between devices  55.4 us (28%)
  starting transfers between devices  49.2 us (25%)
  Pallas kernels  47.5 us (24%)
  blocking collectives  29.5 us (15%)
  local copies, waits for them, and re-layouts  8.5 us (4%)
    ppermute x13, waiting for transfers between devices, shift_by(): lax.ppermute(value, axis, [(i, (i + shift) % size) for i in range(size)])  22 us
    all_to_all x2, waiting for transfers between devices, shards(): got = lax.all_to_all(picked, ('y', 'core'), 0, 0, tiled=True)  21.9 us
    all_to_all x2, starting transfers between devices, shards(): got = lax.all_to_all(picked, ('y', 'core'), 0, 0, tiled=True)  19.1 us
    ppermute x13, starting transfers between devices, shift_by(): lax.ppermute(value, axis, [(i, (i + shift) % size) for i in range(size)])  18.3 us
    psum x2, blocking collectives, shards(): total = lax.psum(squares, 'x')  15.8 us
    all_gather x1, blocking collectives, shards(): lax.all_gather(needed, ('y', 'core'), axis=0)  13.6 us
    pallas_call x2, Pallas kernels, shards(): call(functools.partial(far_kernel, hop), 'far', [whole(SMEM)] * 4 + [whol...  13.3 us
    all_to_all x2, starting transfers between devices, shards(): along = lax.all_to_all(packed, 'z', 0, 0, tiled=True)  11.8 us
  transfers between devices with their start and end apart: 17, of which 12 were waited for; matrix products, arithmetic and copies ran while one was open for 1% of the time, Pallas kernels for 10%

profile of v2, /device:TPU:1, one launch (start us, length us, event | category | flops | bytes accessed | tf_op | source)
XLA Modules:
  0.0 192.4 jit_solution(21062367763916369)
XLA Ops:
  2.6 9.8 %psum.14.sq_ref = f32[8,128]{1,0:T(8,128)} all-reduce(f32[8,128]{1,0:T(8,128)S(1)} %get-tuple-element.35), channel_id=1, replica_groups=mesh['y'=4,'z'=8,'core'=2,'x'=4] {'x'}, use_global_device_ids=true, to_apply=%region_0.0 | all-reduce | flops 1024 | bytes 8192 | tf_op jit(solution)/shard_map/psum | solution.py:377
  12.5 3.0 %norm.1 = (bf16[8,4,128,128]{3,2,1,0:T(8,128)(2,1)}, bf16[1,4,128,128]{3,2,1,0:T(8,128)(2,1)}) custom-call(bf16[4,128,128]{2,1,0:T(8,128)(2,1)} %copy-done.3, f32[8,128]{1,0:T(8,128)} %psum.14.sq_ref), custom_call_target="tpu_custom_call" | custom-call | flops 1048576 | bytes 1048576 | tf_op jit(solution)/shard_map/norm/pallas_call | solution.py:379
  15.4 8.2 %all-to-all-start = ((bf16[8,4,128,128]{3,2,1,0:T(8,128)(2,1)}), bf16[8,4,128,128]{3,2,1,0:T(8,128)(2,1)S(1)}, u32[]{:S(2)}, u32[]{:S(2)}) async-start(bf16[8,4,128,128]{3,2,1,0:T(8,128)(2,1)} %get-tuple-element.46), calls=%async_computation | async-start | bytes 2097152 | tf_op jit(solution)/shard_map/all_to_all | solution.py:385
  24.0 13.6 %all-gather.1 = s32[8,1,128]{2,1,0:T(1,128)S(1)} all-gather(s32[1,1,128]{2,1,0:T(1,128)S(1)} %bitcast.23), channel_id=2, replica_groups=mesh['y'=4,'z'=8,'core'=2,'x'=4] {'y','core'}, dimensions={0}, use_global_device_ids=true | all-gather | bytes 4608 | tf_op jit(solution)/shard_map/all_gather | solution.py:388
  39.1 11.5 %all-to-all-done.z_ref = bf16[8,4,128,128]{3,2,1,0:T(8,128)(2,1)S(1)} async-done(((bf16[8,4,128,128]{3,2,1,0:T(8,128)(2,1)}), bf16[8,4,128,128]{3,2,1,0:T(8,128)(2,1)S(1)}, u32[]{:S(2)}, u32[]{:S(2)}) %all-to-all-start) | async-done | bytes 1048608 | tf_op jit(solution)/shard_map/all_to_all | solution.py:385
  51.7 3.1 %pick.2 = bf16[64,128,128]{2,1,0:T(8,128)(2,1)} custom-call(s32[3]{0:T(128)} %pad_add_fusion.me_ref, s32[128]{0:T(128)} %multiply_add_fusion.idx_ref, bf16[8,4,128,128]{3,2,1,0:T(8,128)(2,1)} %copy-done.12), custom_call_target="tpu_custom_call" | custom-call | flops 1048576 | bytes 1048576 | tf_op jit(solution)/shard_map/pick/pallas_call | solution.py:402
  54.8 7.2 %all-to-all-start.1 = ((bf16[64,128,128]{2,1,0:T(8,128)(2,1)}), bf16[64,128,128]{2,1,0:T(8,128)(2,1)}, u32[]{:S(2)}, u32[]{:S(2)}) async-start(bf16[64,128,128]{2,1,0:T(8,128)(2,1)} %pick.2), calls=%async_computation.1 | async-start | bytes 4194304 | tf_op jit(solution)/shard_map/all_to_all | solution.py:405
  62.7 7.0 %order.1 = (s32[448]{0:T(512)S(1)}, s32[448]{0:T(512)S(1)}, s32[112]{0:T(128)S(1)}, s32[2]{0:T(128)S(1)}) custom-call(s32[3]{0:T(128)S(1)} %copy-done.8, s32[160]{0:T(256)S(1)} %bitcast.17, s32[160]{0:T(256)S(1)} %bitcast.18, s32[1]{0:T(128)S(6)} %copy.17.count_ref), custom_call_target="tpu_custom_call" | custom-call | flops 1048576 | bytes 1048576 | tf_op jit(solution)/shard_map/order/pallas_call | solution.py:369
  72.0 5.2 %own.2.part_ref = f32[4,128,128]{2,1,0:T(8,128)} custom-call(s32[448]{0:T(512)} %copy-done.4, s32[448]{0:T(512)} %copy-done.5, s32[112]{0:T(128)} %copy-done.6, s32[2]{0:T(128)} %copy-done.7, bf16[160,128,128]{2,1,0:T(8,128)(2,1)} %tiles_ref.3, bf16[1,4,128,128]{3,2,1,0:T(8,128)(2,1)} %get-tuple-element.47.own_ref.refs_1_, f32[2,64,1024]{2,1,0:T(8,128)} %bitcast.19), custom_call_target="tpu_custom_call" | custom-call | flops 671088640 | bytes 4194304 | tf_op jit(solution)/shard_map/own/pallas_call | solution.py:407
  77.2 11.1 %all-to-all-done.1.got_ref = bf16[64,128,128]{2,1,0:T(8,128)(2,1)} async-done(((bf16[64,128,128]{2,1,0:T(8,128)(2,1)}), bf16[64,128,128]{2,1,0:T(8,128)(2,1)}, u32[]{:S(2)}, u32[]{:S(2)}) %all-to-all-start.1) | async-done | bytes 2097184 | tf_op jit(solution)/shard_map/all_to_all | solution.py:405
  88.3 7.0 %far.2 = (bf16[8,4,128,128]{3,2,1,0:T(8,128)(2,1)}, f32[4,128,128]{2,1,0:T(8,128)}, f32[8,128]{1,0:T(8,128)}) custom-call(s32[448]{0:T(512)} %copy-done.4, s32[448]{0:T(512)} %copy-done.5, s32[112]{0:T(128)} %copy-done.6, s32[2]{0:T(128)} %copy-done.7, bf16[160,128,128]{2,1,0:T(8,128)(2,1)} %tiles_ref.3, bf16[64,128,128]{2,1,0:T(8,128)(2,1)} %all-to-all-done.1.got_ref, ...), custom_call_target="tpu_custom_call" | custom-call | flops 671088640 | bytes 8388608 | tf_op jit(solution)/shard_map/far/pallas_call | solution.py:424
  95.3 3.6 %all-to-all-start.2 = ((bf16[8,4,128,128]{3,2,1,0:T(8,128)(2,1)}), bf16[8,4,128,128]{3,2,1,0:T(8,128)(2,1)S(1)}, u32[]{:S(2)}, u32[]{:S(2)}) async-start(bf16[8,4,128,128]{3,2,1,0:T(8,128)(2,1)} %get-tuple-element.48), calls=%async_computation.2 | async-start | bytes 2097152 | tf_op jit(solution)/shard_map/all_to_all | solution.py:385
  98.9 6.0 %psum.15.refs_2_ = f32[8,128]{1,0:T(8,128)S(1)} all-reduce(f32[8,128]{1,0:T(8,128)S(1)} %copy-done.21), channel_id=1, replica_groups=mesh['y'=4,'z'=8,'core'=2,'x'=4] {'x'}, use_global_device_ids=true, to_apply=%region_1.2 | all-reduce | flops 1024 | bytes 8192 | tf_op jit(solution)/shard_map/psum | solution.py:377
  104.9 3.0 %collective-permute-start.6 = (f32[8,128]{1,0:T(8,128)S(1)}, f32[8,128]{1,0:T(8,128)S(1)}, u32[]{:S(2)}, u32[]{:S(2)}) collective-permute-start(f32[8,128]{1,0:T(8,128)S(1)} %psum.15.refs_2_), channel_id=1, source_target_pairs={{0,56},{8,0},{16,8},{24,16},{32,24},{40,32},{48,40},{56,48},{1,57}... | collective-permute-start | bytes 12296 | tf_op jit(solution)/shard_map/ppermute | solution.py:347
  107.9 2.6 %collective-permute-start.4 = (f32[8,128]{1,0:T(8,128)S(1)}, f32[8,128]{1,0:T(8,128)S(1)}, u32[]{:S(2)}, u32[]{:S(2)}) collective-permute-start(f32[8,128]{1,0:T(8,128)S(1)} %psum.15.refs_2_), channel_id=1, source_target_pairs={{0,48},{8,56},{16,0},{24,8},{32,16},{40,24},{48,32},{56,40},{1,49}... | collective-permute-start | bytes 12296 | tf_op jit(solution)/shard_map/ppermute | solution.py:347
  110.6 3.3 %collective-permute-start.2 = (f32[8,128]{1,0:T(8,128)S(1)}, f32[8,128]{1,0:T(8,128)S(1)}, u32[]{:S(2)}, u32[]{:S(2)}) collective-permute-start(f32[8,128]{1,0:T(8,128)S(1)} %psum.15.refs_2_), channel_id=1, source_target_pairs={{0,40},{8,48},{16,56},{24,0},{32,8},{40,16},{48,24},{56,32},{1,41}... | collective-permute-start | bytes 12296 | tf_op jit(solution)/shard_map/ppermute | solution.py:347
  113.8 7.4 %collective-permute-done.6.refs_9_ = f32[8,128]{1,0:T(8,128)S(1)} collective-permute-done((f32[8,128]{1,0:T(8,128)S(1)}, f32[8,128]{1,0:T(8,128)S(1)}, u32[]{:S(2)}, u32[]{:S(2)}) %collective-permute-start.6) | collective-permute-done | bytes 4128 | tf_op jit(solution)/shard_map/ppermute | solution.py:347
  121.3 5.2 %collective-permute-start = (f32[8,128]{1,0:T(8,128)S(1)}, f32[8,128]{1,0:T(8,128)S(1)}, u32[]{:S(2)}, u32[]{:S(2)}) collective-permute-start(f32[8,128]{1,0:T(8,128)S(1)} %psum.15.refs_2_), channel_id=1, source_target_pairs={{0,32},{8,40},{16,48},{24,56},{32,0},{40,8},{48,16},{56,24},{1,33}... | collective-permute-start | bytes 12296 | tf_op jit(solution)/shard_map/ppermute | solution.py:347
  129.3 7.8 %pick.3 = (bf16[64,128,128]{2,1,0:T(8,128)(2,1)}, bf16[2,4,128,128]{3,2,1,0:T(8,128)(2,1)}) custom-call(s32[3]{0:T(128)} %pad_add_fusion.me_ref, s32[128]{0:T(128)} %multiply_add_fusion.idx_ref, bf16[8,4,128,128]{3,2,1,0:T(8,128)(2,1)} %copy-done.11, f32[4,128,128]{2,1,0:T(8,128)} %get-tuple-element.49.refs_0_, ...), custom_call_target="tpu_custom_call" | custom-call | flops 1048576 | bytes 1048576 | tf_op jit(solution)/shard_map/pick/pallas_call | solution.py:396
  137.1 11.9 %all-to-all-start.3 = ((bf16[64,128,128]{2,1,0:T(8,128)(2,1)}), bf16[64,128,128]{2,1,0:T(8,128)(2,1)}, u32[]{:S(2)}, u32[]{:S(2)}) async-start(bf16[64,128,128]{2,1,0:T(8,128)(2,1)} %get-tuple-element.53), calls=%async_computation.3 | async-start | bytes 4194304 | tf_op jit(solution)/shard_map/all_to_all | solution.py:405
  149.1 1.5 collective-permute-start.8
  151.4 5.2 %own.3.part_ref = f32[4,128,128]{2,1,0:T(8,128)} custom-call(s32[448]{0:T(512)} %copy-done.4, s32[448]{0:T(512)} %copy-done.5, s32[112]{0:T(128)} %copy-done.6, s32[2]{0:T(128)} %copy-done.7, bf16[160,128,128]{2,1,0:T(8,128)(2,1)} %tiles_ref.3, bf16[2,4,128,128]{3,2,1,0:T(8,128)(2,1)} %get-tuple-element.51.refs_0_.own_ref, f32[2,64,1024]{2,1,0:T(8,128)} %bitcast.20), custom_call_target="tpu_custom_call" | custom-call | flops 671088640 | bytes 4194304 | tf_op jit(solution)/shard_map/own/pallas_call | solution.py:407
  157.0 1.9 collective-permute-done.8.refs_2_
  158.9 4.1 %collective-permute-done.7.refs_1_ = bf16[2,4,128,128]{3,2,1,0:T(8,128)(2,1)} collective-permute-done((bf16[2,4,128,128]{3,2,1,0:T(8,128)(2,1)}, bf16[2,4,128,128]{3,2,1,0:T(8,128)(2,1)}, u32[]{:S(2)}, u32[]{:S(2)}) %collective-permute-start.7) | collective-permute-done | bytes 262176 | tf_op jit(solution)/shard_map/ppermute | solution.py:347
  163.0 1.6 early.1.early_ref
  164.6 10.8 %all-to-all-done.3.got_ref = bf16[64,128,128]{2,1,0:T(8,128)(2,1)} async-done(((bf16[64,128,128]{2,1,0:T(8,128)(2,1)}), bf16[64,128,128]{2,1,0:T(8,128)(2,1)}, u32[]{:S(2)}, u32[]{:S(2)}) %all-to-all-start.3) | async-done | bytes 2097184 | tf_op jit(solution)/shard_map/all_to_all | solution.py:405
  175.4 6.2 %far.3.refs_0_ = bf16[544,128]{1,0:T(8,128)(2,1)} custom-call(s32[448]{0:T(512)} %copy-done.4, s32[448]{0:T(512)} %copy-done.5, s32[112]{0:T(128)} %copy-done.6, s32[2]{0:T(128)} %copy-done.7, bf16[160,128,128]{2,1,0:T(8,128)(2,1)} %tiles_ref.3, bf16[64,128,128]{2,1,0:T(8,128)(2,1)} %all-to-all-done.3.got_ref, f32[4,128,128]{2,1,0:T(8,128)} %own.3.part_ref), custom_call_target="tpu_custom_call" | custom-call | flops 671088640 | bytes 8388608 | tf_op jit(solution)/shard_map/far/pallas_call | solution.py:424
  181.8 1.5 collective-permute-start.11
  183.8 2.5 %collective-permute-done.12.refs_3_ = bf16[544,128]{1,0:T(8,128)(2,1)S(1)} collective-permute-done((bf16[544,128]{1,0:T(8,128)(2,1)}, bf16[544,128]{1,0:T(8,128)(2,1)S(1)}, u32[]{:S(2)}, u32[]{:S(2)}) %collective-permute-start.12) | collective-permute-done | bytes 139296 | tf_op jit(solution)/shard_map/ppermute | solution.py:347
  186.3 1.3 collective-permute-done.11.refs_2_
  187.5 2.7 %collective-permute-done.10.refs_1_ = bf16[544,128]{1,0:T(8,128)(2,1)S(1)} collective-permute-done((bf16[544,128]{1,0:T(8,128)(2,1)}, bf16[544,128]{1,0:T(8,128)(2,1)S(1)}, u32[]{:S(2)}, u32[]{:S(2)}) %collective-permute-start.10) | collective-permute-done | bytes 139296 | tf_op jit(solution)/shard_map/ppermute | solution.py:347
  191.2 1.2 final.1
  (75 shorter events, 13.3 us)
Async XLA Ops:
  0.0 151.1 %copy-start = (bf16[3,256,256]{2,1,0:T(8,128)(2,1)S(1)}, bf16[3,256,256]{2,1,0:T(8,128)(2,1)}, u32[]{:S(2)}) copy-start(bf16[3,256,256]{2,1,0:T(8,128)(2,1)} %param.15) | copy-start | bytes 1179652
  1.0 0.9 copy-start.2
  15.4 35.2 %all-to-all-start = ((bf16[8,4,128,128]{3,2,1,0:T(8,128)(2,1)}), bf16[8,4,128,128]{3,2,1,0:T(8,128)(2,1)S(1)}, u32[]{:S(2)}, u32[]{:S(2)}) async-start(bf16[8,4,128,128]{3,2,1,0:T(8,128)(2,1)} %get-tuple-element.46), calls=%async_computation | async-start | bytes 2097152 | tf_op jit(solution)/shard_map/all_to_all | solution.py:385
  50.7 1.0 copy-start.12
  54.8 7.9 %copy-start.8 = (s32[3]{0:T(128)S(1)}, s32[3]{0:T(128)}, u32[]{:S(2)}) copy-start(s32[3]{0:T(128)} %pad_add_fusion.me_ref) | copy-start | bytes 40
  54.8 7.9 %copy-start.9 = (s32[1,160]{1,0:T(1,128)S(1)}, s32[1,160]{1,0:T(1,128)}, u32[]{:S(2)}) copy-start(s32[1,160]{1,0:T(1,128)} %param.10) | copy-start | bytes 1924
  54.8 7.9 %copy-start.10 = (s32[1,160]{1,0:T(1,128)S(1)}, s32[1,160]{1,0:T(1,128)}, u32[]{:S(2)}) copy-start(s32[1,160]{1,0:T(1,128)} %param.11) | copy-start | bytes 1924
  54.8 33.5 %all-to-all-start.1 = ((bf16[64,128,128]{2,1,0:T(8,128)(2,1)}), bf16[64,128,128]{2,1,0:T(8,128)(2,1)}, u32[]{:S(2)}, u32[]{:S(2)}) async-start(bf16[64,128,128]{2,1,0:T(8,128)(2,1)} %pick.2), calls=%async_computation.1 | async-start | bytes 4194304 | tf_op jit(solution)/shard_map/all_to_all | solution.py:405
  95.3 3.6 %copy-start.21 = (f32[8,128]{1,0:T(8,128)S(1)}, f32[8,128]{1,0:T(8,128)}, u32[]{:S(2)}) copy-start(f32[8,128]{1,0:T(8,128)} %get-tuple-element.50) | copy-start | bytes 12292
  95.3 33.0 %all-to-all-start.2 = ((bf16[8,4,128,128]{3,2,1,0:T(8,128)(2,1)}), bf16[8,4,128,128]{3,2,1,0:T(8,128)(2,1)S(1)}, u32[]{:S(2)}, u32[]{:S(2)}) async-start(bf16[8,4,128,128]{3,2,1,0:T(8,128)(2,1)} %get-tuple-element.48), calls=%async_computation.2 | async-start | bytes 2097152 | tf_op jit(solution)/shard_map/all_to_all | solution.py:385
  104.9 23.4 %copy-start.13 = (f32[8,128]{1,0:T(8,128)}, f32[8,128]{1,0:T(8,128)S(1)}, u32[]{:S(2)}) copy-start(f32[8,128]{1,0:T(8,128)S(1)} %psum.15.refs_2_) | copy-start | bytes 12292
  104.9 16.3 %collective-permute-start.6 = (f32[8,128]{1,0:T(8,128)S(1)}, f32[8,128]{1,0:T(8,128)S(1)}, u32[]{:S(2)}, u32[]{:S(2)}) collective-permute-start(f32[8,128]{1,0:T(8,128)S(1)} %psum.15.refs_2_), channel_id=1, source_target_pairs={{0,56},{8,0},{16,8},{24,16},{32,24},{40,32},{48,40},{56,48},{1,57}... | collective-permute-start | bytes 12296 | tf_op jit(solution)/shard_map/ppermute | solution.py:347
  107.9 13.3 %collective-permute-start.5 = (f32[8,128]{1,0:T(8,128)S(1)}, f32[8,128]{1,0:T(8,128)S(1)}, u32[]{:S(2)}, u32[]{:S(2)}) collective-permute-start(f32[8,128]{1,0:T(8,128)S(1)} %psum.15.refs_2_), channel_id=1, source_target_pairs={{0,8},{8,16},{16,24},{24,32},{32,40},{40,48},{48,56},{56,0},{1,9},... | collective-permute-start | bytes 12296 | tf_op jit(solution)/shard_map/ppermute | solution.py:347
  107.9 18.6 %collective-permute-start.4 = (f32[8,128]{1,0:T(8,128)S(1)}, f32[8,128]{1,0:T(8,128)S(1)}, u32[]{:S(2)}, u32[]{:S(2)}) collective-permute-start(f32[8,128]{1,0:T(8,128)S(1)} %psum.15.refs_2_), channel_id=1, source_target_pairs={{0,48},{8,56},{16,0},{24,8},{32,16},{40,24},{48,32},{56,40},{1,49}... | collective-permute-start | bytes 12296 | tf_op jit(solution)/shard_map/ppermute | solution.py:347
  110.5 16.0 %collective-permute-start.3 = (f32[8,128]{1,0:T(8,128)S(1)}, f32[8,128]{1,0:T(8,128)S(1)}, u32[]{:S(2)}, u32[]{:S(2)}) collective-permute-start(f32[8,128]{1,0:T(8,128)S(1)} %psum.15.refs_2_), channel_id=1, source_target_pairs={{0,16},{8,24},{16,32},{24,40},{32,48},{40,56},{48,0},{56,8},{1,17}... | collective-permute-start | bytes 12296 | tf_op jit(solution)/shard_map/ppermute | solution.py:347
  110.6 16.0 %collective-permute-start.2 = (f32[8,128]{1,0:T(8,128)S(1)}, f32[8,128]{1,0:T(8,128)S(1)}, u32[]{:S(2)}, u32[]{:S(2)}) collective-permute-start(f32[8,128]{1,0:T(8,128)S(1)} %psum.15.refs_2_), channel_id=1, source_target_pairs={{0,40},{8,48},{16,56},{24,0},{32,8},{40,16},{48,24},{56,32},{1,41}... | collective-permute-start | bytes 12296 | tf_op jit(solution)/shard_map/ppermute | solution.py:347
  121.2 7.1 %copy-start.14 = (f32[8,128]{1,0:T(8,128)}, f32[8,128]{1,0:T(8,128)S(1)}, u32[]{:S(2)}) copy-start(f32[8,128]{1,0:T(8,128)S(1)} %collective-permute-done.6.refs_9_) | copy-start | bytes 12292
  121.3 6.2 %collective-permute-start.1 = (f32[8,128]{1,0:T(8,128)S(1)}, f32[8,128]{1,0:T(8,128)S(1)}, u32[]{:S(2)}, u32[]{:S(2)}) collective-permute-start(f32[8,128]{1,0:T(8,128)S(1)} %psum.15.refs_2_), channel_id=1, source_target_pairs={{0,24},{8,32},{16,40},{24,48},{32,56},{40,0},{48,8},{56,16},{1,25}... | collective-permute-start | bytes 12296 | tf_op jit(solution)/shard_map/ppermute | solution.py:347
  121.3 7.1 %copy-start.15 = (f32[8,128]{1,0:T(8,128)}, f32[8,128]{1,0:T(8,128)S(1)}, u32[]{:S(2)}) copy-start(f32[8,128]{1,0:T(8,128)S(1)} %collective-permute-done.5.refs_8_) | copy-start | bytes 12292
  121.3 7.0 %collective-permute-start = (f32[8,128]{1,0:T(8,128)S(1)}, f32[8,128]{1,0:T(8,128)S(1)}, u32[]{:S(2)}, u32[]{:S(2)}) collective-permute-start(f32[8,128]{1,0:T(8,128)S(1)} %psum.15.refs_2_), channel_id=1, source_target_pairs={{0,32},{8,40},{16,48},{24,56},{32,0},{40,8},{48,16},{56,24},{1,33}... | collective-permute-start | bytes 12296 | tf_op jit(solution)/shard_map/ppermute | solution.py:347
  126.5 1.8 copy-start.16
  126.5 1.8 copy-start.17
  126.5 1.8 copy-start.18
  127.4 1.0 copy-start.19
  128.3 1.0 copy-start.11
  137.1 38.3 %all-to-all-start.3 = ((bf16[64,128,128]{2,1,0:T(8,128)(2,1)}), bf16[64,128,128]{2,1,0:T(8,128)(2,1)}, u32[]{:S(2)}, u32[]{:S(2)}) async-start(bf16[64,128,128]{2,1,0:T(8,128)(2,1)} %get-tuple-element.53), calls=%async_computation.3 | async-start | bytes 4194304 | tf_op jit(solution)/shard_map/all_to_all | solution.py:405
  149.1 8.0 %collective-permute-start.9 = (bf16[2,4,128,128]{3,2,1,0:T(8,128)(2,1)}, bf16[2,4,128,128]{3,2,1,0:T(8,128)(2,1)}, u32[]{:S(2)}, u32[]{:S(2)}) collective-permute-start(bf16[2,4,128,128]{3,2,1,0:T(8,128)(2,1)} %get-tuple-element.51.refs_0_.own_ref), channel_id=1, source_target_pairs={{0,3},{1,0},{2,1},{3,2},{4,7},{5,4},{6,5},{7,6},{8,11},{9,8},{10,9... | collective-permute-start | bytes 786440 | tf_op jit(solution)/shard_map/ppermute | solution.py:347
  149.1 9.8 %collective-permute-start.8 = (bf16[2,4,128,128]{3,2,1,0:T(8,128)(2,1)}, bf16[2,4,128,128]{3,2,1,0:T(8,128)(2,1)}, u32[]{:S(2)}, u32[]{:S(2)}) collective-permute-start(bf16[2,4,128,128]{3,2,1,0:T(8,128)(2,1)} %get-tuple-element.51.refs_0_.own_ref), channel_id=1, source_target_pairs={{0,1},{1,2},{2,3},{3,0},{4,5},{5,6},{6,7},{7,4},{8,9},{9,10},{10,1... | collective-permute-start | bytes 786440 | tf_op jit(solution)/shard_map/ppermute | solution.py:347
  150.5 12.5 %collective-permute-start.7 = (bf16[2,4,128,128]{3,2,1,0:T(8,128)(2,1)}, bf16[2,4,128,128]{3,2,1,0:T(8,128)(2,1)}, u32[]{:S(2)}, u32[]{:S(2)}) collective-permute-start(bf16[2,4,128,128]{3,2,1,0:T(8,128)(2,1)} %get-tuple-element.51.refs_0_.own_ref), channel_id=1, source_target_pairs={{0,2},{1,3},{2,0},{3,1},{4,6},{5,7},{6,4},{7,5},{8,10},{9,11},{10,... | collective-permute-start | bytes 786440 | tf_op jit(solution)/shard_map/ppermute | solution.py:347
  181.7 4.6 %collective-permute-start.12 = (bf16[544,128]{1,0:T(8,128)(2,1)}, bf16[544,128]{1,0:T(8,128)(2,1)S(1)}, u32[]{:S(2)}, u32[]{:S(2)}) collective-permute-start(bf16[544,128]{1,0:T(8,128)(2,1)} %far.3.refs_0_), channel_id=1, source_target_pairs={{0,3},{1,0},{2,1},{3,2},{4,7},{5,4},{6,5},{7,6},{8,11},{9,8},{10,9... | collective-permute-start | bytes 417800 | tf_op jit(solution)/shard_map/ppermute | solution.py:347
  181.8 5.8 %collective-permute-start.11 = (bf16[544,128]{1,0:T(8,128)(2,1)}, bf16[544,128]{1,0:T(8,128)(2,1)S(1)}, u32[]{:S(2)}, u32[]{:S(2)}) collective-permute-start(bf16[544,128]{1,0:T(8,128)(2,1)} %far.3.refs_0_), channel_id=1, source_target_pairs={{0,1},{1,2},{2,3},{3,0},{4,5},{5,6},{6,7},{7,4},{8,9},{9,10},{10,1... | collective-permute-start | bytes 417800 | tf_op jit(solution)/shard_map/ppermute | solution.py:347
  183.2 7.1 %collective-permute-start.10 = (bf16[544,128]{1,0:T(8,128)(2,1)}, bf16[544,128]{1,0:T(8,128)(2,1)S(1)}, u32[]{:S(2)}, u32[]{:S(2)}) collective-permute-start(bf16[544,128]{1,0:T(8,128)(2,1)} %far.3.refs_0_), channel_id=1, source_target_pairs={{0,2},{1,3},{2,0},{3,1},{4,6},{5,7},{6,4},{7,5},{8,10},{9,11},{10,... | collective-permute-start | bytes 417800 | tf_op jit(solution)/shard_map/ppermute | solution.py:347
  (7 other events, 4.4 us)

commit v3 on v2

--- a/solution.py
+++ b/solution.py
@@ -21,7 +21,8 @@
 MAXG = TPD // GROUP + BUCKETS
 SLOTS = MAXG * GROUP
 SHIFTS = (0, 2, 1, 3)
-ZSHIFTS = (0, 4, 3, 5, 2, 6, 1, 7)
+N_ROW = NY * NZ * NC
+BATCH = 8
 DEPTH = 4
 FULL = 63 << 20
 MOST = 65_000_000
@@ -87,55 +88,38 @@
     sq_ref[...] = jnp.concatenate(rows, axis=0)
 
 
-def norm_kernel(raw_ref, sq_ref, out_ref, own_ref, buf, sem):
-    columns = row_scale(sq_ref[...])
+def send_kernel(hop, me_ref, idx_ref, raw_ref, *refs):
+    sum_refs = refs[:NX]
+    out_ref, own_ref, slots, buf, sem = refs[-5:]
+    total = sum_refs[0][...]
+    for ref in sum_refs[1:]:
+        total = total + ref[...]
+    columns = row_scale(total)
+    if hop:
+        own_ref[0:hop] = refs[NX][...]
+    for p in range(PAIRS):
+        v = (raw_ref[p].astype(f32) * pair_scale(columns, p)).astype(bf16)
+        own_ref[hop, p] = v
+        slots[p] = v
+        slots[PAIRS + p] = jnp.concatenate([v[:, WIDTH:], v[:, :WIDTH]], axis=1)
+    mask = lane_low((BLK, BLK))
+    mine = (me_ref[0] * NZ + me_ref[1]) * NC + me_ref[2]
     copies = []
-    for p in range(PAIRS):
-        v = (raw_ref[p].astype(f32) * pair_scale(columns, p)).astype(bf16)
-        buf[p] = v
-        own_ref[0, p] = v
-    for z in range(NZ):
-        copy = pltpu.make_async_copy(buf, out_ref.at[z], sem.at[z])
-        copy.start()
-        copies.append(copy)
-    for copy in copies:
-        copy.wait()
-
-
-def pick_kernel(raw, me_ref, idx_ref, z_ref, *refs):
-    out_ref, slots, buf, sem = refs[0], *refs[-3:]
-    if raw:
-        u_ref, before_ref = refs[0], refs[1]
-        sum_refs = refs[2 : 2 + NZ]
-        out_ref, own_ref = refs[2 + NZ], refs[3 + NZ]
-        columns = row_scale(sum_refs[0][...])
-        for p in range(PAIRS):
-            own_ref[1, p] = (u_ref[p] * pair_scale(columns, p)).astype(bf16)
-        own_ref[0] = before_ref[0]
-    for j in range(NZ):
-        z = (me_ref[1] + NZ - ZSHIFTS[j]) % NZ if raw else j
-        if raw:
-            columns = row_scale(sum_refs[j][...])
-        for p in range(PAIRS):
-            v = z_ref[z, p]
-            if raw:
-                v = (v.astype(f32) * pair_scale(columns, p)).astype(bf16)
-            slots[z * BPD + p] = v
-            slots[z * BPD + PAIRS + p] = jnp.concatenate([v[:, WIDTH:], v[:, :WIDTH]], axis=1)
-    mask = lane_low((BLK, BLK))
-    mine = me_ref[0] * NC + me_ref[2]
-    copies = []
-    for dest in range(NY * NC):
-        for z in range(NZ):
-            i = dest * NZ + z
-            buf[i] = jnp.where(mask, slots[idx_ref[2 * i]], slots[idx_ref[2 * i + 1]])
-
-        @pl.when(mine == dest)
+    for part in range(N_ROW // BATCH):
+        for j in range(BATCH):
+            i = part * BATCH + j
+            first = idx_ref[i, 0]
+            second = idx_ref[i, 1]
+            low = slots[(first >> 1) | ((first & 1) << 2)]
+            high = slots[((second >> 1) | ((second & 1) << 2)) ^ PAIRS]
+            buf[i] = jnp.where(mask, low, high)
+
+        @pl.when(mine // BATCH == part)
         def _():
-            buf[dest * NZ + me_ref[1]] = jnp.zeros((BLK, BLK), bf16)
+            buf[mine] = jnp.zeros((BLK, BLK), bf16)
 
         copy = pltpu.make_async_copy(
-            buf.at[pl.ds(dest * NZ, NZ)], out_ref.at[pl.ds(dest * NZ, NZ)], sem.at[dest]
+            buf.at[pl.ds(part * BATCH, BATCH)], out_ref.at[pl.ds(part * BATCH, BATCH)], sem.at[part]
         )
         copy.start()
         copies.append(copy)
@@ -145,7 +129,7 @@
 
 def order_kernel(me_ref, rows_ref, srcs_ref, count_ref, tile_ref, slab_ref, into_ref, groups_ref, fill, begin):
     count = count_ref[0]
-    empty = (me_ref[0] * NC + me_ref[2]) * NZ + me_ref[1]
+    empty = (me_ref[0] * NZ + me_ref[1]) * NC + me_ref[2]
 
     @pl.loop(0, SLOTS // 8)
     def _(i):
@@ -164,7 +148,7 @@
 
     def bucket_of(t):
         s = srcs_ref[t]
-        return jnp.where(s < BPD, 0, BUCKETS) + rows_ref[t] * 2 + s % 2
+        return jnp.where(s < BPD, 0, BUCKETS) + rows_ref[t] * 2 + (s & 1)
 
     @pl.loop(0, count)
     def _(t):
@@ -190,12 +174,8 @@
         at = begin[b]
         begin[b] = at + 1
         s = srcs_ref[t]
-        o = (s - BPD) // 2
-        y = o // (NZ * NC)
-        z = (o // NC) % NZ
-        k = o % NC
         tile_ref[at] = t
-        slab_ref[at] = jnp.where(s < BPD, s // 2, (y * NC + k) * NZ + z)
+        slab_ref[at] = jnp.where(s < BPD, s >> 1, (s - BPD) >> 1)
 
 
 def add_groups(kind, tile_ref, slab_ref, into_ref, groups_ref, tiles_ref, src, acc, ring, sem):
@@ -261,7 +241,7 @@
     if last:
         out_ref, acc, ring, sem = rest
     else:
-        out_ref, u_ref, sq_ref, acc, ring, sem, buf, out_sem = rest
+        out_ref, sq_ref, acc, ring, sem = rest
     begin, run = add_groups(1, tile_ref, slab_ref, into_ref, groups_ref, tiles_ref, got_ref, acc, ring, sem)
     for step in range(DEPTH):
         begin(step)
@@ -274,12 +254,7 @@
         if last:
             out_ref[p * BLK : (p + 1) * BLK] = u.astype(bf16)
         else:
-            buf[p] = u.astype(bf16)
-            u_ref[p] = u
-    if not last:
-        copies = [pltpu.make_async_copy(buf, out_ref.at[z], out_sem.at[z]) for z in range(NZ)]
-        for copy in copies:
-            copy.start()
+            out_ref[p] = u
     total = pair_squares(pairs)
     if last:
         hi = total.astype(bf16).astype(f32)
@@ -289,8 +264,6 @@
         out_ref[PAIRS * BLK + 16 : PAIRS * BLK + 32] = jnp.concatenate([lo, jnp.zeros_like(lo)], axis=0).astype(bf16)
     else:
         sq_ref[...] = total
-        for copy in copies:
-            copy.wait()
 
 
 def early_kernel(x_ref, w_ref, *refs):
@@ -357,8 +330,9 @@
         pack_kernel, "pack", [whole()],
         [((PAIRS, BLK, BLK), bf16, VMEM), ((BPD, BLK), f32, VMEM)],
     )(features.T)
-    packed, squares, needed, rows, srcs, count, enc_weight, tile_vals = lax.optimization_barrier(
-        (packed, squares, needed.reshape(-1), tile_rows.reshape(-1), tile_srcs.reshape(-1), tile_count, enc_weight, tile_vals)
+    asked = lax.all_to_all(jnp.pad(needed[0], ((0, 0), (0, BLK - 2))), ("y", "z", "core"), 0, 0, tiled=True)
+    packed, squares, rows, srcs, count, enc_weight = lax.optimization_barrier(
+        (packed, squares, tile_rows.reshape(-1), tile_srcs.reshape(-1), tile_count, enc_weight)
     )
 
     weights = lax.dynamic_slice_in_dim(enc_weight, x_index * WIDTH, WIDTH, axis=2).reshape(HOPS + 1, NX, WIDTH, WIDTH)
@@ -371,38 +345,20 @@
         [((2 * SLOTS,), jnp.int32, SMEM), ((2 * SLOTS,), jnp.int32, SMEM), ((2 * MAXG,), jnp.int32, SMEM), ((2,), jnp.int32, SMEM)],
         [SMEM((2 * BUCKETS,), jnp.int32), SMEM((2 * BUCKETS,), jnp.int32)],
     )(me, rows, srcs, count)
-    table = None
+    owned = None
     for hop in range(HOPS):
         last = hop == HOPS - 1
-        total = lax.psum(squares, "x")
-        if not hop:
-            packed, owned = call(
-                norm_kernel, "norm", [whole()] * 2,
-                [((NZ, PAIRS, BLK, BLK), bf16, HBM), ((1, PAIRS, BLK, BLK), bf16, VMEM)],
-                [VMEM((PAIRS, BLK, BLK), bf16), DMA((NZ,))],
-                limit=TIGHT,
-            )(packed, total)
-        along = lax.all_to_all(packed, "z", 0, 0, tiled=True)
-        if table is None:
-            needed, owned = lax.optimization_barrier((needed, owned))
-            asked = lax.all_gather(needed, ("y", "core"), axis=0).reshape(NY * NC, NY, NZ, NC, 2)
-            asked = lax.dynamic_slice(asked, (0, me[0], 0, me[2], 0), (NY * NC, 1, NZ, 1, 2)).reshape(NY * NC, NZ, 2)
-            odd = (asked % 2) ^ jnp.arange(2, dtype=jnp.int32)
-            table = (jnp.arange(NZ, dtype=jnp.int32)[:, None] * BPD + asked // 2 + PAIRS * odd).reshape(-1)
-        scratch = [VMEM((NZ * BPD, BLK, BLK), bf16), VMEM((NY * NC * NZ, BLK, BLK), bf16), DMA((NY * NC,))]
-        outs = [((NY * NC * NZ, BLK, BLK), bf16, HBM)]
-        if hop:
-            totals = [total] + [shift_by(total, "z", shift) for shift in ZSHIFTS[1:]]
-            picked, owned = call(
-                functools.partial(pick_kernel, True), "pick", [whole(SMEM)] * 2 + [whole()] * (3 + NZ),
-                outs + [((2, PAIRS, BLK, BLK), bf16, VMEM)], scratch, limit=MOST,
-            )(me, table, along, values, owned, *totals)
+        totals = [squares] + [shift_by(squares, "x", shift) for shift in SHIFTS[1:]]
+        before = [owned] if hop else []
+        picked, owned = call(
+            functools.partial(send_kernel, hop), "send", [whole(SMEM)] * 2 + [whole()] * (1 + NX + hop),
+            [((N_ROW, BLK, BLK), bf16, HBM), ((hop + 1, PAIRS, BLK, BLK), bf16, VMEM)],
+            [VMEM((BPD, BLK, BLK), bf16), VMEM((N_ROW, BLK, BLK), bf16), DMA((N_ROW // BATCH,))],
+            limit=MOST,
+        )(me, asked, packed, *totals, *before)
+        if last:
             spread = [owned] + [shift_by(owned, "x", shift) for shift in SHIFTS[1:]]
-        else:
-            picked = call(
-                functools.partial(pick_kernel, False), "pick", [whole(SMEM)] * 2 + [whole()], outs, scratch, limit=MOST
-            )(me, table, along)
-        got = lax.all_to_all(picked, ("y", "core"), 0, 0, tiled=True)
+        got = lax.all_to_all(picked, ("y", "z", "core"), 0, 0, tiled=True)
         ring = [VMEM((DEPTH, STEP * GROUP, BLK, BLK), bf16), DMA((DEPTH, STEP * GROUP))]
         part = call(
             functools.partial(own_kernel, hop), "own", [whole(SMEM)] * 4 + [whole(HBM), whole(), whole(HBM)],
@@ -419,18 +375,18 @@
             outs = [((PAIRS * BLK + 32, BLK), bf16, VMEM)]
             more = []
         else:
-            outs = [((NZ, PAIRS, BLK, BLK), bf16, HBM), ((PAIRS, BLK, BLK), f32, VMEM), ((BPD, BLK), f32, VMEM)]
-            more = [VMEM((PAIRS, BLK, BLK), bf16), DMA((NZ,))]
+            outs = [((PAIRS, BLK, BLK), f32, VMEM), ((BPD, BLK), f32, VMEM)]
+            more = []
         result = call(
             functools.partial(far_kernel, hop), "far", [whole(SMEM)] * 4 + [whole(HBM), whole(), whole()], outs,
             [VMEM((BUCKETS, BLK, BLK), f32)] + ring + more,
             limit=ROOM, flops=TPD * 2 * BLK**3, moved=8 << 20,
         )(*lists, tile_vals, got, part)
         if not last:
-            packed, values, squares = result
+            packed, squares = result
     tails = [result] + [shift_by(result, "x", shift) for shift in SHIFTS[1:]]
     return call(
-        final_kernel, "final", [whole(SMEM)] + [whole()] * (2 + NX), [((WIDTH, BPD * BLK), bf16, VMEM)]
+        final_kernel, "final", [whole(SMEM)] + [whole()] * (2 + NX), [((WIDTH, BPD * BLK), bf16, VMEM)],
     )(x_only, weights, early, *tails).T
 
 

time: 195 us -> 190 us (0.974); the launches traced: 192 us -> 189 us
  waiting for transfers between devices: 55.4 us -> 94.2 us
  blocking collectives: 29.5 us -> 0 us
  starting transfers between devices: 49.2 us -> 41.2 us
  Pallas kernels: 47.5 us -> 44.7 us
    all_to_all x4 -> x3, waiting for transfers between devices: 33.4 us -> 78 us  [the longest x2 69.4 us: shards(): got = lax.all_to_all(picked, ('y', 'z', 'core'), 0, 0, tiled=True)]
    psum x2 -> x0, blocking collectives: 15.8 us -> none  [shards(): total = lax.psum(squares, 'x')]
    all_gather x1 -> x0, blocking collectives: 13.6 us -> none  [shards(): lax.all_gather(needed, ('y', 'core'), axis=0)]
    pallas_call x3 -> x2, Pallas kernels: 13.9 us -> 8.03 us  [shards(): call(functools.partial(send_kernel, hop), 'send', [whole(SMEM)] * 2 + [wh...]
    ppermute x13 -> x12, waiting for transfers between devices: 22 us -> 16.2 us  [shift_by(): lax.ppermute(value, axis, [(i, (i + shift) % size) for i in range(size)])]
    all_to_all x4 -> x3, starting transfers between devices: 30.9 us -> 25.8 us  [the longest x1 13.2 us: shards(): lax.all_to_all(jnp.pad(needed[0], ((0, 0), (0, BLK - 2))), ('y', 'z', 'co...]
    ppermute x13 -> x12, starting transfers between devices: 18.3 us -> 15.4 us  [shift_by(): lax.ppermute(value, axis, [(i, (i + shift) % size) for i in range(size)])]
    unnamed x45 -> x38, local copies, waits for them, and re-layouts: 7.52 us -> 6.01 us
  transfers between devices with their start and end apart: 17 -> 15, of which waited for: 12 -> 9; matrix products, arithmetic and copies ran while one was open for 1% -> 1% of each run, Pallas kernels for 10% -> 11%
where the time goes in v3:
time: 190 us; the launch traced here: 189 us
  waiting for transfers between devices  94.2 us (50%)
  Pallas kernels  44.7 us (24%)
  starting transfers between devices  41.2 us (22%)
  local copies, waits for them, and re-layouts  7.51 us (4%)
    all_to_all x2, waiting for transfers between devices, shards(): got = lax.all_to_all(picked, ('y', 'z', 'core'), 0, 0, tiled=True)  69.4 us
    ppermute x12, waiting for transfers between devices, shift_by(): lax.ppermute(value, axis, [(i, (i + shift) % size) for i in range(size)])  16.2 us
    ppermute x12, starting transfers between devices, shift_by(): lax.ppermute(value, axis, [(i, (i + shift) % size) for i in range(size)])  15.4 us
    pallas_call x2, Pallas kernels, shards(): call(functools.partial(far_kernel, hop), 'far', [whole(SMEM)] * 4 + [whol...  15.1 us
    all_to_all x1, starting transfers between devices, shards(): lax.all_to_all(jnp.pad(needed[0], ((0, 0), (0, BLK - 2))), ('y', 'z', 'co...  13.2 us
    all_to_all x2, starting transfers between devices, shards(): got = lax.all_to_all(picked, ('y', 'z', 'core'), 0, 0, tiled=True)  12.6 us
    pallas_call x2, Pallas kernels, shards(): call(functools.partial(own_kernel, hop), 'own', [whole(SMEM)] * 4 + [whol...  11.2 us
    all_to_all x1, waiting for transfers between devices, shards(): lax.all_to_all(jnp.pad(needed[0], ((0, 0), (0, BLK - 2))), ('y', 'z', 'co...  8.6 us
  transfers between devices with their start and end apart: 15, of which 9 were waited for; matrix products, arithmetic and copies ran while one was open for 1% of the time, Pallas kernels for 11%

profile of v3, /device:TPU:1, one launch (start us, length us, event | category | flops | bytes accessed | tf_op | source)
XLA Modules:
  0.0 189.4 jit_solution(13636079114173046398)
XLA Ops:
  0.0 1.0 copy-done.2
  1.7 3.3 %collective-permute-start.2 = (f32[8,128]{1,0:T(8,128)S(1)}, f32[8,128]{1,0:T(8,128)S(1)}, u32[]{:S(2)}, u32[]{:S(2)}) collective-permute-start(f32[8,128]{1,0:T(8,128)S(1)} %get-tuple-element.36.refs_0_), channel_id=1, source_target_pairs={{0,3},{1,0},{2,1},{3,2},{4,7},{5,4},{6,5},{7,6},{8,11},{9,8},{10,9... | collective-permute-start | bytes 12296 | tf_op jit(solution)/shard_map/ppermute | solution.py:320
  5.0 1.7 collective-permute-start
  8.1 13.2 %all-to-all-start = ((s32[64,1,128]{2,1,0:T(1,128)}), s32[64,1,128]{2,1,0:T(1,128)S(1)}, u32[]{:S(2)}, u32[]{:S(2)}) async-start(s32[64,1,128]{2,1,0:T(1,128)} %copy.10), calls=%async_computation | async-start | bytes 65536 | tf_op jit(solution)/shard_map/all_to_all | solution.py:333
  22.0 8.6 %all-to-all-done = s32[64,1,128]{2,1,0:T(1,128)S(1)} async-done(((s32[64,1,128]{2,1,0:T(1,128)}), s32[64,1,128]{2,1,0:T(1,128)S(1)}, u32[]{:S(2)}, u32[]{:S(2)}) %all-to-all-start) | async-done | bytes 32800 | tf_op jit(solution)/shard_map/all_to_all | solution.py:333
  31.2 4.0 %send.2 = (bf16[64,128,128]{2,1,0:T(8,128)(2,1)}, bf16[1,4,128,128]{3,2,1,0:T(8,128)(2,1)}) custom-call(s32[3]{0:T(128)} %pad_add_fusion.me_ref, s32[64,128]{1,0:T(8,128)} %bitcast.20, bf16[4,128,128]{2,1,0:T(8,128)(2,1)} %copy-done.3, f32[8,128]{1,0:T(8,128)} %copy-done.9, f32[8,128]{1,0:T(8,128)} %copy-done.18, f32[8,128]{1,0:T(8,128)} %copy-done.17, ...), custom_call_target="tpu_custom_call" | custom-call | flops 1048576 | bytes 1048576 | tf_op jit(solution)/shard_map/send/pallas_call | solution.py:353
  35.3 5.6 %all-to-all-start.1 = ((bf16[64,128,128]{2,1,0:T(8,128)(2,1)}), bf16[64,128,128]{2,1,0:T(8,128)(2,1)}, u32[]{:S(2)}, u32[]{:S(2)}) async-start(bf16[64,128,128]{2,1,0:T(8,128)(2,1)} %get-tuple-element.37), calls=%async_computation.1 | async-start | bytes 4194304 | tf_op jit(solution)/shard_map/all_to_all | solution.py:361
  41.5 7.5 %order.1 = (s32[448]{0:T(512)S(1)}, s32[448]{0:T(512)S(1)}, s32[112]{0:T(128)S(1)}, s32[2]{0:T(128)S(1)}) custom-call(s32[3]{0:T(128)S(1)} %copy-done.8, s32[160]{0:T(256)S(1)} %bitcast.15, s32[160]{0:T(256)S(1)} %bitcast.16, s32[1]{0:T(128)S(6)} %copy.11.count_ref), custom_call_target="tpu_custom_call" | custom-call | flops 1048576 | bytes 1048576 | tf_op jit(solution)/shard_map/order/pallas_call | solution.py:343
  51.3 5.6 %own.2.part_ref = f32[4,128,128]{2,1,0:T(8,128)} custom-call(s32[448]{0:T(512)} %copy-done.4, s32[448]{0:T(512)} %copy-done.5, s32[112]{0:T(128)} %copy-done.6, s32[2]{0:T(128)} %copy-done.7, bf16[160,128,128]{2,1,0:T(8,128)(2,1)} %tiles_ref.7, bf16[1,4,128,128]{3,2,1,0:T(8,128)(2,1)} %get-tuple-element.38.own_ref.refs_4_, f32[2,64,1024]{2,1,0:T(8,128)} %bitcast.17), custom_call_target="tpu_custom_call" | custom-call | flops 671088640 | bytes 4194304 | tf_op jit(solution)/shard_map/own/pallas_call | solution.py:363
  56.9 35.2 %all-to-all-done.1.got_ref = bf16[64,128,128]{2,1,0:T(8,128)(2,1)} async-done(((bf16[64,128,128]{2,1,0:T(8,128)(2,1)}), bf16[64,128,128]{2,1,0:T(8,128)(2,1)}, u32[]{:S(2)}, u32[]{:S(2)}) %all-to-all-start.1) | async-done | bytes 2097184 | tf_op jit(solution)/shard_map/all_to_all | solution.py:361
  92.1 7.5 %far.2 = (f32[4,128,128]{2,1,0:T(8,128)}, f32[8,128]{1,0:T(8,128)}) custom-call(s32[448]{0:T(512)} %copy-done.4, s32[448]{0:T(512)} %copy-done.5, s32[112]{0:T(128)} %copy-done.6, s32[2]{0:T(128)} %copy-done.7, bf16[160,128,128]{2,1,0:T(8,128)(2,1)} %tiles_ref.7, bf16[64,128,128]{2,1,0:T(8,128)(2,1)} %all-to-all-done.1.got_ref, f32[4,128,128]{2,1,0:T(8,128)} %own.2.part_ref), custom_call_target="tpu_custom_call" | custom-call | flops 671088640 | bytes 8388608 | tf_op jit(solution)/shard_map/far/pallas_call | solution.py:380
  99.7 0.9 collective-permute-start.5
  100.6 0.8 collective-permute-start.4
  101.3 1.7 collective-permute-start.3
  103.1 1.4 collective-permute-done.4.refs_2_
  104.5 1.0 collective-permute-done.3.refs_1_
  106.1 4.0 %send.3 = (bf16[64,128,128]{2,1,0:T(8,128)(2,1)}, bf16[2,4,128,128]{3,2,1,0:T(8,128)(2,1)}) custom-call(s32[3]{0:T(128)} %pad_add_fusion.me_ref, s32[64,128]{1,0:T(8,128)} %bitcast.21, f32[4,128,128]{2,1,0:T(8,128)} %get-tuple-element.39.raw_ref, f32[8,128]{1,0:T(8,128)} %get-tuple-element.40.refs_0_, f32[8,128]{1,0:T(8,128)} %copy-done.15, ...), custom_call_target="tpu_custom_call" | custom-call | flops 1048576 | bytes 1048576 | tf_op jit(solution)/shard_map/send/pallas_call | solution.py:353
  110.2 7.0 %all-to-all-start.2 = ((bf16[64,128,128]{2,1,0:T(8,128)(2,1)}), bf16[64,128,128]{2,1,0:T(8,128)(2,1)}, u32[]{:S(2)}, u32[]{:S(2)}) async-start(bf16[64,128,128]{2,1,0:T(8,128)(2,1)} %get-tuple-element.43), calls=%async_computation.2 | async-start | bytes 4194304 | tf_op jit(solution)/shard_map/all_to_all | solution.py:361
  117.2 2.3 %collective-permute-start.8 = (bf16[2,4,128,128]{3,2,1,0:T(8,128)(2,1)}, bf16[2,4,128,128]{3,2,1,0:T(8,128)(2,1)}, u32[]{:S(2)}, u32[]{:S(2)}) collective-permute-start(bf16[2,4,128,128]{3,2,1,0:T(8,128)(2,1)} %get-tuple-element.41.refs_0_.own_ref), channel_id=1, source_target_pairs={{0,3},{1,0},{2,1},{3,2},{4,7},{5,4},{6,5},{7,6},{8,11},{9,8},{10,9... | collective-permute-start | bytes 786440 | tf_op jit(solution)/shard_map/ppermute | solution.py:320
  119.5 1.3 collective-permute-start.6
  121.1 5.6 %own.3.part_ref = f32[4,128,128]{2,1,0:T(8,128)} custom-call(s32[448]{0:T(512)} %copy-done.4, s32[448]{0:T(512)} %copy-done.5, s32[112]{0:T(128)} %copy-done.6, s32[2]{0:T(128)} %copy-done.7, bf16[160,128,128]{2,1,0:T(8,128)(2,1)} %tiles_ref.7, bf16[2,4,128,128]{3,2,1,0:T(8,128)(2,1)} %get-tuple-element.41.refs_0_.own_ref, f32[2,64,1024]{2,1,0:T(8,128)} %bitcast.18), custom_call_target="tpu_custom_call" | custom-call | flops 671088640 | bytes 4194304 | tf_op jit(solution)/shard_map/own/pallas_call | solution.py:363
  126.7 2.4 %collective-permute-done.7.refs_2_ = bf16[2,4,128,128]{3,2,1,0:T(8,128)(2,1)} collective-permute-done((bf16[2,4,128,128]{3,2,1,0:T(8,128)(2,1)}, bf16[2,4,128,128]{3,2,1,0:T(8,128)(2,1)}, u32[]{:S(2)}, u32[]{:S(2)}) %collective-permute-start.7) | collective-permute-done | bytes 262176 | tf_op jit(solution)/shard_map/ppermute | solution.py:320
  129.1 3.4 %collective-permute-done.6.refs_1_ = bf16[2,4,128,128]{3,2,1,0:T(8,128)(2,1)} collective-permute-done((bf16[2,4,128,128]{3,2,1,0:T(8,128)(2,1)}, bf16[2,4,128,128]{3,2,1,0:T(8,128)(2,1)}, u32[]{:S(2)}, u32[]{:S(2)}) %collective-permute-start.6) | collective-permute-done | bytes 262176 | tf_op jit(solution)/shard_map/ppermute | solution.py:320
  132.6 1.6 early.1.early_ref
  134.2 34.3 %all-to-all-done.2.got_ref = bf16[64,128,128]{2,1,0:T(8,128)(2,1)} async-done(((bf16[64,128,128]{2,1,0:T(8,128)(2,1)}), bf16[64,128,128]{2,1,0:T(8,128)(2,1)}, u32[]{:S(2)}, u32[]{:S(2)}) %all-to-all-start.2) | async-done | bytes 2097184 | tf_op jit(solution)/shard_map/all_to_all | solution.py:361
  168.4 7.6 %far.3.refs_0_ = bf16[544,128]{1,0:T(8,128)(2,1)} custom-call(s32[448]{0:T(512)} %copy-done.4, s32[448]{0:T(512)} %copy-done.5, s32[112]{0:T(128)} %copy-done.6, s32[2]{0:T(128)} %copy-done.7, bf16[160,128,128]{2,1,0:T(8,128)(2,1)} %tiles_ref.7, bf16[64,128,128]{2,1,0:T(8,128)(2,1)} %all-to-all-done.2.got_ref, f32[4,128,128]{2,1,0:T(8,128)} %own.3.part_ref), custom_call_target="tpu_custom_call" | custom-call | flops 671088640 | bytes 8388608 | tf_op jit(solution)/shard_map/far/pallas_call | solution.py:380
  176.0 2.1 %collective-permute-start.11 = (bf16[544,128]{1,0:T(8,128)(2,1)}, bf16[544,128]{1,0:T(8,128)(2,1)S(1)}, u32[]{:S(2)}, u32[]{:S(2)}) collective-permute-start(bf16[544,128]{1,0:T(8,128)(2,1)} %far.3.refs_0_), channel_id=1, source_target_pairs={{0,3},{1,0},{2,1},{3,2},{4,7},{5,4},{6,5},{7,6},{8,11},{9,8},{10,9... | collective-permute-start | bytes 417800 | tf_op jit(solution)/shard_map/ppermute | solution.py:320
  178.2 1.3 collective-permute-start.9
  179.4 1.6 collective-permute-done.11.refs_3_
  181.1 6.2 %collective-permute-done.10.refs_2_ = bf16[544,128]{1,0:T(8,128)(2,1)S(1)} collective-permute-done((bf16[544,128]{1,0:T(8,128)(2,1)}, bf16[544,128]{1,0:T(8,128)(2,1)S(1)}, u32[]{:S(2)}, u32[]{:S(2)}) %collective-permute-start.10) | collective-permute-done | bytes 139296 | tf_op jit(solution)/shard_map/ppermute | solution.py:320
  187.3 0.9 copy-done.1
  188.2 1.2 final.1
  (51 shorter events, 6.6 us)
Async XLA Ops:
  0.0 120.8 %copy-start = (bf16[3,256,256]{2,1,0:T(8,128)(2,1)S(1)}, bf16[3,256,256]{2,1,0:T(8,128)(2,1)}, u32[]{:S(2)}) copy-start(bf16[3,256,256]{2,1,0:T(8,128)(2,1)} %param.15) | copy-start | bytes 1179652
  0.0 1.0 copy-start.2
  1.1 0.7 copy-start.3
  1.7 28.9 %copy-start.9 = (f32[8,128]{1,0:T(8,128)}, f32[8,128]{1,0:T(8,128)S(1)}, u32[]{:S(2)}) copy-start(f32[8,128]{1,0:T(8,128)S(1)} %get-tuple-element.36.refs_0_) | copy-start | bytes 12292
  1.7 20.3 %collective-permute-start.2 = (f32[8,128]{1,0:T(8,128)S(1)}, f32[8,128]{1,0:T(8,128)S(1)}, u32[]{:S(2)}, u32[]{:S(2)}) collective-permute-start(f32[8,128]{1,0:T(8,128)S(1)} %get-tuple-element.36.refs_0_), channel_id=1, source_target_pairs={{0,3},{1,0},{2,1},{3,2},{4,7},{5,4},{6,5},{7,6},{8,11},{9,8},{10,9... | collective-permute-start | bytes 12296 | tf_op jit(solution)/shard_map/ppermute | solution.py:320
  5.0 17.0 %collective-permute-start.1 = (f32[8,128]{1,0:T(8,128)S(1)}, f32[8,128]{1,0:T(8,128)S(1)}, u32[]{:S(2)}, u32[]{:S(2)}) collective-permute-start(f32[8,128]{1,0:T(8,128)S(1)} %get-tuple-element.36.refs_0_), channel_id=1, source_target_pairs={{0,1},{1,2},{2,3},{3,0},{4,5},{5,6},{6,7},{7,4},{8,9},{9,10},{10,1... | collective-permute-start | bytes 12296 | tf_op jit(solution)/shard_map/ppermute | solution.py:320
  5.0 17.0 %collective-permute-start = (f32[8,128]{1,0:T(8,128)S(1)}, f32[8,128]{1,0:T(8,128)S(1)}, u32[]{:S(2)}, u32[]{:S(2)}) collective-permute-start(f32[8,128]{1,0:T(8,128)S(1)} %get-tuple-element.36.refs_0_), channel_id=1, source_target_pairs={{0,2},{1,3},{2,0},{3,1},{4,6},{5,7},{6,4},{7,5},{8,10},{9,11},{10,... | collective-permute-start | bytes 12296 | tf_op jit(solution)/shard_map/ppermute | solution.py:320
  8.1 22.5 %all-to-all-start = ((s32[64,1,128]{2,1,0:T(1,128)}), s32[64,1,128]{2,1,0:T(1,128)S(1)}, u32[]{:S(2)}, u32[]{:S(2)}) async-start(s32[64,1,128]{2,1,0:T(1,128)} %copy.10), calls=%async_computation | async-start | bytes 65536 | tf_op jit(solution)/shard_map/all_to_all | solution.py:333
  22.0 8.6 %copy-start.16 = (f32[8,128]{1,0:T(8,128)}, f32[8,128]{1,0:T(8,128)S(1)}, u32[]{:S(2)}) copy-start(f32[8,128]{1,0:T(8,128)S(1)} %collective-permute-done.2.refs_3_) | copy-start | bytes 12292
  22.0 8.6 %copy-start.17 = (f32[8,128]{1,0:T(8,128)}, f32[8,128]{1,0:T(8,128)S(1)}, u32[]{:S(2)}) copy-start(f32[8,128]{1,0:T(8,128)S(1)} %collective-permute-done.1.refs_2_) | copy-start | bytes 12292
  22.0 8.6 %copy-start.18 = (f32[8,128]{1,0:T(8,128)}, f32[8,128]{1,0:T(8,128)S(1)}, u32[]{:S(2)}) copy-start(f32[8,128]{1,0:T(8,128)S(1)} %collective-permute-done.refs_1_) | copy-start | bytes 12292
  30.6 0.6 copy-start.12
  35.2 6.3 %copy-start.8 = (s32[3]{0:T(128)S(1)}, s32[3]{0:T(128)}, u32[]{:S(2)}) copy-start(s32[3]{0:T(128)} %pad_add_fusion.me_ref) | copy-start | bytes 40
  35.2 6.3 %copy-start.10 = (s32[1,160]{1,0:T(1,128)S(1)}, s32[1,160]{1,0:T(1,128)}, u32[]{:S(2)}) copy-start(s32[1,160]{1,0:T(1,128)} %param.10) | copy-start | bytes 1924
  35.3 6.3 %copy-start.11 = (s32[1,160]{1,0:T(1,128)S(1)}, s32[1,160]{1,0:T(1,128)}, u32[]{:S(2)}) copy-start(s32[1,160]{1,0:T(1,128)} %param.11) | copy-start | bytes 1924
  35.3 56.8 %all-to-all-start.1 = ((bf16[64,128,128]{2,1,0:T(8,128)(2,1)}), bf16[64,128,128]{2,1,0:T(8,128)(2,1)}, u32[]{:S(2)}, u32[]{:S(2)}) async-start(bf16[64,128,128]{2,1,0:T(8,128)(2,1)} %get-tuple-element.37), calls=%async_computation.1 | async-start | bytes 4194304 | tf_op jit(solution)/shard_map/all_to_all | solution.py:361
  49.0 0.6 copy-start.4
  49.6 0.6 copy-start.5
  99.7 3.4 %collective-permute-start.5 = (f32[8,128]{1,0:T(8,128)}, f32[8,128]{1,0:T(8,128)S(1)}, u32[]{:S(2)}, u32[]{:S(2)}) collective-permute-start(f32[8,128]{1,0:T(8,128)} %get-tuple-element.40.refs_0_), channel_id=1, source_target_pairs={{0,3},{1,0},{2,1},{3,2},{4,7},{5,4},{6,5},{7,6},{8,11},{9,8},{10,9... | collective-permute-start | bytes 12296 | tf_op jit(solution)/shard_map/ppermute | solution.py:320
  100.6 3.9 %collective-permute-start.4 = (f32[8,128]{1,0:T(8,128)}, f32[8,128]{1,0:T(8,128)S(1)}, u32[]{:S(2)}, u32[]{:S(2)}) collective-permute-start(f32[8,128]{1,0:T(8,128)} %get-tuple-element.40.refs_0_), channel_id=1, source_target_pairs={{0,1},{1,2},{2,3},{3,0},{4,5},{5,6},{6,7},{7,4},{8,9},{9,10},{10,1... | collective-permute-start | bytes 12296 | tf_op jit(solution)/shard_map/ppermute | solution.py:320
  101.3 4.2 %collective-permute-start.3 = (f32[8,128]{1,0:T(8,128)}, f32[8,128]{1,0:T(8,128)S(1)}, u32[]{:S(2)}, u32[]{:S(2)}) collective-permute-start(f32[8,128]{1,0:T(8,128)} %get-tuple-element.40.refs_0_), channel_id=1, source_target_pairs={{0,2},{1,3},{2,0},{3,1},{4,6},{5,7},{6,4},{7,5},{8,10},{9,11},{10,... | collective-permute-start | bytes 12296 | tf_op jit(solution)/shard_map/ppermute | solution.py:320
  103.0 2.5 %copy-start.13 = (f32[8,128]{1,0:T(8,128)}, f32[8,128]{1,0:T(8,128)S(1)}, u32[]{:S(2)}) copy-start(f32[8,128]{1,0:T(8,128)S(1)} %collective-permute-done.5.refs_3_) | copy-start | bytes 12292
  104.5 1.1 copy-start.14
  105.5 0.6 copy-start.15
  110.2 58.3 %all-to-all-start.2 = ((bf16[64,128,128]{2,1,0:T(8,128)(2,1)}), bf16[64,128,128]{2,1,0:T(8,128)(2,1)}, u32[]{:S(2)}, u32[]{:S(2)}) async-start(bf16[64,128,128]{2,1,0:T(8,128)(2,1)} %get-tuple-element.43), calls=%async_computation.2 | async-start | bytes 4194304 | tf_op jit(solution)/shard_map/all_to_all | solution.py:361
  117.2 9.5 %collective-permute-start.8 = (bf16[2,4,128,128]{3,2,1,0:T(8,128)(2,1)}, bf16[2,4,128,128]{3,2,1,0:T(8,128)(2,1)}, u32[]{:S(2)}, u32[]{:S(2)}) collective-permute-start(bf16[2,4,128,128]{3,2,1,0:T(8,128)(2,1)} %get-tuple-element.41.refs_0_.own_ref), channel_id=1, source_target_pairs={{0,3},{1,0},{2,1},{3,2},{4,7},{5,4},{6,5},{7,6},{8,11},{9,8},{10,9... | collective-permute-start | bytes 786440 | tf_op jit(solution)/shard_map/ppermute | solution.py:320
  119.5 9.6 %collective-permute-start.7 = (bf16[2,4,128,128]{3,2,1,0:T(8,128)(2,1)}, bf16[2,4,128,128]{3,2,1,0:T(8,128)(2,1)}, u32[]{:S(2)}, u32[]{:S(2)}) collective-permute-start(bf16[2,4,128,128]{3,2,1,0:T(8,128)(2,1)} %get-tuple-element.41.refs_0_.own_ref), channel_id=1, source_target_pairs={{0,1},{1,2},{2,3},{3,0},{4,5},{5,6},{6,7},{7,4},{8,9},{9,10},{10,1... | collective-permute-start | bytes 786440 | tf_op jit(solution)/shard_map/ppermute | solution.py:320
  119.5 13.0 %collective-permute-start.6 = (bf16[2,4,128,128]{3,2,1,0:T(8,128)(2,1)}, bf16[2,4,128,128]{3,2,1,0:T(8,128)(2,1)}, u32[]{:S(2)}, u32[]{:S(2)}) collective-permute-start(bf16[2,4,128,128]{3,2,1,0:T(8,128)(2,1)} %get-tuple-element.41.refs_0_.own_ref), channel_id=1, source_target_pairs={{0,2},{1,3},{2,0},{3,1},{4,6},{5,7},{6,4},{7,5},{8,10},{9,11},{10,... | collective-permute-start | bytes 786440 | tf_op jit(solution)/shard_map/ppermute | solution.py:320
  176.0 5.1 %collective-permute-start.11 = (bf16[544,128]{1,0:T(8,128)(2,1)}, bf16[544,128]{1,0:T(8,128)(2,1)S(1)}, u32[]{:S(2)}, u32[]{:S(2)}) collective-permute-start(bf16[544,128]{1,0:T(8,128)(2,1)} %far.3.refs_0_), channel_id=1, source_target_pairs={{0,3},{1,0},{2,1},{3,2},{4,7},{5,4},{6,5},{7,6},{8,11},{9,8},{10,9... | collective-permute-start | bytes 417800 | tf_op jit(solution)/shard_map/ppermute | solution.py:320
  178.2 9.2 %collective-permute-start.10 = (bf16[544,128]{1,0:T(8,128)(2,1)}, bf16[544,128]{1,0:T(8,128)(2,1)S(1)}, u32[]{:S(2)}, u32[]{:S(2)}) collective-permute-start(bf16[544,128]{1,0:T(8,128)(2,1)} %far.3.refs_0_), channel_id=1, source_target_pairs={{0,1},{1,2},{2,3},{3,0},{4,5},{5,6},{6,7},{7,4},{8,9},{9,10},{10,1... | collective-permute-start | bytes 417800 | tf_op jit(solution)/shard_map/ppermute | solution.py:320
  178.2 9.2 %collective-permute-start.9 = (bf16[544,128]{1,0:T(8,128)(2,1)}, bf16[544,128]{1,0:T(8,128)(2,1)S(1)}, u32[]{:S(2)}, u32[]{:S(2)}) collective-permute-start(bf16[544,128]{1,0:T(8,128)(2,1)} %far.3.refs_0_), channel_id=1, source_target_pairs={{0,2},{1,3},{2,0},{3,1},{4,6},{5,7},{6,4},{7,5},{8,10},{9,11},{10,... | collective-permute-start | bytes 417800 | tf_op jit(solution)/shard_map/ppermute | solution.py:320
  187.3 0.9 copy-start.1
  (2 other events, 1.1 us)

commit v4 on v3

--- a/solution.py
+++ b/solution.py
@@ -22,6 +22,10 @@
 SLOTS = MAXG * GROUP
 SHIFTS = (0, 2, 1, 3)
 N_ROW = NY * NZ * NC
+N_YC = NY * NC
+SIDE = 48
+ZSHIFTS = (0, 4, 3, 5, 2, 6, 1, 7)
+YSHIFTS = (0, 4, 3, 5, 2, 6, 1, 7)
 BATCH = 8
 DEPTH = 4
 FULL = 63 << 20
@@ -91,18 +95,23 @@
 def send_kernel(hop, me_ref, idx_ref, raw_ref, *refs):
     sum_refs = refs[:NX]
     out_ref, own_ref, slots, buf, sem = refs[-5:]
+    rows = buf.shape[1]
     total = sum_refs[0][...]
     for ref in sum_refs[1:]:
         total = total + ref[...]
     columns = row_scale(total)
     if hop:
         own_ref[0:hop] = refs[NX][...]
+        side_ref = refs[NX + 1]
     for p in range(PAIRS):
         v = (raw_ref[p].astype(f32) * pair_scale(columns, p)).astype(bf16)
         own_ref[hop, p] = v
+        if hop:
+            side_ref[p] = v[rows:]
+        v = v[:rows]
         slots[p] = v
         slots[PAIRS + p] = jnp.concatenate([v[:, WIDTH:], v[:, :WIDTH]], axis=1)
-    mask = lane_low((BLK, BLK))
+    mask = lane_low((rows, BLK))
     mine = (me_ref[0] * NZ + me_ref[1]) * NC + me_ref[2]
     copies = []
     for part in range(N_ROW // BATCH):
@@ -116,7 +125,7 @@
 
         @pl.when(mine // BATCH == part)
         def _():
-            buf[mine] = jnp.zeros((BLK, BLK), bf16)
+            buf[mine] = jnp.zeros((rows, BLK), bf16)
 
         copy = pltpu.make_async_copy(
             buf.at[pl.ds(part * BATCH, BATCH)], out_ref.at[pl.ds(part * BATCH, BATCH)], sem.at[part]
@@ -125,6 +134,24 @@
         copies.append(copy)
     for copy in copies:
         copy.wait()
+
+
+def pick_kernel(me_ref, table_ref, *refs):
+    z_refs, out_refs, slots = refs[:NZ], refs[NZ : NZ + N_YC], refs[-1]
+    for j in range(NZ):
+        z = (me_ref[1] + NZ - ZSHIFTS[j]) % NZ
+        for p in range(PAIRS):
+            v = z_refs[j][p]
+            slots[z * BPD + p] = v
+            slots[z * BPD + PAIRS + p] = jnp.concatenate([v[:, WIDTH:], v[:, :WIDTH]], axis=1)
+    mask = lane_low((SIDE, BLK))
+    mine = me_ref[0] * NC + me_ref[2]
+    for j in range(N_YC):
+        dest = (mine + YSHIFTS[j]) % N_YC
+        for z in range(NZ):
+            at = (dest * NZ + z) * 2
+            out_refs[j][z] = jnp.where(mask, slots[table_ref[at]], slots[table_ref[at + 1]])
+    out_refs[0][me_ref[1]] = jnp.zeros((SIDE, BLK), bf16)
 
 
 def order_kernel(me_ref, rows_ref, srcs_ref, count_ref, tile_ref, slab_ref, into_ref, groups_ref, fill, begin):
@@ -178,7 +205,7 @@
         slab_ref[at] = jnp.where(s < BPD, s >> 1, (s - BPD) >> 1)
 
 
-def add_groups(kind, tile_ref, slab_ref, into_ref, groups_ref, tiles_ref, src, acc, ring, sem):
+def add_groups(kind, tile_ref, slab_ref, into_ref, groups_ref, tiles_ref, source, acc, ring, sem):
     steps = (groups_ref[kind] + STEP - 1) // STEP
 
     def copies(step):
@@ -203,7 +230,9 @@
         parts = []
         for h in range(STEP):
             left = jnp.concatenate([ring[slot, h * GROUP + j] for j in range(GROUP)], axis=1)
-            right = jnp.concatenate([src[slab_ref[(group + h) * GROUP + j]] for j in range(GROUP)], axis=0)
+            right = jnp.concatenate(
+                [piece for j in range(GROUP) for piece in source(slab_ref[(group + h) * GROUP + j])], axis=0
+            )
             parts.append(jnp.dot(left, right, preferred_element_type=f32))
         for h in range(STEP):
             acc[into_ref[group + h]] += parts[h]
@@ -222,7 +251,7 @@
 
 
 def own_kernel(hop, tile_ref, slab_ref, into_ref, groups_ref, tiles_ref, own_ref, noise_ref, part_ref, acc, src, noise, ring, sem, load):
-    begin, run = add_groups(0, tile_ref, slab_ref, into_ref, groups_ref, tiles_ref, src, acc, ring, sem)
+    begin, run = add_groups(0, tile_ref, slab_ref, into_ref, groups_ref, tiles_ref, lambda i: [src[i]], acc, ring, sem)
     for step in range(DEPTH):
         begin(step)
     noise_copy = pltpu.make_async_copy(noise_ref.at[hop], noise, load)
@@ -236,15 +265,32 @@
         part_ref[p] = stacked_pair(noise, p).T + fold(acc, p)
 
 
-def far_kernel(hop, tile_ref, slab_ref, into_ref, groups_ref, tiles_ref, got_ref, part_ref, *rest):
+def far_kernel(hop, me_ref, tile_ref, slab_ref, into_ref, groups_ref, tiles_ref, got_ref, part_ref, *rest):
     last = hop == HOPS - 1
     if last:
-        out_ref, acc, ring, sem = rest
+        side_refs = rest[:N_YC]
+        out_ref, acc, ring, sem, side, load = rest[N_YC:]
+        mine = me_ref[0] * NC + me_ref[2]
+        loads = []
+        for j in range(N_YC):
+            at = (mine + N_YC - YSHIFTS[j]) % N_YC
+            loads.append(pltpu.make_async_copy(side_refs[j], side.at[pl.ds(at * NZ, NZ)], load.at[j]))
+            loads[-1].start()
+
+        def source(i):
+            return [got_ref[i], side[((i >> 4) * NC + (i & 1)) * NZ + ((i >> 1) & (NZ - 1))]]
     else:
         out_ref, sq_ref, acc, ring, sem = rest
-    begin, run = add_groups(1, tile_ref, slab_ref, into_ref, groups_ref, tiles_ref, got_ref, acc, ring, sem)
+        loads = []
+
+        def source(i):
+            return [got_ref[i]]
+
+    begin, run = add_groups(1, tile_ref, slab_ref, into_ref, groups_ref, tiles_ref, source, acc, ring, sem)
     for step in range(DEPTH):
         begin(step)
+    for copy in loads:
+        copy.wait()
     acc[...] = jnp.zeros_like(acc)
     run()
     pairs = []
@@ -316,7 +362,7 @@
 
 
 def shift_by(value, axis, shift):
-    size = lax.axis_size(axis)
+    size = N_YC if axis == ("y", "core") else lax.axis_size(axis)
     return lax.ppermute(value, axis, [(i, (i + shift) % size) for i in range(size)])
 
 
@@ -350,15 +396,33 @@
         last = hop == HOPS - 1
         totals = [squares] + [shift_by(squares, "x", shift) for shift in SHIFTS[1:]]
         before = [owned] if hop else []
-        picked, owned = call(
-            functools.partial(send_kernel, hop), "send", [whole(SMEM)] * 2 + [whole()] * (1 + NX + hop),
-            [((N_ROW, BLK, BLK), bf16, HBM), ((hop + 1, PAIRS, BLK, BLK), bf16, VMEM)],
-            [VMEM((BPD, BLK, BLK), bf16), VMEM((N_ROW, BLK, BLK), bf16), DMA((N_ROW // BATCH,))],
+        rows_sent = BLK - SIDE if last else BLK
+        outs = [((N_ROW, rows_sent, BLK), bf16, HBM), ((hop + 1, PAIRS, BLK, BLK), bf16, VMEM)]
+        if last:
+            outs = [((PAIRS, SIDE, BLK), bf16, VMEM)] + outs
+        *sides, picked, owned = call(
+            functools.partial(send_kernel, hop), "send", [whole(SMEM)] * 2 + [whole()] * (1 + NX + hop), outs,
+            [VMEM((BPD, rows_sent, BLK), bf16), VMEM((N_ROW, rows_sent, BLK), bf16), DMA((N_ROW // BATCH,))],
             limit=MOST,
         )(me, asked, packed, *totals, *before)
+        got = lax.all_to_all(picked, ("y", "z", "core"), 0, 0, tiled=True)
         if last:
+            along = sides + [shift_by(sides[0], "z", shift) for shift in ZSHIFTS[1:]]
+            sides = call(
+                pick_kernel, "pick", [whole(SMEM)] * 2 + [whole()] * NZ,
+                [((NZ, SIDE, BLK), bf16, VMEM)] * N_YC,
+                [VMEM((NZ * BPD, SIDE, BLK), bf16)],
+            )(me, table, *along)
+            sides = [sides[0]] + [shift_by(side, ("y", "core"), shift) for side, shift in zip(sides[1:], YSHIFTS[1:])]
+            owned, first = lax.optimization_barrier((owned, sides[0]))
+            sides = [first] + sides[1:]
             spread = [owned] + [shift_by(owned, "x", shift) for shift in SHIFTS[1:]]
-        got = lax.all_to_all(picked, ("y", "z", "core"), 0, 0, tiled=True)
+        else:
+            wide, owned = lax.optimization_barrier((needed.reshape(-1), owned))
+            table = lax.all_gather(wide, ("y", "core"), axis=0).reshape(N_YC, NY, NZ, NC, 2)
+            table = lax.dynamic_slice(table, (0, me[0], 0, me[2], 0), (N_YC, 1, NZ, 1, 2)).reshape(N_YC, NZ, 2)
+            odd = (table % 2) ^ jnp.arange(2, dtype=jnp.int32)
+            table = (jnp.arange(NZ, dtype=jnp.int32)[:, None] * BPD + table // 2 + PAIRS * odd).reshape(-1)
         ring = [VMEM((DEPTH, STEP * GROUP, BLK, BLK), bf16), DMA((DEPTH, STEP * GROUP))]
         part = call(
             functools.partial(own_kernel, hop), "own", [whole(SMEM)] * 4 + [whole(HBM), whole(), whole(HBM)],
@@ -366,6 +430,8 @@
             [VMEM((BUCKETS, BLK, BLK), f32), VMEM((PAIRS + 1, BLK, BLK), bf16), VMEM((WIDTH, BPD * BLK), f32)] + ring + [DMA(())],
             limit=FULL, flops=TPD * 2 * BLK**3, moved=4 << 20,
         )(*lists, tile_vals, owned, noise)
+        if not last:
+            part, table = lax.optimization_barrier((part, table))
         if last:
             early = call(
                 early_kernel, "early", [whole(SMEM)] + [whole()] * (1 + NX), [((PAIRS, BLK, BLK), f32, VMEM)]
@@ -373,15 +439,15 @@
             early, part = lax.optimization_barrier((early, part))
         if last:
             outs = [((PAIRS * BLK + 32, BLK), bf16, VMEM)]
-            more = []
+            more = [VMEM((N_YC * NZ, SIDE, BLK), bf16), DMA((N_YC,))]
         else:
             outs = [((PAIRS, BLK, BLK), f32, VMEM), ((BPD, BLK), f32, VMEM)]
             more = []
         result = call(
-            functools.partial(far_kernel, hop), "far", [whole(SMEM)] * 4 + [whole(HBM), whole(), whole()], outs,
+            functools.partial(far_kernel, hop), "far", [whole(SMEM)] * 5 + [whole(HBM), whole(), whole()] + [whole(HBM)] * len(sides), outs,
             [VMEM((BUCKETS, BLK, BLK), f32)] + ring + more,
             limit=ROOM, flops=TPD * 2 * BLK**3, moved=8 << 20,
-        )(*lists, tile_vals, got, part)
+        )(me, *lists, tile_vals, got, part, *sides)
         if not last:
             packed, squares = result
     tails = [result] + [shift_by(result, "x", shift) for shift in SHIFTS[1:]]

time: 190 us -> 212 us (1.12)
  the two profiles are of different devices: /device:TPU:1 before, /device:TPU:6 now
where the time goes in v4:
time: 212 us; the launch traced here: 210 us
  waiting for transfers between devices  74.3 us (35%)
  starting transfers between devices  64.8 us (31%)
  Pallas kernels  40.8 us (19%)
  local copies, waits for them, and re-layouts  15.1 us (7%)
  blocking collectives  12.9 us (6%)
    ppermute x26, waiting for transfers between devices, shift_by(): lax.ppermute(value, axis, [(i, (i + shift) % size) for i in range(size)])  41.9 us
    ppermute x26, starting transfers between devices, shift_by(): lax.ppermute(value, axis, [(i, (i + shift) % size) for i in range(size)])  40.6 us
    all_to_all x2, waiting for transfers between devices, shards(): got = lax.all_to_all(picked, ('y', 'z', 'core'), 0, 0, tiled=True)  23.6 us
    pallas_call x2, Pallas kernels, shards(): call(functools.partial(far_kernel, hop), 'far', [whole(SMEM)] * 5 + [whol...  13.6 us
    all_gather x1, blocking collectives, shards(): lax.all_gather(wide, ('y', 'core'), axis=0).reshape(N_YC, NY, NZ, NC, 2)  12.9 us
    unnamed x67, local copies, waits for them, and re-layouts  12.7 us
    all_to_all x1, starting transfers between devices, shards(): lax.all_to_all(jnp.pad(needed[0], ((0, 0), (0, BLK - 2))), ('y', 'z', 'co...  12.1 us
    all_to_all x2, starting transfers between devices, shards(): got = lax.all_to_all(picked, ('y', 'z', 'core'), 0, 0, tiled=True)  12.1 us
  transfers between devices with their start and end apart: 29, of which 14 were waited for; matrix products, arithmetic and copies ran while one was open for 2% of the time, Pallas kernels for 9%

profile of v4, /device:TPU:6, one launch (start us, length us, event | category | flops | bytes accessed | tf_op | source)
XLA Modules:
  0.0 209.7 jit_solution(12507832906478413301)
XLA Ops:
  3.1 2.1 collective-permute-start.1
  6.6 12.1 %all-to-all-start = ((s32[64,1,128]{2,1,0:T(1,128)}), s32[64,1,128]{2,1,0:T(1,128)S(1)}, u32[]{:S(2)}, u32[]{:S(2)}) async-start(s32[64,1,128]{2,1,0:T(1,128)} %copy.16), calls=%async_computation | async-start | bytes 65536 | tf_op jit(solution)/shard_map/all_to_all | solution.py:379
  19.4 8.8 %all-to-all-done = s32[64,1,128]{2,1,0:T(1,128)S(1)} async-done(((s32[64,1,128]{2,1,0:T(1,128)}), s32[64,1,128]{2,1,0:T(1,128)S(1)}, u32[]{:S(2)}, u32[]{:S(2)}) %all-to-all-start) | async-done | bytes 32800 | tf_op jit(solution)/shard_map/all_to_all | solution.py:379
  28.9 4.0 %send.2 = (bf16[64,128,128]{2,1,0:T(8,128)(2,1)}, bf16[1,4,128,128]{3,2,1,0:T(8,128)(2,1)}) custom-call(s32[3]{0:T(128)} %pad_add_fusion.me_ref, s32[64,128]{1,0:T(8,128)} %bitcast.26, bf16[4,128,128]{2,1,0:T(8,128)(2,1)} %copy-done.11, f32[8,128]{1,0:T(8,128)} %copy-done.20, f32[8,128]{1,0:T(8,128)} %copy-done.30, f32[8,128]{1,0:T(8,128)} %copy-done.31, ...), custom_call_target="tpu_custom_call" | custom-call | flops 1048576 | bytes 1048576 | tf_op jit(solution)/shard_map/send/pallas_call | solution.py:403
  32.9 5.6 %all-to-all-start.1 = ((bf16[64,128,128]{2,1,0:T(8,128)(2,1)}), bf16[64,128,128]{2,1,0:T(8,128)(2,1)}, u32[]{:S(2)}, u32[]{:S(2)}) async-start(bf16[64,128,128]{2,1,0:T(8,128)(2,1)} %get-tuple-element.52), calls=%async_computation.1 | async-start | bytes 4194304 | tf_op jit(solution)/shard_map/all_to_all | solution.py:408
  39.8 5.3 %order.1 = (s32[448]{0:T(512)S(1)}, s32[448]{0:T(512)S(1)}, s32[112]{0:T(128)S(1)}, s32[2]{0:T(128)S(1)}) custom-call(s32[3]{0:T(128)S(1)} %copy-done.16, s32[160]{0:T(256)S(1)} %bitcast.21, s32[160]{0:T(256)S(1)} %bitcast.22, s32[1]{0:T(128)S(6)} %copy.20.count_ref), custom_call_target="tpu_custom_call" | custom-call | flops 1048576 | bytes 1048576 | tf_op jit(solution)/shard_map/order/pallas_call | solution.py:389
  47.4 12.9 %all-gather.1 = s32[8,1,128]{2,1,0:T(1,128)S(1)} all-gather(s32[1,1,128]{2,1,0:T(1,128)S(1)} %bitcast.30), channel_id=2, replica_groups=mesh['y'=4,'z'=8,'core'=2,'x'=4] {'y','core'}, dimensions={0}, use_global_device_ids=true | all-gather | bytes 4608 | tf_op jit(solution)/shard_map/all_gather | solution.py:422
  60.7 5.2 %own.2.part_ref = f32[4,128,128]{2,1,0:T(8,128)} custom-call(s32[448]{0:T(512)} %copy-done.14, s32[448]{0:T(512)} %copy-done.15, s32[112]{0:T(128)} %copy-done.18, s32[2]{0:T(128)} %copy-done.19, bf16[160,128,128]{2,1,0:T(8,128)(2,1)} %tiles_ref.7, bf16[1,4,128,128]{3,2,1,0:T(8,128)(2,1)} %get-tuple-element.54.own_ref.refs_4_, f32[2,64,1024]{2,1,0:T(8,128)} %bitcast.23), custom_call_target="tpu_custom_call" | custom-call | flops 671088640 | bytes 4194304 | tf_op jit(solution)/shard_map/own/pallas_call | solution.py:427
  65.9 23.6 %all-to-all-done.1.got_ref = bf16[64,128,128]{2,1,0:T(8,128)(2,1)} async-done(((bf16[64,128,128]{2,1,0:T(8,128)(2,1)}), bf16[64,128,128]{2,1,0:T(8,128)(2,1)}, u32[]{:S(2)}, u32[]{:S(2)}) %all-to-all-start.1) | async-done | bytes 2097184 | tf_op jit(solution)/shard_map/all_to_all | solution.py:408
  89.5 6.5 %far.2 = (f32[4,128,128]{2,1,0:T(8,128)}, f32[8,128]{1,0:T(8,128)}) custom-call(s32[3]{0:T(128)} %pad_add_fusion.me_ref, s32[448]{0:T(512)} %copy-done.14, s32[448]{0:T(512)} %copy-done.15, s32[112]{0:T(128)} %copy-done.18, s32[2]{0:T(128)} %copy-done.19, bf16[160,128,128]{2,1,0:T(8,128)(2,1)} %tiles_ref.7, bf16[64,128,128]{2,1,0:T(8,128)(2,1)} %all-to-all-done.1.got_ref, ...), custom_call_target="tpu_custom_call" | custom-call | flops 671088640 | bytes 8388608 | tf_op jit(solution)/shard_map/far/pallas_call | solution.py:446
  96.0 2.1 %collective-permute-start.3 = (f32[8,128]{1,0:T(8,128)}, f32[8,128]{1,0:T(8,128)S(1)}, u32[]{:S(2)}, u32[]{:S(2)}) collective-permute-start(f32[8,128]{1,0:T(8,128)} %get-tuple-element.58.refs_0_), channel_id=1, source_target_pairs={{0,2},{1,3},{2,0},{3,1},{4,6},{5,7},{6,4},{7,5},{8,10},{9,11},{10,... | collective-permute-start | bytes 12296 | tf_op jit(solution)/shard_map/ppermute | solution.py:366
  102.0 2.4 %collective-permute-done.5.refs_3_ = f32[8,128]{1,0:T(8,128)S(1)} collective-permute-done((f32[8,128]{1,0:T(8,128)}, f32[8,128]{1,0:T(8,128)S(1)}, u32[]{:S(2)}, u32[]{:S(2)}) %collective-permute-start.5) | collective-permute-done | bytes 4128 | tf_op jit(solution)/shard_map/ppermute | solution.py:366
  105.0 3.8 %send.3 = (bf16[4,48,128]{2,1,0:T(8,128)(2,1)}, bf16[64,80,128]{2,1,0:T(8,128)(2,1)}, bf16[2,4,128,128]{3,2,1,0:T(8,128)(2,1)}) custom-call(s32[3]{0:T(128)} %pad_add_fusion.me_ref, s32[64,128]{1,0:T(8,128)} %bitcast.27, f32[4,128,128]{2,1,0:T(8,128)} %get-tuple-element.57.raw_ref, f32[8,128]{1,0:T(8,128)} %get-tuple-element.58.refs_0_, ...), custom_call_target="tpu_custom_call" | custom-call | flops 1048576 | bytes 1048576 | tf_op jit(solution)/shard_map/send/pallas_call | solution.py:403
  108.8 6.5 %all-to-all-start.2 = ((bf16[64,80,128]{2,1,0:T(8,128)(2,1)}), bf16[64,80,128]{2,1,0:T(8,128)(2,1)}, u32[]{:S(2)}, u32[]{:S(2)}) async-start(bf16[64,80,128]{2,1,0:T(8,128)(2,1)} %get-tuple-element.65), calls=%async_computation.2 | async-start | bytes 2621440 | tf_op jit(solution)/shard_map/all_to_all | solution.py:408
  115.3 3.9 %collective-permute-start.10 = (bf16[4,48,128]{2,1,0:T(8,128)(2,1)S(1)}, bf16[4,48,128]{2,1,0:T(8,128)(2,1)S(1)}, u32[]{:S(2)}, u32[]{:S(2)}) collective-permute-start(bf16[4,48,128]{2,1,0:T(8,128)(2,1)S(1)} %copy-done.13), channel_id=1, source_target_pairs={{0,48},{8,56},{16,0},{24,8},{32,16},{40,24},{48,32},{56,40},{1,49}... | collective-permute-start | bytes 147464 | tf_op jit(solution)/shard_map/ppermute | solution.py:366
  119.8 2.7 %collective-permute-start.12 = (bf16[4,48,128]{2,1,0:T(8,128)(2,1)S(1)}, bf16[4,48,128]{2,1,0:T(8,128)(2,1)S(1)}, u32[]{:S(2)}, u32[]{:S(2)}) collective-permute-start(bf16[4,48,128]{2,1,0:T(8,128)(2,1)S(1)} %copy-done.13), channel_id=1, source_target_pairs={{0,56},{8,0},{16,8},{24,16},{32,24},{40,32},{48,40},{56,48},{1,57}... | collective-permute-start | bytes 147464 | tf_op jit(solution)/shard_map/ppermute | solution.py:366
  122.5 2.4 %collective-permute-start.6 = (bf16[4,48,128]{2,1,0:T(8,128)(2,1)S(1)}, bf16[4,48,128]{2,1,0:T(8,128)(2,1)S(1)}, u32[]{:S(2)}, u32[]{:S(2)}) collective-permute-start(bf16[4,48,128]{2,1,0:T(8,128)(2,1)S(1)} %copy-done.13), channel_id=1, source_target_pairs={{0,32},{8,40},{16,48},{24,56},{32,0},{40,8},{48,16},{56,24},{1,33}... | collective-permute-start | bytes 147464 | tf_op jit(solution)/shard_map/ppermute | solution.py:366
  126.0 23.0 %collective-permute-done.10.refs_5_ = bf16[4,48,128]{2,1,0:T(8,128)(2,1)S(1)} collective-permute-done((bf16[4,48,128]{2,1,0:T(8,128)(2,1)S(1)}, bf16[4,48,128]{2,1,0:T(8,128)(2,1)S(1)}, u32[]{:S(2)}, u32[]{:S(2)}) %collective-permute-start.10) | collective-permute-done | bytes 49184 | tf_op jit(solution)/shard_map/ppermute | solution.py:366
  149.0 2.5 %collective-permute-start.8 = (bf16[4,48,128]{2,1,0:T(8,128)(2,1)S(1)}, bf16[4,48,128]{2,1,0:T(8,128)(2,1)S(1)}, u32[]{:S(2)}, u32[]{:S(2)}) collective-permute-start(bf16[4,48,128]{2,1,0:T(8,128)(2,1)S(1)} %copy-done.13), channel_id=1, source_target_pairs={{0,40},{8,48},{16,56},{24,0},{32,8},{40,16},{48,24},{56,32},{1,41}... | collective-permute-start | bytes 147464 | tf_op jit(solution)/shard_map/ppermute | solution.py:366
  154.0 2.2 %collective-permute-done.8.refs_3_ = bf16[4,48,128]{2,1,0:T(8,128)(2,1)S(1)} collective-permute-done((bf16[4,48,128]{2,1,0:T(8,128)(2,1)S(1)}, bf16[4,48,128]{2,1,0:T(8,128)(2,1)S(1)}, u32[]{:S(2)}, u32[]{:S(2)}) %collective-permute-start.8) | collective-permute-done | bytes 49184 | tf_op jit(solution)/shard_map/ppermute | solution.py:366
  157.8 1.6 pick.1
  160.0 1.6 collective-permute-start.13
  163.7 3.7 %collective-permute-start.16 = (bf16[8,48,128]{2,1,0:T(8,128)(2,1)S(1)}, bf16[8,48,128]{2,1,0:T(8,128)(2,1)S(1)}, u32[]{:S(2)}, u32[]{:S(2)}) collective-permute-start(bf16[8,48,128]{2,1,0:T(8,128)(2,1)S(1)} %get-tuple-element.68), channel_id=1, source_target_pairs={{0,128},{4,132},{64,192},{68,196},{128,0},{132,4},{192,64},{196,68... | collective-permute-start | bytes 294920 | tf_op jit(solution)/shard_map/ppermute | solution.py:366
  167.5 2.5 %collective-permute-done.16.rest_1_ = bf16[8,48,128]{2,1,0:T(8,128)(2,1)S(1)} collective-permute-done((bf16[8,48,128]{2,1,0:T(8,128)(2,1)S(1)}, bf16[8,48,128]{2,1,0:T(8,128)(2,1)S(1)}, u32[]{:S(2)}, u32[]{:S(2)}) %collective-permute-start.16) | collective-permute-done | bytes 98336 | tf_op jit(solution)/shard_map/ppermute | solution.py:366
  170.9 2.1 collective-permute-done.17.rest_2_
  174.3 2.6 %collective-permute-start.20 = (bf16[8,48,128]{2,1,0:T(8,128)(2,1)}, bf16[8,48,128]{2,1,0:T(8,128)(2,1)}, u32[]{:S(2)}, u32[]{:S(2)}) collective-permute-start(bf16[8,48,128]{2,1,0:T(8,128)(2,1)} %get-tuple-element.72), channel_id=1, source_target_pairs={{0,192},{4,196},{64,0},{68,4},{128,64},{132,68},{192,128},{196,132... | collective-permute-start | bytes 294920 | tf_op jit(solution)/shard_map/ppermute | solution.py:366
  178.7 2.6 %collective-permute-start.22 = (bf16[8,48,128]{2,1,0:T(8,128)(2,1)S(1)}, bf16[8,48,128]{2,1,0:T(8,128)(2,1)}, u32[]{:S(2)}, u32[]{:S(2)}) collective-permute-start(bf16[8,48,128]{2,1,0:T(8,128)(2,1)S(1)} %get-tuple-element.74), channel_id=1, source_target_pairs={{0,196},{4,0},{64,4},{68,64},{128,68},{132,128},{192,132},{196,192... | collective-permute-start | bytes 294920 | tf_op jit(solution)/shard_map/ppermute | solution.py:366
  181.4 5.4 %own.3.part_ref = f32[4,128,128]{2,1,0:T(8,128)} custom-call(s32[448]{0:T(512)} %copy-done.14, s32[448]{0:T(512)} %copy-done.15, s32[112]{0:T(128)} %copy-done.18, s32[2]{0:T(128)} %copy-done.19, bf16[160,128,128]{2,1,0:T(8,128)(2,1)} %tiles_ref.7, bf16[2,4,128,128]{3,2,1,0:T(8,128)(2,1)} %get-tuple-element.63.refs_0_.own_ref, f32[2,64,1024]{2,1,0:T(8,128)} %bitcast.24), custom_call_target="tpu_custom_call" | custom-call | flops 671088640 | bytes 4194304 | tf_op jit(solution)/shard_map/own/pallas_call | solution.py:427
  191.2 7.1 %far.3.refs_0_ = bf16[544,128]{1,0:T(8,128)(2,1)} custom-call(s32[3]{0:T(128)} %pad_add_fusion.me_ref, s32[448]{0:T(512)} %copy-done.14, s32[448]{0:T(512)} %copy-done.15, s32[112]{0:T(128)} %copy-done.18, s32[2]{0:T(128)} %copy-done.19, bf16[160,128,128]{2,1,0:T(8,128)(2,1)} %tiles_ref.7, bf16[64,80,128]{2,1,0:T(8,128)(2,1)} %all-to-all-done.2.got_ref, ...), custom_call_target="tpu_custom_call" | custom-call | flops 671088640 | bytes 8388608 | tf_op jit(solution)/shard_map/far/pallas_call | solution.py:446
  198.3 2.0 collective-permute-start.23
  202.4 2.9 %collective-permute-done.23.refs_1_ = bf16[544,128]{1,0:T(8,128)(2,1)S(1)} collective-permute-done((bf16[544,128]{1,0:T(8,128)(2,1)}, bf16[544,128]{1,0:T(8,128)(2,1)S(1)}, u32[]{:S(2)}, u32[]{:S(2)}) %collective-permute-start.23) | collective-permute-done | bytes 139296 | tf_op jit(solution)/shard_map/ppermute | solution.py:366
  205.8 1.7 collective-permute-done.25.refs_3_
  (121 shorter events, 35.0 us)
Async XLA Ops:
  0.0 167.4 %copy-start = (bf16[3,256,256]{2,1,0:T(8,128)(2,1)S(1)}, bf16[3,256,256]{2,1,0:T(8,128)(2,1)}, u32[]{:S(2)}) copy-start(bf16[3,256,256]{2,1,0:T(8,128)(2,1)} %param.15) | copy-start | bytes 1179652
  1.7 17.7 %collective-permute-start = (f32[8,128]{1,0:T(8,128)S(1)}, f32[8,128]{1,0:T(8,128)S(1)}, u32[]{:S(2)}, u32[]{:S(2)}) collective-permute-start(f32[8,128]{1,0:T(8,128)S(1)} %get-tuple-element.51.refs_0_), channel_id=1, source_target_pairs={{0,2},{1,3},{2,0},{3,1},{4,6},{5,7},{6,4},{7,5},{8,10},{9,11},{10,... | collective-permute-start | bytes 12296 | tf_op jit(solution)/shard_map/ppermute | solution.py:366
  3.1 16.3 %collective-permute-start.1 = (f32[8,128]{1,0:T(8,128)S(1)}, f32[8,128]{1,0:T(8,128)S(1)}, u32[]{:S(2)}, u32[]{:S(2)}) collective-permute-start(f32[8,128]{1,0:T(8,128)S(1)} %get-tuple-element.51.refs_0_), channel_id=1, source_target_pairs={{0,1},{1,2},{2,3},{3,0},{4,5},{5,6},{6,7},{7,4},{8,9},{9,10},{10,1... | collective-permute-start | bytes 12296 | tf_op jit(solution)/shard_map/ppermute | solution.py:366
  5.2 14.2 %collective-permute-start.2 = (f32[8,128]{1,0:T(8,128)S(1)}, f32[8,128]{1,0:T(8,128)S(1)}, u32[]{:S(2)}, u32[]{:S(2)}) collective-permute-start(f32[8,128]{1,0:T(8,128)S(1)} %get-tuple-element.51.refs_0_), channel_id=1, source_target_pairs={{0,3},{1,0},{2,1},{3,2},{4,7},{5,4},{6,5},{7,6},{8,11},{9,8},{10,9... | collective-permute-start | bytes 12296 | tf_op jit(solution)/shard_map/ppermute | solution.py:366
  6.6 21.6 %all-to-all-start = ((s32[64,1,128]{2,1,0:T(1,128)}), s32[64,1,128]{2,1,0:T(1,128)S(1)}, u32[]{:S(2)}, u32[]{:S(2)}) async-start(s32[64,1,128]{2,1,0:T(1,128)} %copy.16), calls=%async_computation | async-start | bytes 65536 | tf_op jit(solution)/shard_map/all_to_all | solution.py:379
  32.9 56.6 %all-to-all-start.1 = ((bf16[64,128,128]{2,1,0:T(8,128)(2,1)}), bf16[64,128,128]{2,1,0:T(8,128)(2,1)}, u32[]{:S(2)}, u32[]{:S(2)}) async-start(bf16[64,128,128]{2,1,0:T(8,128)(2,1)} %get-tuple-element.52), calls=%async_computation.1 | async-start | bytes 4194304 | tf_op jit(solution)/shard_map/all_to_all | solution.py:408
  96.0 61.8 %copy-start.17 = (s32[3]{0:T(128)S(1)}, s32[3]{0:T(128)}, u32[]{:S(2)}) copy-start(s32[3]{0:T(128)} %pad_add_fusion.me_ref) | copy-start | bytes 40
  96.0 5.4 %collective-permute-start.3 = (f32[8,128]{1,0:T(8,128)}, f32[8,128]{1,0:T(8,128)S(1)}, u32[]{:S(2)}, u32[]{:S(2)}) collective-permute-start(f32[8,128]{1,0:T(8,128)} %get-tuple-element.58.refs_0_), channel_id=1, source_target_pairs={{0,2},{1,3},{2,0},{3,1},{4,6},{5,7},{6,4},{7,5},{8,10},{9,11},{10,... | collective-permute-start | bytes 12296 | tf_op jit(solution)/shard_map/ppermute | solution.py:366
  98.1 3.9 %collective-permute-start.4 = (f32[8,128]{1,0:T(8,128)}, f32[8,128]{1,0:T(8,128)S(1)}, u32[]{:S(2)}, u32[]{:S(2)}) collective-permute-start(f32[8,128]{1,0:T(8,128)} %get-tuple-element.58.refs_0_), channel_id=1, source_target_pairs={{0,1},{1,2},{2,3},{3,0},{4,5},{5,6},{6,7},{7,4},{8,9},{9,10},{10,1... | collective-permute-start | bytes 12296 | tf_op jit(solution)/shard_map/ppermute | solution.py:366
  99.4 5.0 %collective-permute-start.5 = (f32[8,128]{1,0:T(8,128)}, f32[8,128]{1,0:T(8,128)S(1)}, u32[]{:S(2)}, u32[]{:S(2)}) collective-permute-start(f32[8,128]{1,0:T(8,128)} %get-tuple-element.58.refs_0_), channel_id=1, source_target_pairs={{0,3},{1,0},{2,1},{3,2},{4,7},{5,4},{6,5},{7,6},{8,11},{9,8},{10,9... | collective-permute-start | bytes 12296 | tf_op jit(solution)/shard_map/ppermute | solution.py:366
  108.8 51.2 %copy-start.1 = (bf16[2,4,128,128]{3,2,1,0:T(8,128)(2,1)S(1)}, bf16[2,4,128,128]{3,2,1,0:T(8,128)(2,1)}, u32[]{:S(2)}) copy-start(bf16[2,4,128,128]{3,2,1,0:T(8,128)(2,1)} %get-tuple-element.63.refs_0_.own_ref) | copy-start | bytes 786436
  108.8 82.3 %all-to-all-start.2 = ((bf16[64,80,128]{2,1,0:T(8,128)(2,1)}), bf16[64,80,128]{2,1,0:T(8,128)(2,1)}, u32[]{:S(2)}, u32[]{:S(2)}) async-start(bf16[64,80,128]{2,1,0:T(8,128)(2,1)} %get-tuple-element.65), calls=%async_computation.2 | async-start | bytes 2621440 | tf_op jit(solution)/shard_map/all_to_all | solution.py:408
  115.3 33.6 %collective-permute-start.10 = (bf16[4,48,128]{2,1,0:T(8,128)(2,1)S(1)}, bf16[4,48,128]{2,1,0:T(8,128)(2,1)S(1)}, u32[]{:S(2)}, u32[]{:S(2)}) collective-permute-start(bf16[4,48,128]{2,1,0:T(8,128)(2,1)S(1)} %copy-done.13), channel_id=1, source_target_pairs={{0,48},{8,56},{16,0},{24,8},{32,16},{40,24},{48,32},{56,40},{1,49}... | collective-permute-start | bytes 147464 | tf_op jit(solution)/shard_map/ppermute | solution.py:366
  119.2 32.3 %collective-permute-start.11 = (bf16[4,48,128]{2,1,0:T(8,128)(2,1)S(1)}, bf16[4,48,128]{2,1,0:T(8,128)(2,1)S(1)}, u32[]{:S(2)}, u32[]{:S(2)}) collective-permute-start(bf16[4,48,128]{2,1,0:T(8,128)(2,1)S(1)} %copy-done.13), channel_id=1, source_target_pairs={{0,8},{8,16},{16,24},{24,32},{32,40},{40,48},{48,56},{56,0},{1,9},... | collective-permute-start | bytes 147464 | tf_op jit(solution)/shard_map/ppermute | solution.py:366
  119.8 33.1 %collective-permute-start.12 = (bf16[4,48,128]{2,1,0:T(8,128)(2,1)S(1)}, bf16[4,48,128]{2,1,0:T(8,128)(2,1)S(1)}, u32[]{:S(2)}, u32[]{:S(2)}) collective-permute-start(bf16[4,48,128]{2,1,0:T(8,128)(2,1)S(1)} %copy-done.13), channel_id=1, source_target_pairs={{0,56},{8,0},{16,8},{24,16},{32,24},{40,32},{48,40},{56,48},{1,57}... | collective-permute-start | bytes 147464 | tf_op jit(solution)/shard_map/ppermute | solution.py:366
  122.5 31.6 %collective-permute-start.6 = (bf16[4,48,128]{2,1,0:T(8,128)(2,1)S(1)}, bf16[4,48,128]{2,1,0:T(8,128)(2,1)S(1)}, u32[]{:S(2)}, u32[]{:S(2)}) collective-permute-start(bf16[4,48,128]{2,1,0:T(8,128)(2,1)S(1)} %copy-done.13), channel_id=1, source_target_pairs={{0,32},{8,40},{16,48},{24,56},{32,0},{40,8},{48,16},{56,24},{1,33}... | collective-permute-start | bytes 147464 | tf_op jit(solution)/shard_map/ppermute | solution.py:366
  124.8 29.2 %collective-permute-start.7 = (bf16[4,48,128]{2,1,0:T(8,128)(2,1)S(1)}, bf16[4,48,128]{2,1,0:T(8,128)(2,1)S(1)}, u32[]{:S(2)}, u32[]{:S(2)}) collective-permute-start(bf16[4,48,128]{2,1,0:T(8,128)(2,1)S(1)} %copy-done.13), channel_id=1, source_target_pairs={{0,24},{8,32},{16,40},{24,48},{32,56},{40,0},{48,8},{56,16},{1,25}... | collective-permute-start | bytes 147464 | tf_op jit(solution)/shard_map/ppermute | solution.py:366
  149.0 7.3 %collective-permute-start.8 = (bf16[4,48,128]{2,1,0:T(8,128)(2,1)S(1)}, bf16[4,48,128]{2,1,0:T(8,128)(2,1)S(1)}, u32[]{:S(2)}, u32[]{:S(2)}) collective-permute-start(bf16[4,48,128]{2,1,0:T(8,128)(2,1)S(1)} %copy-done.13), channel_id=1, source_target_pairs={{0,40},{8,48},{16,56},{24,0},{32,8},{40,16},{48,24},{56,32},{1,41}... | collective-permute-start | bytes 147464 | tf_op jit(solution)/shard_map/ppermute | solution.py:366
  151.5 6.3 %collective-permute-start.9 = (bf16[4,48,128]{2,1,0:T(8,128)(2,1)S(1)}, bf16[4,48,128]{2,1,0:T(8,128)(2,1)S(1)}, u32[]{:S(2)}, u32[]{:S(2)}) collective-permute-start(bf16[4,48,128]{2,1,0:T(8,128)(2,1)S(1)} %copy-done.13), channel_id=1, source_target_pairs={{0,16},{8,24},{16,32},{24,40},{32,48},{40,56},{48,0},{56,8},{1,17}... | collective-permute-start | bytes 147464 | tf_op jit(solution)/shard_map/ppermute | solution.py:366
  160.0 13.6 %collective-permute-start.13 = (bf16[2,4,128,128]{3,2,1,0:T(8,128)(2,1)S(1)}, bf16[2,4,128,128]{3,2,1,0:T(8,128)(2,1)S(1)}, u32[]{:S(2)}, u32[]{:S(2)}) collective-permute-start(bf16[2,4,128,128]{3,2,1,0:T(8,128)(2,1)S(1)} %copy-done.1), channel_id=1, source_target_pairs={{0,2},{1,3},{2,0},{3,1},{4,6},{5,7},{6,4},{7,5},{8,10},{9,11},{10,... | collective-permute-start | bytes 786440 | tf_op jit(solution)/shard_map/ppermute | solution.py:366
  161.7 15.2 %collective-permute-start.14 = (bf16[2,4,128,128]{3,2,1,0:T(8,128)(2,1)S(1)}, bf16[2,4,128,128]{3,2,1,0:T(8,128)(2,1)S(1)}, u32[]{:S(2)}, u32[]{:S(2)}) collective-permute-start(bf16[2,4,128,128]{3,2,1,0:T(8,128)(2,1)S(1)} %copy-done.1), channel_id=1, source_target_pairs={{0,1},{1,2},{2,3},{3,0},{4,5},{5,6},{6,7},{7,4},{8,9},{9,10},{10,1... | collective-permute-start | bytes 786440 | tf_op jit(solution)/shard_map/ppermute | solution.py:366
  162.3 15.6 %collective-permute-start.15 = (bf16[2,4,128,128]{3,2,1,0:T(8,128)(2,1)S(1)}, bf16[2,4,128,128]{3,2,1,0:T(8,128)(2,1)S(1)}, u32[]{:S(2)}, u32[]{:S(2)}) collective-permute-start(bf16[2,4,128,128]{3,2,1,0:T(8,128)(2,1)S(1)} %copy-done.1), channel_id=1, source_target_pairs={{0,3},{1,0},{2,1},{3,2},{4,7},{5,4},{6,5},{7,6},{8,11},{9,8},{10,9... | collective-permute-start | bytes 786440 | tf_op jit(solution)/shard_map/ppermute | solution.py:366
  163.7 6.4 %collective-permute-start.16 = (bf16[8,48,128]{2,1,0:T(8,128)(2,1)S(1)}, bf16[8,48,128]{2,1,0:T(8,128)(2,1)S(1)}, u32[]{:S(2)}, u32[]{:S(2)}) collective-permute-start(bf16[8,48,128]{2,1,0:T(8,128)(2,1)S(1)} %get-tuple-element.68), channel_id=1, source_target_pairs={{0,128},{4,132},{64,192},{68,196},{128,0},{132,4},{192,64},{196,68... | collective-permute-start | bytes 294920 | tf_op jit(solution)/shard_map/ppermute | solution.py:366
  167.4 5.5 %collective-permute-start.17 = (bf16[8,48,128]{2,1,0:T(8,128)(2,1)S(1)}, bf16[8,48,128]{2,1,0:T(8,128)(2,1)S(1)}, u32[]{:S(2)}, u32[]{:S(2)}) collective-permute-start(bf16[8,48,128]{2,1,0:T(8,128)(2,1)S(1)} %get-tuple-element.69), channel_id=1, source_target_pairs={{0,68},{4,128},{64,132},{68,192},{128,196},{132,0},{192,4},{196,64... | collective-permute-start | bytes 294920 | tf_op jit(solution)/shard_map/ppermute | solution.py:366
  170.1 21.1 %collective-permute-start.18 = (bf16[8,48,128]{2,1,0:T(8,128)(2,1)}, bf16[8,48,128]{2,1,0:T(8,128)(2,1)}, u32[]{:S(2)}, u32[]{:S(2)}) collective-permute-start(bf16[8,48,128]{2,1,0:T(8,128)(2,1)} %get-tuple-element.70), channel_id=1, source_target_pairs={{0,132},{4,192},{64,196},{68,0},{128,4},{132,64},{192,68},{196,128... | collective-permute-start | bytes 294920 | tf_op jit(solution)/shard_map/ppermute | solution.py:366
  172.9 18.2 %collective-permute-start.19 = (bf16[8,48,128]{2,1,0:T(8,128)(2,1)}, bf16[8,48,128]{2,1,0:T(8,128)(2,1)}, u32[]{:S(2)}, u32[]{:S(2)}) collective-permute-start(bf16[8,48,128]{2,1,0:T(8,128)(2,1)} %get-tuple-element.71), channel_id=1, source_target_pairs={{0,64},{4,68},{64,128},{68,132},{128,192},{132,196},{192,0},{196,4... | collective-permute-start | bytes 294920 | tf_op jit(solution)/shard_map/ppermute | solution.py:366
  174.3 16.8 %collective-permute-start.20 = (bf16[8,48,128]{2,1,0:T(8,128)(2,1)}, bf16[8,48,128]{2,1,0:T(8,128)(2,1)}, u32[]{:S(2)}, u32[]{:S(2)}) collective-permute-start(bf16[8,48,128]{2,1,0:T(8,128)(2,1)} %get-tuple-element.72), channel_id=1, source_target_pairs={{0,192},{4,196},{64,0},{68,4},{128,64},{132,68},{192,128},{196,132... | collective-permute-start | bytes 294920 | tf_op jit(solution)/shard_map/ppermute | solution.py:366
  177.6 13.5 %collective-permute-start.21 = (bf16[8,48,128]{2,1,0:T(8,128)(2,1)}, bf16[8,48,128]{2,1,0:T(8,128)(2,1)}, u32[]{:S(2)}, u32[]{:S(2)}) collective-permute-start(bf16[8,48,128]{2,1,0:T(8,128)(2,1)} %get-tuple-element.73), channel_id=1, source_target_pairs={{0,4},{4,64},{64,68},{68,128},{128,132},{132,192},{192,196},{196,0... | collective-permute-start | bytes 294920 | tf_op jit(solution)/shard_map/ppermute | solution.py:366
  178.7 12.5 %collective-permute-start.22 = (bf16[8,48,128]{2,1,0:T(8,128)(2,1)S(1)}, bf16[8,48,128]{2,1,0:T(8,128)(2,1)}, u32[]{:S(2)}, u32[]{:S(2)}) collective-permute-start(bf16[8,48,128]{2,1,0:T(8,128)(2,1)S(1)} %get-tuple-element.74), channel_id=1, source_target_pairs={{0,196},{4,0},{64,4},{68,64},{128,68},{132,128},{192,132},{196,192... | collective-permute-start | bytes 294920 | tf_op jit(solution)/shard_map/ppermute | solution.py:366
  198.3 7.0 %collective-permute-start.23 = (bf16[544,128]{1,0:T(8,128)(2,1)}, bf16[544,128]{1,0:T(8,128)(2,1)S(1)}, u32[]{:S(2)}, u32[]{:S(2)}) collective-permute-start(bf16[544,128]{1,0:T(8,128)(2,1)} %far.3.refs_0_), channel_id=1, source_target_pairs={{0,2},{1,3},{2,0},{3,1},{4,6},{5,7},{6,4},{7,5},{8,10},{9,11},{10,... | collective-permute-start | bytes 417800 | tf_op jit(solution)/shard_map/ppermute | solution.py:366
  200.3 5.5 %collective-permute-start.24 = (bf16[544,128]{1,0:T(8,128)(2,1)}, bf16[544,128]{1,0:T(8,128)(2,1)S(1)}, u32[]{:S(2)}, u32[]{:S(2)}) collective-permute-start(bf16[544,128]{1,0:T(8,128)(2,1)} %far.3.refs_0_), channel_id=1, source_target_pairs={{0,1},{1,2},{2,3},{3,0},{4,5},{5,6},{6,7},{7,4},{8,9},{9,10},{10,1... | collective-permute-start | bytes 417800 | tf_op jit(solution)/shard_map/ppermute | solution.py:366
  201.1 6.5 %collective-permute-start.25 = (bf16[544,128]{1,0:T(8,128)(2,1)}, bf16[544,128]{1,0:T(8,128)(2,1)S(1)}, u32[]{:S(2)}, u32[]{:S(2)}) collective-permute-start(bf16[544,128]{1,0:T(8,128)(2,1)} %far.3.refs_0_), channel_id=1, source_target_pairs={{0,3},{1,0},{2,1},{3,2},{4,7},{5,4},{6,5},{7,6},{8,11},{9,8},{10,9... | collective-permute-start | bytes 417800 | tf_op jit(solution)/shard_map/ppermute | solution.py:366
  (30 other events, 133.5 us)

commit v5 on v3

--- a/solution.py
+++ b/solution.py
@@ -88,31 +88,41 @@
     sq_ref[...] = jnp.concatenate(rows, axis=0)
 
 
-def send_kernel(hop, me_ref, idx_ref, raw_ref, *refs):
-    sum_refs = refs[:NX]
-    out_ref, own_ref, slots, buf, sem = refs[-5:]
-    total = sum_refs[0][...]
-    for ref in sum_refs[1:]:
+def total_of(refs):
+    total = refs[0][...]
+    for ref in refs[1:]:
         total = total + ref[...]
-    columns = row_scale(total)
-    if hop:
-        own_ref[0:hop] = refs[NX][...]
+    return total
+
+
+def swapped(v):
+    return jnp.concatenate([v[:, WIDTH:], v[:, :WIDTH]], axis=1)
+
+
+def norm_kernel(raw_ref, *refs):
+    out_ref, own_ref, buf, sem = refs[NX:]
+    columns = row_scale(total_of(refs[:NX]))
+    copies = []
     for p in range(PAIRS):
         v = (raw_ref[p].astype(f32) * pair_scale(columns, p)).astype(bf16)
-        own_ref[hop, p] = v
-        slots[p] = v
-        slots[PAIRS + p] = jnp.concatenate([v[:, WIDTH:], v[:, :WIDTH]], axis=1)
+        buf[p] = v
+        own_ref[0, p] = v
+    for z in range(NZ):
+        copy = pltpu.make_async_copy(buf, out_ref.at[z], sem.at[z])
+        copy.start()
+        copies.append(copy)
+    for copy in copies:
+        copy.wait()
+
+
+def write_slabs(me_ref, idx_ref, slots, out_ref, buf, sem):
     mask = lane_low((BLK, BLK))
-    mine = (me_ref[0] * NZ + me_ref[1]) * NC + me_ref[2]
+    mine = (me_ref[0] * NC + me_ref[2]) * NZ + me_ref[1]
     copies = []
     for part in range(N_ROW // BATCH):
         for j in range(BATCH):
             i = part * BATCH + j
-            first = idx_ref[i, 0]
-            second = idx_ref[i, 1]
-            low = slots[(first >> 1) | ((first & 1) << 2)]
-            high = slots[((second >> 1) | ((second & 1) << 2)) ^ PAIRS]
-            buf[i] = jnp.where(mask, low, high)
+            buf[i] = jnp.where(mask, slots[idx_ref[2 * i]], slots[idx_ref[2 * i + 1]])
 
         @pl.when(mine // BATCH == part)
         def _():
@@ -127,9 +137,30 @@
         copy.wait()
 
 
+def pick_kernel(me_ref, idx_ref, z_ref, out_ref, slots, buf, sem):
+    for z in range(NZ):
+        for p in range(PAIRS):
+            v = z_ref[z, p]
+            slots[z * BPD + p] = v
+            slots[z * BPD + PAIRS + p] = swapped(v)
+    write_slabs(me_ref, idx_ref, slots, out_ref, buf, sem)
+
+
+def send_kernel(me_ref, idx_ref, raw_ref, *refs):
+    before_ref, out_ref, own_ref, slots, buf, sem = refs[NX:]
+    columns = row_scale(total_of(refs[:NX]))
+    own_ref[0] = before_ref[0]
+    for p in range(PAIRS):
+        v = (raw_ref[p] * pair_scale(columns, p)).astype(bf16)
+        own_ref[1, p] = v
+        slots[p] = v
+        slots[PAIRS + p] = swapped(v)
+    write_slabs(me_ref, idx_ref, slots, out_ref, buf, sem)
+
+
 def order_kernel(me_ref, rows_ref, srcs_ref, count_ref, tile_ref, slab_ref, into_ref, groups_ref, fill, begin):
     count = count_ref[0]
-    empty = (me_ref[0] * NZ + me_ref[1]) * NC + me_ref[2]
+    empty = (me_ref[0] * NC + me_ref[2]) * NZ + me_ref[1]
 
     @pl.loop(0, SLOTS // 8)
     def _(i):
@@ -175,7 +206,9 @@
         begin[b] = at + 1
         s = srcs_ref[t]
         tile_ref[at] = t
-        slab_ref[at] = jnp.where(s < BPD, s >> 1, (s - BPD) >> 1)
+        o = (s - BPD) >> 1
+        far_slab = (((o >> 4) * NC) + (o & 1)) * NZ + ((o >> 1) & (NZ - 1))
+        slab_ref[at] = jnp.where(s < BPD, s >> 1, far_slab)
 
 
 def add_groups(kind, tile_ref, slab_ref, into_ref, groups_ref, tiles_ref, src, acc, ring, sem):
@@ -320,6 +353,12 @@
     return lax.ppermute(value, axis, [(i, (i + shift) % size) for i in range(size)])
 
 
+def slot_table(asked, start, base):
+    mine = lax.dynamic_slice(asked, (0, *start, 0), (asked.shape[0], 1, base.shape[0], 1, 2)).reshape(asked.shape[0], base.shape[0], 2)
+    odd = (mine & 1) ^ jnp.arange(2, dtype=jnp.int32)
+    return (base[:, None] + (mine >> 1) + PAIRS * odd).reshape(-1)
+
+
 def shards(features, tile_vals, tile_rows, tile_srcs, tile_count, needed, hop_noise, enc_weight):
     me = jnp.stack([lax.axis_index("y"), lax.axis_index("z"), lax.axis_index("core")]).astype(jnp.int32)
     x_index = lax.axis_index("x").astype(jnp.int32)
@@ -330,9 +369,8 @@
         pack_kernel, "pack", [whole()],
         [((PAIRS, BLK, BLK), bf16, VMEM), ((BPD, BLK), f32, VMEM)],
     )(features.T)
-    asked = lax.all_to_all(jnp.pad(needed[0], ((0, 0), (0, BLK - 2))), ("y", "z", "core"), 0, 0, tiled=True)
-    packed, squares, rows, srcs, count, enc_weight = lax.optimization_barrier(
-        (packed, squares, tile_rows.reshape(-1), tile_srcs.reshape(-1), tile_count, enc_weight)
+    packed, squares, rows, srcs, count, enc_weight, needed = lax.optimization_barrier(
+        (packed, squares, tile_rows.reshape(-1), tile_srcs.reshape(-1), tile_count, enc_weight, needed.reshape(-1))
     )
 
     weights = lax.dynamic_slice_in_dim(enc_weight, x_index * WIDTH, WIDTH, axis=2).reshape(HOPS + 1, NX, WIDTH, WIDTH)
@@ -349,16 +387,36 @@
     for hop in range(HOPS):
         last = hop == HOPS - 1
         totals = [squares] + [shift_by(squares, "x", shift) for shift in SHIFTS[1:]]
-        before = [owned] if hop else []
-        picked, owned = call(
-            functools.partial(send_kernel, hop), "send", [whole(SMEM)] * 2 + [whole()] * (1 + NX + hop),
-            [((N_ROW, BLK, BLK), bf16, HBM), ((hop + 1, PAIRS, BLK, BLK), bf16, VMEM)],
-            [VMEM((BPD, BLK, BLK), bf16), VMEM((N_ROW, BLK, BLK), bf16), DMA((N_ROW // BATCH,))],
-            limit=MOST,
-        )(me, asked, packed, *totals, *before)
+        wide = [((N_ROW, BLK, BLK), bf16, HBM)]
         if last:
+            picked, owned = call(
+                send_kernel, "send", [whole(SMEM)] * 2 + [whole()] * (2 + NX), wide + [((2, PAIRS, BLK, BLK), bf16, VMEM)],
+                [VMEM((BPD, BLK, BLK), bf16), VMEM((N_ROW, BLK, BLK), bf16), DMA((N_ROW // BATCH,))],
+                limit=MOST,
+            )(me, table, packed, *totals, owned)
             spread = [owned] + [shift_by(owned, "x", shift) for shift in SHIFTS[1:]]
-        got = lax.all_to_all(picked, ("y", "z", "core"), 0, 0, tiled=True)
+            got = lax.all_to_all(picked, ("y", "core", "z"), 0, 0, tiled=True)
+        else:
+            packed, owned = call(
+                norm_kernel, "norm", [whole()] * (1 + NX),
+                [((NZ, PAIRS, BLK, BLK), bf16, HBM), ((1, PAIRS, BLK, BLK), bf16, VMEM)],
+                [VMEM((PAIRS, BLK, BLK), bf16), DMA((NZ,))],
+                limit=TIGHT,
+            )(packed, *totals)
+            along = lax.all_to_all(packed, "z", 0, 0, tiled=True)
+            needed, owned = lax.optimization_barrier((needed, owned))
+            asked = lax.all_gather(needed, ("y", "core"), axis=0)
+            table = slot_table(asked.reshape(NY * NC, NY, NZ, NC, 2), (me[0], 0, me[2]), jnp.arange(NZ, dtype=jnp.int32) * BPD)
+            at, table, asked, *lists = lax.optimization_barrier((me, table, asked, *lists))
+            picked = call(
+                pick_kernel, "pick", [whole(SMEM)] * 2 + [whole()], wide,
+                [VMEM((NZ * BPD, BLK, BLK), bf16), VMEM((N_ROW, BLK, BLK), bf16), DMA((N_ROW // BATCH,))],
+                limit=MOST,
+            )(at, table, along)
+            picked, asked = lax.optimization_barrier((picked, asked))
+            got = lax.all_to_all(picked, ("y", "core"), 0, 0, tiled=True)
+            everyone = lax.all_gather(asked, "z", axis=1).reshape(NY * NC * NZ, NY, NZ, NC, 2)
+            table = slot_table(everyone, (me[0], me[1], me[2]), jnp.zeros((1,), jnp.int32))
         ring = [VMEM((DEPTH, STEP * GROUP, BLK, BLK), bf16), DMA((DEPTH, STEP * GROUP))]
         part = call(
             functools.partial(own_kernel, hop), "own", [whole(SMEM)] * 4 + [whole(HBM), whole(), whole(HBM)],
@@ -366,6 +424,8 @@
             [VMEM((BUCKETS, BLK, BLK), f32), VMEM((PAIRS + 1, BLK, BLK), bf16), VMEM((WIDTH, BPD * BLK), f32)] + ring + [DMA(())],
             limit=FULL, flops=TPD * 2 * BLK**3, moved=4 << 20,
         )(*lists, tile_vals, owned, noise)
+        if not last:
+            part, table = lax.optimization_barrier((part, table))
         if last:
             early = call(
                 early_kernel, "early", [whole(SMEM)] + [whole()] * (1 + NX), [((PAIRS, BLK, BLK), f32, VMEM)]

time: 190 us -> 195 us (1.026)
  waiting for transfers between devices: 94.2 us -> 57.3 us
  blocking collectives: 0 us -> 29.3 us
  local copies, waits for them, and re-layouts: 7.51 us -> 12.8 us
  Pallas kernels: 44.7 us -> 47.5 us
  starting transfers between devices: 41.2 us -> 43.4 us
    all_to_all x3, waiting for transfers between devices: 78 us -> 38.9 us  [the longest x1 32.9 us: shards(): got = lax.all_to_all(picked, ('y', 'core', 'z'), 0, 0, tiled=True)]
    all_gather x0 -> x2, blocking collectives: none -> 29.3 us  [the longest x1 19.9 us: shards(): lax.all_gather(asked, 'z', axis=1).reshape(NY * NC * NZ, NY, NZ, NC, 2)]
    reshape x0 -> x2, local copies, waits for them, and re-layouts: none -> 3.34 us  [the longest x1 3.2 us: shards(): lax.all_gather(asked, 'z', axis=1).reshape(NY * NC * NZ, NY, NZ, NC, 2)]
    ppermute x12, waiting for transfers between devices: 16.2 us -> 18.4 us  [shift_by(): lax.ppermute(value, axis, [(i, (i + shift) % size) for i in range(size)])]
    unnamed x38 -> x40, local copies, waits for them, and re-layouts: 6.01 us -> 7.96 us
    pallas_call x2 -> x3, Pallas kernels: 8.03 us -> 9.95 us  [the longest x1 3.86 us: shards(): call(send_kernel, 'send', [whole(SMEM)] * 2 + [whole()] * (2 + NX), wide...]
  transfers between devices with their start and end apart: 15 -> 15, of which waited for: 9 -> 10; matrix products, arithmetic and copies ran while one was open for 1% -> 3% of each run, Pallas kernels for 11% -> 11%
where the time goes in v5:
time: 195 us; the launch traced here: 193 us
  waiting for transfers between devices  57.3 us (29%)
  Pallas kernels  47.5 us (24%)
  starting transfers between devices  43.4 us (22%)
  blocking collectives  29.3 us (15%)
  local copies, waits for them, and re-layouts  12.8 us (7%)
    all_to_all x1, waiting for transfers between devices, shards(): got = lax.all_to_all(picked, ('y', 'core', 'z'), 0, 0, tiled=True)  32.9 us
    all_gather x1, blocking collectives, shards(): lax.all_gather(asked, 'z', axis=1).reshape(NY * NC * NZ, NY, NZ, NC, 2)  19.9 us
    ppermute x12, waiting for transfers between devices, shift_by(): lax.ppermute(value, axis, [(i, (i + shift) % size) for i in range(size)])  18.4 us
    ppermute x12, starting transfers between devices, shift_by(): lax.ppermute(value, axis, [(i, (i + shift) % size) for i in range(size)])  17.4 us
    pallas_call x2, Pallas kernels, shards(): call(functools.partial(far_kernel, hop), 'far', [whole(SMEM)] * 4 + [whol...  14.8 us
    pallas_call x2, Pallas kernels, shards(): call(functools.partial(own_kernel, hop), 'own', [whole(SMEM)] * 4 + [whol...  12.3 us
    all_to_all x1, starting transfers between devices, shards(): got = lax.all_to_all(picked, ('y', 'core', 'z'), 0, 0, tiled=True)  11.2 us
    all_gather x1, blocking collectives, shards(): asked = lax.all_gather(needed, ('y', 'core'), axis=0)  9.37 us
  transfers between devices with their start and end apart: 15, of which 10 were waited for; matrix products, arithmetic and copies ran while one was open for 3% of the time, Pallas kernels for 11%

profile of v5, /device:TPU:1, one launch (start us, length us, event | category | flops | bytes accessed | tf_op | source)
XLA Modules:
  0.0 192.7 jit_solution(9001380414517310016)
XLA Ops:
  2.6 3.3 %collective-permute-start.2 = (f32[8,128]{1,0:T(8,128)S(1)}, f32[8,128]{1,0:T(8,128)S(1)}, u32[]{:S(2)}, u32[]{:S(2)}) collective-permute-start(f32[8,128]{1,0:T(8,128)S(1)} %get-tuple-element.44.refs_0_), channel_id=1, source_target_pairs={{0,3},{1,0},{2,1},{3,2},{4,7},{5,4},{6,5},{7,6},{8,11},{9,8},{10,9... | collective-permute-start | bytes 12296 | tf_op jit(solution)/shard_map/ppermute | solution.py:353
  5.9 1.7 collective-permute-start
  7.7 1.9 %collective-permute-done.1.refs_2_ = f32[8,128]{1,0:T(8,128)S(1)} collective-permute-done((f32[8,128]{1,0:T(8,128)S(1)}, f32[8,128]{1,0:T(8,128)S(1)}, u32[]{:S(2)}, u32[]{:S(2)}) %collective-permute-start.1) | collective-permute-done | bytes 4128 | tf_op jit(solution)/shard_map/ppermute | solution.py:353
  10.8 3.0 %norm.1 = (bf16[8,4,128,128]{3,2,1,0:T(8,128)(2,1)}, bf16[1,4,128,128]{3,2,1,0:T(8,128)(2,1)}) custom-call(bf16[4,128,128]{2,1,0:T(8,128)(2,1)} %copy-done.2, f32[8,128]{1,0:T(8,128)} %copy-done.9, f32[8,128]{1,0:T(8,128)} %copy-done.18, f32[8,128]{1,0:T(8,128)} %copy-done.17, f32[8,128]{1,0:T(8,128)} %copy-done.16), custom_call_target="tpu_custom_call" | custom-call | flops 1048576 | bytes 1048576 | tf_op jit(solution)/shard_map/norm/pallas_call | solution.py:400
  13.8 8.2 %all-to-all-start = ((bf16[8,4,128,128]{3,2,1,0:T(8,128)(2,1)}), bf16[8,4,128,128]{3,2,1,0:T(8,128)(2,1)S(1)}, u32[]{:S(2)}, u32[]{:S(2)}) async-start(bf16[8,4,128,128]{3,2,1,0:T(8,128)(2,1)} %get-tuple-element.61), calls=%async_computation | async-start | bytes 2097152 | tf_op jit(solution)/shard_map/all_to_all | solution.py:406
  23.1 7.6 %order.1 = (s32[448]{0:T(512)S(1)}, s32[448]{0:T(512)S(1)}, s32[112]{0:T(128)S(1)}, s32[2]{0:T(128)S(1)}) custom-call(s32[3]{0:T(128)S(1)} %pad_add_fusion.me_ref, s32[160]{0:T(256)S(1)} %bitcast.24, s32[160]{0:T(256)S(1)} %bitcast.25, s32[1]{0:T(128)S(6)} %copy.26.count_ref), custom_call_target="tpu_custom_call" | custom-call | flops 1048576 | bytes 1048576 | tf_op jit(solution)/shard_map/order/pallas_call | solution.py:381
  32.8 9.4 %all-gather.2 = s32[8,1,128]{2,1,0:T(1,128)S(1)} all-gather(s32[1,1,128]{2,1,0:T(1,128)S(1)} %bitcast.31), channel_id=2, replica_groups=mesh['y'=4,'z'=8,'core'=2,'x'=4] {'y','core'}, dimensions={0}, use_global_device_ids=true | all-gather | bytes 4608 | tf_op jit(solution)/shard_map/all_gather | solution.py:408
  43.5 6.1 %all-to-all-done.z_ref = bf16[8,4,128,128]{3,2,1,0:T(8,128)(2,1)S(1)} async-done(((bf16[8,4,128,128]{3,2,1,0:T(8,128)(2,1)}), bf16[8,4,128,128]{3,2,1,0:T(8,128)(2,1)S(1)}, u32[]{:S(2)}, u32[]{:S(2)}) %all-to-all-start) | async-done | bytes 1048608 | tf_op jit(solution)/shard_map/all_to_all | solution.py:406
  50.5 3.1 %pick.1 = bf16[64,128,128]{2,1,0:T(8,128)(2,1)} custom-call(s32[3]{0:T(128)} %copy-done.8, s32[128]{0:T(128)} %multiply_add_fusion.1.idx_ref, bf16[8,4,128,128]{3,2,1,0:T(8,128)(2,1)} %copy-done.12), custom_call_target="tpu_custom_call" | custom-call | flops 1048576 | bytes 1048576 | tf_op jit(solution)/shard_map/pick/pallas_call | solution.py:411
  53.6 6.6 %all-to-all-start.1 = ((bf16[64,128,128]{2,1,0:T(8,128)(2,1)}), bf16[64,128,128]{2,1,0:T(8,128)(2,1)}, u32[]{:S(2)}, u32[]{:S(2)}) async-start(bf16[64,128,128]{2,1,0:T(8,128)(2,1)} %pick.1), calls=%async_computation.1 | async-start | bytes 4194304 | tf_op jit(solution)/shard_map/all_to_all | solution.py:417
  60.4 6.1 %own.2.part_ref = f32[4,128,128]{2,1,0:T(8,128)} custom-call(s32[448]{0:T(512)} %copy-done.4, s32[448]{0:T(512)} %copy-done.5, s32[112]{0:T(128)} %copy-done.6, s32[2]{0:T(128)} %copy-done.7, bf16[160,128,128]{2,1,0:T(8,128)(2,1)} %tiles_ref.7, bf16[1,4,128,128]{3,2,1,0:T(8,128)(2,1)} %get-tuple-element.58.own_ref.refs_4_, f32[2,64,1024]{2,1,0:T(8,128)} %bitcast.26), custom_call_target="tpu_custom_call" | custom-call | flops 671088640 | bytes 4194304 | tf_op jit(solution)/shard_map/own/pallas_call | solution.py:421
  66.5 19.9 %all-gather.1 = s32[8,1024]{1,0:T(8,128)S(1)} all-gather(s32[8,128]{1,0:T(8,128)S(1)} %bitcast.30), channel_id=3, replica_groups=mesh['y'=4,'z'=8,'core'=2,'x'=4] {'z'}, dimensions={1}, use_global_device_ids=true | all-gather | bytes 36864 | tf_op jit(solution)/shard_map/all_gather | solution.py:418
  86.4 3.2 %reshape.59 = s32[64,4,8,2,2]{4,3,2,1,0:T(2,128)S(1)} reshape(s32[8,1024]{1,0:T(8,128)S(1)} %all-gather.1) | data formatting | bytes 65536 | tf_op jit(solution)/shard_map/reshape | solution.py:418
  90.6 7.4 %far.2 = (f32[4,128,128]{2,1,0:T(8,128)}, f32[8,128]{1,0:T(8,128)}) custom-call(s32[448]{0:T(512)} %copy-done.4, s32[448]{0:T(512)} %copy-done.5, s32[112]{0:T(128)} %copy-done.6, s32[2]{0:T(128)} %copy-done.7, bf16[160,128,128]{2,1,0:T(8,128)(2,1)} %tiles_ref.7, bf16[64,128,128]{2,1,0:T(8,128)(2,1)} %all-to-all-done.1.got_ref, f32[4,128,128]{2,1,0:T(8,128)} %own.2.part_ref), custom_call_target="tpu_custom_call" | custom-call | flops 671088640 | bytes 8388608 | tf_op jit(solution)/shard_map/far/pallas_call | solution.py:440
  98.0 2.5 %collective-permute-start.5 = (f32[8,128]{1,0:T(8,128)}, f32[8,128]{1,0:T(8,128)S(1)}, u32[]{:S(2)}, u32[]{:S(2)}) collective-permute-start(f32[8,128]{1,0:T(8,128)} %get-tuple-element.68.refs_0_), channel_id=1, source_target_pairs={{0,3},{1,0},{2,1},{3,2},{4,7},{5,4},{6,5},{7,6},{8,11},{9,8},{10,9... | collective-permute-start | bytes 12296 | tf_op jit(solution)/shard_map/ppermute | solution.py:353
  100.5 1.3 collective-permute-start.3
  101.8 2.6 %collective-permute-done.4.refs_2_ = f32[8,128]{1,0:T(8,128)S(1)} collective-permute-done((f32[8,128]{1,0:T(8,128)}, f32[8,128]{1,0:T(8,128)S(1)}, u32[]{:S(2)}, u32[]{:S(2)}) %collective-permute-start.4) | collective-permute-done | bytes 4128 | tf_op jit(solution)/shard_map/ppermute | solution.py:353
  105.3 3.9 %send.1 = (bf16[64,128,128]{2,1,0:T(8,128)(2,1)}, bf16[2,4,128,128]{3,2,1,0:T(8,128)(2,1)}) custom-call(s32[3]{0:T(128)} %copy-done.8, s32[128]{0:T(128)} %multiply_add_fusion.idx_ref, f32[4,128,128]{2,1,0:T(8,128)} %get-tuple-element.67.raw_ref, f32[8,128]{1,0:T(8,128)} %get-tuple-element.68.refs_0_, f32[8,128]{1,0:T(8,128)} %copy-done.15, ...), custom_call_target="tpu_custom_call" | custom-call | flops 1048576 | bytes 1048576 | tf_op jit(solution)/shard_map/send/pallas_call | solution.py:392
  109.1 11.2 %all-to-all-start.2 = ((bf16[64,128,128]{2,1,0:T(8,128)(2,1)}), bf16[64,128,128]{2,1,0:T(8,128)(2,1)}, u32[]{:S(2)}, u32[]{:S(2)}) async-start(bf16[64,128,128]{2,1,0:T(8,128)(2,1)} %get-tuple-element.71), calls=%async_computation.2 | async-start | bytes 4194304 | tf_op jit(solution)/shard_map/all_to_all | solution.py:398
  120.3 3.0 %collective-permute-start.8 = (bf16[2,4,128,128]{3,2,1,0:T(8,128)(2,1)}, bf16[2,4,128,128]{3,2,1,0:T(8,128)(2,1)}, u32[]{:S(2)}, u32[]{:S(2)}) collective-permute-start(bf16[2,4,128,128]{3,2,1,0:T(8,128)(2,1)} %get-tuple-element.69.refs_0_.own_ref), channel_id=1, source_target_pairs={{0,3},{1,0},{2,1},{3,2},{4,7},{5,4},{6,5},{7,6},{8,11},{9,8},{10,9... | collective-permute-start | bytes 786440 | tf_op jit(solution)/shard_map/ppermute | solution.py:353
  123.4 1.3 collective-permute-start.6
  124.9 6.1 %own.3.part_ref = f32[4,128,128]{2,1,0:T(8,128)} custom-call(s32[448]{0:T(512)} %copy-done.4, s32[448]{0:T(512)} %copy-done.5, s32[112]{0:T(128)} %copy-done.6, s32[2]{0:T(128)} %copy-done.7, bf16[160,128,128]{2,1,0:T(8,128)(2,1)} %tiles_ref.7, bf16[2,4,128,128]{3,2,1,0:T(8,128)(2,1)} %get-tuple-element.69.refs_0_.own_ref, f32[2,64,1024]{2,1,0:T(8,128)} %bitcast.27), custom_call_target="tpu_custom_call" | custom-call | flops 671088640 | bytes 4194304 | tf_op jit(solution)/shard_map/own/pallas_call | solution.py:421
  131.1 3.2 %collective-permute-done.8.refs_3_ = bf16[2,4,128,128]{3,2,1,0:T(8,128)(2,1)} collective-permute-done((bf16[2,4,128,128]{3,2,1,0:T(8,128)(2,1)}, bf16[2,4,128,128]{3,2,1,0:T(8,128)(2,1)}, u32[]{:S(2)}, u32[]{:S(2)}) %collective-permute-start.8) | collective-permute-done | bytes 262176 | tf_op jit(solution)/shard_map/ppermute | solution.py:353
  134.3 3.3 %collective-permute-done.7.refs_2_ = bf16[2,4,128,128]{3,2,1,0:T(8,128)(2,1)} collective-permute-done((bf16[2,4,128,128]{3,2,1,0:T(8,128)(2,1)}, bf16[2,4,128,128]{3,2,1,0:T(8,128)(2,1)}, u32[]{:S(2)}, u32[]{:S(2)}) %collective-permute-start.7) | collective-permute-done | bytes 262176 | tf_op jit(solution)/shard_map/ppermute | solution.py:353
  137.6 1.6 early.1.early_ref
  139.2 32.9 %all-to-all-done.2.got_ref = bf16[64,128,128]{2,1,0:T(8,128)(2,1)} async-done(((bf16[64,128,128]{2,1,0:T(8,128)(2,1)}), bf16[64,128,128]{2,1,0:T(8,128)(2,1)}, u32[]{:S(2)}, u32[]{:S(2)}) %all-to-all-start.2) | async-done | bytes 2097184 | tf_op jit(solution)/shard_map/all_to_all | solution.py:398
  172.1 7.4 %far.3.refs_0_ = bf16[544,128]{1,0:T(8,128)(2,1)} custom-call(s32[448]{0:T(512)} %copy-done.4, s32[448]{0:T(512)} %copy-done.5, s32[112]{0:T(128)} %copy-done.6, s32[2]{0:T(128)} %copy-done.7, bf16[160,128,128]{2,1,0:T(8,128)(2,1)} %tiles_ref.7, bf16[64,128,128]{2,1,0:T(8,128)(2,1)} %all-to-all-done.2.got_ref, f32[4,128,128]{2,1,0:T(8,128)} %own.3.part_ref), custom_call_target="tpu_custom_call" | custom-call | flops 671088640 | bytes 8388608 | tf_op jit(solution)/shard_map/far/pallas_call | solution.py:440
  179.5 3.0 %collective-permute-start.11 = (bf16[544,128]{1,0:T(8,128)(2,1)}, bf16[544,128]{1,0:T(8,128)(2,1)S(1)}, u32[]{:S(2)}, u32[]{:S(2)}) collective-permute-start(bf16[544,128]{1,0:T(8,128)(2,1)} %far.3.refs_0_), channel_id=1, source_target_pairs={{0,3},{1,0},{2,1},{3,2},{4,7},{5,4},{6,5},{7,6},{8,11},{9,8},{10,9... | collective-permute-start | bytes 417800 | tf_op jit(solution)/shard_map/ppermute | solution.py:353
  182.6 1.3 collective-permute-start.9
  183.8 1.1 collective-permute-done.11.refs_3_
  184.9 5.7 %collective-permute-done.10.refs_2_ = bf16[544,128]{1,0:T(8,128)(2,1)S(1)} collective-permute-done((bf16[544,128]{1,0:T(8,128)(2,1)}, bf16[544,128]{1,0:T(8,128)(2,1)S(1)}, u32[]{:S(2)}, u32[]{:S(2)}) %collective-permute-start.10) | collective-permute-done | bytes 139296 | tf_op jit(solution)/shard_map/ppermute | solution.py:353
  191.5 1.2 final.1
  (75 shorter events, 11.8 us)
Async XLA Ops:
  0.0 124.6 %copy-start = (bf16[3,256,256]{2,1,0:T(8,128)(2,1)S(1)}, bf16[3,256,256]{2,1,0:T(8,128)(2,1)}, u32[]{:S(2)}) copy-start(bf16[3,256,256]{2,1,0:T(8,128)(2,1)} %param.15) | copy-start | bytes 1179652
  0.0 23.1 %copy-start.11 = (s32[1,160]{1,0:T(1,128)S(1)}, s32[1,160]{1,0:T(1,128)}, u32[]{:S(2)}) copy-start(s32[1,160]{1,0:T(1,128)} %param.11) | copy-start | bytes 1924
  0.0 23.1 %copy-start.10 = (s32[1,160]{1,0:T(1,128)S(1)}, s32[1,160]{1,0:T(1,128)}, u32[]{:S(2)}) copy-start(s32[1,160]{1,0:T(1,128)} %param.10) | copy-start | bytes 1924
  1.0 0.9 copy-start.3
  2.0 0.7 copy-start.2
  2.6 7.3 %copy-start.9 = (f32[8,128]{1,0:T(8,128)}, f32[8,128]{1,0:T(8,128)S(1)}, u32[]{:S(2)}) copy-start(f32[8,128]{1,0:T(8,128)S(1)} %get-tuple-element.44.refs_0_) | copy-start | bytes 12292
  2.6 5.0 %collective-permute-start.2 = (f32[8,128]{1,0:T(8,128)S(1)}, f32[8,128]{1,0:T(8,128)S(1)}, u32[]{:S(2)}, u32[]{:S(2)}) collective-permute-start(f32[8,128]{1,0:T(8,128)S(1)} %get-tuple-element.44.refs_0_), channel_id=1, source_target_pairs={{0,3},{1,0},{2,1},{3,2},{4,7},{5,4},{6,5},{7,6},{8,11},{9,8},{10,9... | collective-permute-start | bytes 12296 | tf_op jit(solution)/shard_map/ppermute | solution.py:353
  5.9 3.7 %collective-permute-start.1 = (f32[8,128]{1,0:T(8,128)S(1)}, f32[8,128]{1,0:T(8,128)S(1)}, u32[]{:S(2)}, u32[]{:S(2)}) collective-permute-start(f32[8,128]{1,0:T(8,128)S(1)} %get-tuple-element.44.refs_0_), channel_id=1, source_target_pairs={{0,1},{1,2},{2,3},{3,0},{4,5},{5,6},{6,7},{7,4},{8,9},{9,10},{10,1... | collective-permute-start | bytes 12296 | tf_op jit(solution)/shard_map/ppermute | solution.py:353
  5.9 4.0 %collective-permute-start = (f32[8,128]{1,0:T(8,128)S(1)}, f32[8,128]{1,0:T(8,128)S(1)}, u32[]{:S(2)}, u32[]{:S(2)}) collective-permute-start(f32[8,128]{1,0:T(8,128)S(1)} %get-tuple-element.44.refs_0_), channel_id=1, source_target_pairs={{0,2},{1,3},{2,0},{3,1},{4,6},{5,7},{6,4},{7,5},{8,10},{9,11},{10,... | collective-permute-start | bytes 12296 | tf_op jit(solution)/shard_map/ppermute | solution.py:353
  7.7 2.2 %copy-start.16 = (f32[8,128]{1,0:T(8,128)}, f32[8,128]{1,0:T(8,128)S(1)}, u32[]{:S(2)}) copy-start(f32[8,128]{1,0:T(8,128)S(1)} %collective-permute-done.2.refs_3_) | copy-start | bytes 12292
  9.6 0.6 copy-start.17
  10.2 0.6 copy-start.18
  13.8 35.8 %all-to-all-start = ((bf16[8,4,128,128]{3,2,1,0:T(8,128)(2,1)}), bf16[8,4,128,128]{3,2,1,0:T(8,128)(2,1)S(1)}, u32[]{:S(2)}, u32[]{:S(2)}) async-start(bf16[8,4,128,128]{3,2,1,0:T(8,128)(2,1)} %get-tuple-element.61), calls=%async_computation | async-start | bytes 2097152 | tf_op jit(solution)/shard_map/all_to_all | solution.py:406
  23.1 26.5 %copy-start.8 = (s32[3]{0:T(128)}, s32[3]{0:T(128)S(1)}, u32[]{:S(2)}) copy-start(s32[3]{0:T(128)S(1)} %pad_add_fusion.me_ref) | copy-start | bytes 40
  30.7 0.6 copy-start.4
  31.2 0.6 copy-start.5
  49.5 1.0 copy-start.12
  53.6 37.0 %all-to-all-start.1 = ((bf16[64,128,128]{2,1,0:T(8,128)(2,1)}), bf16[64,128,128]{2,1,0:T(8,128)(2,1)}, u32[]{:S(2)}, u32[]{:S(2)}) async-start(bf16[64,128,128]{2,1,0:T(8,128)(2,1)} %pick.1), calls=%async_computation.1 | async-start | bytes 4194304 | tf_op jit(solution)/shard_map/all_to_all | solution.py:417
  98.0 3.8 %collective-permute-start.5 = (f32[8,128]{1,0:T(8,128)}, f32[8,128]{1,0:T(8,128)S(1)}, u32[]{:S(2)}, u32[]{:S(2)}) collective-permute-start(f32[8,128]{1,0:T(8,128)} %get-tuple-element.68.refs_0_), channel_id=1, source_target_pairs={{0,3},{1,0},{2,1},{3,2},{4,7},{5,4},{6,5},{7,6},{8,11},{9,8},{10,9... | collective-permute-start | bytes 12296 | tf_op jit(solution)/shard_map/ppermute | solution.py:353
  100.5 3.9 %collective-permute-start.4 = (f32[8,128]{1,0:T(8,128)}, f32[8,128]{1,0:T(8,128)S(1)}, u32[]{:S(2)}, u32[]{:S(2)}) collective-permute-start(f32[8,128]{1,0:T(8,128)} %get-tuple-element.68.refs_0_), channel_id=1, source_target_pairs={{0,1},{1,2},{2,3},{3,0},{4,5},{5,6},{6,7},{7,4},{8,9},{9,10},{10,1... | collective-permute-start | bytes 12296 | tf_op jit(solution)/shard_map/ppermute | solution.py:353
  100.5 4.2 %collective-permute-start.3 = (f32[8,128]{1,0:T(8,128)}, f32[8,128]{1,0:T(8,128)S(1)}, u32[]{:S(2)}, u32[]{:S(2)}) collective-permute-start(f32[8,128]{1,0:T(8,128)} %get-tuple-element.68.refs_0_), channel_id=1, source_target_pairs={{0,2},{1,3},{2,0},{3,1},{4,6},{5,7},{6,4},{7,5},{8,10},{9,11},{10,... | collective-permute-start | bytes 12296 | tf_op jit(solution)/shard_map/ppermute | solution.py:353
  101.8 2.9 %copy-start.13 = (f32[8,128]{1,0:T(8,128)}, f32[8,128]{1,0:T(8,128)S(1)}, u32[]{:S(2)}) copy-start(f32[8,128]{1,0:T(8,128)S(1)} %collective-permute-done.5.refs_3_) | copy-start | bytes 12292
  104.4 0.6 copy-start.14
  104.7 0.6 copy-start.15
  109.1 62.9 %all-to-all-start.2 = ((bf16[64,128,128]{2,1,0:T(8,128)(2,1)}), bf16[64,128,128]{2,1,0:T(8,128)(2,1)}, u32[]{:S(2)}, u32[]{:S(2)}) async-start(bf16[64,128,128]{2,1,0:T(8,128)(2,1)} %get-tuple-element.71), calls=%async_computation.2 | async-start | bytes 4194304 | tf_op jit(solution)/shard_map/all_to_all | solution.py:398
  120.3 14.0 %collective-permute-start.8 = (bf16[2,4,128,128]{3,2,1,0:T(8,128)(2,1)}, bf16[2,4,128,128]{3,2,1,0:T(8,128)(2,1)}, u32[]{:S(2)}, u32[]{:S(2)}) collective-permute-start(bf16[2,4,128,128]{3,2,1,0:T(8,128)(2,1)} %get-tuple-element.69.refs_0_.own_ref), channel_id=1, source_target_pairs={{0,3},{1,0},{2,1},{3,2},{4,7},{5,4},{6,5},{7,6},{8,11},{9,8},{10,9... | collective-permute-start | bytes 786440 | tf_op jit(solution)/shard_map/ppermute | solution.py:353
  123.4 14.2 %collective-permute-start.7 = (bf16[2,4,128,128]{3,2,1,0:T(8,128)(2,1)}, bf16[2,4,128,128]{3,2,1,0:T(8,128)(2,1)}, u32[]{:S(2)}, u32[]{:S(2)}) collective-permute-start(bf16[2,4,128,128]{3,2,1,0:T(8,128)(2,1)} %get-tuple-element.69.refs_0_.own_ref), channel_id=1, source_target_pairs={{0,1},{1,2},{2,3},{3,0},{4,5},{5,6},{6,7},{7,4},{8,9},{9,10},{10,1... | collective-permute-start | bytes 786440 | tf_op jit(solution)/shard_map/ppermute | solution.py:353
  123.4 14.2 %collective-permute-start.6 = (bf16[2,4,128,128]{3,2,1,0:T(8,128)(2,1)}, bf16[2,4,128,128]{3,2,1,0:T(8,128)(2,1)}, u32[]{:S(2)}, u32[]{:S(2)}) collective-permute-start(bf16[2,4,128,128]{3,2,1,0:T(8,128)(2,1)} %get-tuple-element.69.refs_0_.own_ref), channel_id=1, source_target_pairs={{0,2},{1,3},{2,0},{3,1},{4,6},{5,7},{6,4},{7,5},{8,10},{9,11},{10,... | collective-permute-start | bytes 786440 | tf_op jit(solution)/shard_map/ppermute | solution.py:353
  179.5 5.4 %collective-permute-start.11 = (bf16[544,128]{1,0:T(8,128)(2,1)}, bf16[544,128]{1,0:T(8,128)(2,1)S(1)}, u32[]{:S(2)}, u32[]{:S(2)}) collective-permute-start(bf16[544,128]{1,0:T(8,128)(2,1)} %far.3.refs_0_), channel_id=1, source_target_pairs={{0,3},{1,0},{2,1},{3,2},{4,7},{5,4},{6,5},{7,6},{8,11},{9,8},{10,9... | collective-permute-start | bytes 417800 | tf_op jit(solution)/shard_map/ppermute | solution.py:353
  182.5 8.0 %collective-permute-start.10 = (bf16[544,128]{1,0:T(8,128)(2,1)}, bf16[544,128]{1,0:T(8,128)(2,1)S(1)}, u32[]{:S(2)}, u32[]{:S(2)}) collective-permute-start(bf16[544,128]{1,0:T(8,128)(2,1)} %far.3.refs_0_), channel_id=1, source_target_pairs={{0,1},{1,2},{2,3},{3,0},{4,5},{5,6},{6,7},{7,4},{8,9},{9,10},{10,1... | collective-permute-start | bytes 417800 | tf_op jit(solution)/shard_map/ppermute | solution.py:353
  182.6 8.0 %collective-permute-start.9 = (bf16[544,128]{1,0:T(8,128)(2,1)}, bf16[544,128]{1,0:T(8,128)(2,1)S(1)}, u32[]{:S(2)}, u32[]{:S(2)}) collective-permute-start(bf16[544,128]{1,0:T(8,128)(2,1)} %far.3.refs_0_), channel_id=1, source_target_pairs={{0,2},{1,3},{2,0},{3,1},{4,6},{5,7},{6,4},{7,5},{8,10},{9,11},{10,... | collective-permute-start | bytes 417800 | tf_op jit(solution)/shard_map/ppermute | solution.py:353
  190.6 0.9 copy-start.1
  (2 other events, 1.0 us)

commit v6 on v5

--- a/solution.py
+++ b/solution.py
@@ -22,7 +22,7 @@
 SLOTS = MAXG * GROUP
 SHIFTS = (0, 2, 1, 3)
 N_ROW = NY * NZ * NC
-BATCH = 8
+ZSHIFTS = (0, 4, 3, 5, 2, 6, 1, 7)
 DEPTH = 4
 FULL = 63 << 20
 MOST = 65_000_000
@@ -115,21 +115,20 @@
         copy.wait()
 
 
-def write_slabs(me_ref, idx_ref, slots, out_ref, buf, sem):
-    mask = lane_low((BLK, BLK))
-    mine = (me_ref[0] * NC + me_ref[2]) * NZ + me_ref[1]
+def write_slabs(me_ref, slab_of, out_ref, buf, sem):
+    mine = me_ref[0] * NC + me_ref[2]
     copies = []
-    for part in range(N_ROW // BATCH):
-        for j in range(BATCH):
-            i = part * BATCH + j
-            buf[i] = jnp.where(mask, slots[idx_ref[2 * i]], slots[idx_ref[2 * i + 1]])
-
-        @pl.when(mine // BATCH == part)
+    for dest in range(NY * NC):
+        for j in range(NZ):
+            z, slab = slab_of(dest, j)
+            buf[dest * NZ + z] = slab
+
+        @pl.when(mine == dest)
         def _():
-            buf[mine] = jnp.zeros((BLK, BLK), bf16)
+            buf[dest * NZ + me_ref[1]] = jnp.zeros((BLK, BLK), bf16)
 
         copy = pltpu.make_async_copy(
-            buf.at[pl.ds(part * BATCH, BATCH)], out_ref.at[pl.ds(part * BATCH, BATCH)], sem.at[part]
+            buf.at[pl.ds(dest * NZ, NZ)], out_ref.at[pl.ds(dest * NZ, NZ)], sem.at[dest]
         )
         copy.start()
         copies.append(copy)
@@ -143,10 +142,17 @@
             v = z_ref[z, p]
             slots[z * BPD + p] = v
             slots[z * BPD + PAIRS + p] = swapped(v)
-    write_slabs(me_ref, idx_ref, slots, out_ref, buf, sem)
-
-
-def send_kernel(me_ref, idx_ref, raw_ref, *refs):
+    mask = lane_low((BLK, BLK))
+
+    def slab_of(dest, j):
+        i = 2 * (dest * NZ + j)
+        return j, jnp.where(mask, slots[idx_ref[i]], slots[idx_ref[i + 1]])
+
+    write_slabs(me_ref, slab_of, out_ref, buf, sem)
+
+
+def send_kernel(me_ref, *refs):
+    asked_refs, raw_ref, refs = refs[:NZ], refs[NZ], refs[NZ + 1 :]
     before_ref, out_ref, own_ref, slots, buf, sem = refs[NX:]
     columns = row_scale(total_of(refs[:NX]))
     own_ref[0] = before_ref[0]
@@ -155,7 +161,18 @@
         own_ref[1, p] = v
         slots[p] = v
         slots[PAIRS + p] = swapped(v)
-    write_slabs(me_ref, idx_ref, slots, out_ref, buf, sem)
+    mask = lane_low((BLK, BLK))
+    at = ((me_ref[0] * NZ + me_ref[1]) * NC + me_ref[2]) * 2
+
+    def slab_of(dest, j):
+        z = (me_ref[1] + NZ - ZSHIFTS[j]) & (NZ - 1)
+        first = asked_refs[j][dest, at]
+        second = asked_refs[j][dest, at + 1]
+        low = (first >> 1) | ((first & 1) << 2)
+        high = ((second >> 1) | ((second & 1) << 2)) ^ PAIRS
+        return z, jnp.where(mask, slots[low], slots[high])
+
+    write_slabs(me_ref, slab_of, out_ref, buf, sem)
 
 
 def order_kernel(me_ref, rows_ref, srcs_ref, count_ref, tile_ref, slab_ref, into_ref, groups_ref, fill, begin):
@@ -370,7 +387,7 @@
         [((PAIRS, BLK, BLK), bf16, VMEM), ((BPD, BLK), f32, VMEM)],
     )(features.T)
     packed, squares, rows, srcs, count, enc_weight, needed = lax.optimization_barrier(
-        (packed, squares, tile_rows.reshape(-1), tile_srcs.reshape(-1), tile_count, enc_weight, needed.reshape(-1))
+        (packed, squares, tile_rows.reshape(-1), tile_srcs.reshape(-1), tile_count, enc_weight, needed)
     )
 
     weights = lax.dynamic_slice_in_dim(enc_weight, x_index * WIDTH, WIDTH, axis=2).reshape(HOPS + 1, NX, WIDTH, WIDTH)
@@ -390,10 +407,10 @@
         wide = [((N_ROW, BLK, BLK), bf16, HBM)]
         if last:
             picked, owned = call(
-                send_kernel, "send", [whole(SMEM)] * 2 + [whole()] * (2 + NX), wide + [((2, PAIRS, BLK, BLK), bf16, VMEM)],
-                [VMEM((BPD, BLK, BLK), bf16), VMEM((N_ROW, BLK, BLK), bf16), DMA((N_ROW // BATCH,))],
+                send_kernel, "send", [whole(SMEM)] * (1 + NZ) + [whole()] * (2 + NX), wide + [((2, PAIRS, BLK, BLK), bf16, VMEM)],
+                [VMEM((BPD, BLK, BLK), bf16), VMEM((N_ROW, BLK, BLK), bf16), DMA((NY * NC,))],
                 limit=MOST,
-            )(me, table, packed, *totals, owned)
+            )(me, *tables, packed, *totals, owned)
             spread = [owned] + [shift_by(owned, "x", shift) for shift in SHIFTS[1:]]
             got = lax.all_to_all(picked, ("y", "core", "z"), 0, 0, tiled=True)
         else:
@@ -405,18 +422,17 @@
             )(packed, *totals)
             along = lax.all_to_all(packed, "z", 0, 0, tiled=True)
             needed, owned = lax.optimization_barrier((needed, owned))
-            asked = lax.all_gather(needed, ("y", "core"), axis=0)
+            asked = lax.all_gather(needed.reshape(-1), ("y", "core"), axis=0)
             table = slot_table(asked.reshape(NY * NC, NY, NZ, NC, 2), (me[0], 0, me[2]), jnp.arange(NZ, dtype=jnp.int32) * BPD)
             at, table, asked, *lists = lax.optimization_barrier((me, table, asked, *lists))
             picked = call(
                 pick_kernel, "pick", [whole(SMEM)] * 2 + [whole()], wide,
-                [VMEM((NZ * BPD, BLK, BLK), bf16), VMEM((N_ROW, BLK, BLK), bf16), DMA((N_ROW // BATCH,))],
+                [VMEM((NZ * BPD, BLK, BLK), bf16), VMEM((N_ROW, BLK, BLK), bf16), DMA((NY * NC,))],
                 limit=MOST,
             )(at, table, along)
             picked, asked = lax.optimization_barrier((picked, asked))
             got = lax.all_to_all(picked, ("y", "core"), 0, 0, tiled=True)
-            everyone = lax.all_gather(asked, "z", axis=1).reshape(NY * NC * NZ, NY, NZ, NC, 2)
-            table = slot_table(everyone, (me[0], me[1], me[2]), jnp.zeros((1,), jnp.int32))
+            tables = [asked] + [shift_by(asked, "z", shift) for shift in ZSHIFTS[1:]]
         ring = [VMEM((DEPTH, STEP * GROUP, BLK, BLK), bf16), DMA((DEPTH, STEP * GROUP))]
         part = call(
             functools.partial(own_kernel, hop), "own", [whole(SMEM)] * 4 + [whole(HBM), whole(), whole(HBM)],
@@ -425,7 +441,7 @@
             limit=FULL, flops=TPD * 2 * BLK**3, moved=4 << 20,
         )(*lists, tile_vals, owned, noise)
         if not last:
-            part, table = lax.optimization_barrier((part, table))
+            part, *tables = lax.optimization_barrier((part, *tables))
         if last:
             early = call(
                 early_kernel, "early", [whole(SMEM)] + [whole()] * (1 + NX), [((PAIRS, BLK, BLK), f32, VMEM)]

time: 195 us -> 185 us (0.949)
  waiting for transfers between devices: 57.3 us -> 70.1 us
  blocking collectives: 29.3 us -> 16.8 us
  Pallas kernels: 47.5 us -> 36.7 us
  starting transfers between devices: 43.4 us -> 49.8 us
  local copies, waits for them, and re-layouts: 12.8 us -> 8.8 us
    all_to_all x1, waiting for transfers between devices: 0.01 us -> 12.7 us  [shards(): got = lax.all_to_all(picked, ('y', 'core'), 0, 0, tiled=True)]
    all_gather x2 -> x1, blocking collectives: 29.3 us -> 16.8 us  [shards(): asked = lax.all_gather(needed.reshape(-1), ('y', 'core'), axis=0)]
    ppermute x12 -> x19, starting transfers between devices: 17.4 us -> 27 us  [shift_by(): lax.ppermute(value, axis, [(i, (i + shift) % size) for i in range(size)])]
    pallas_call x2, Pallas kernels: 12.3 us -> 7.97 us  [shards(): call(functools.partial(own_kernel, hop), 'own', [whole(SMEM)] * 4 + [whol...]
    all_to_all x1, waiting for transfers between devices: 6.07 us -> 1.96 us  [shards(): along = lax.all_to_all(packed, 'z', 0, 0, tiled=True)]
    pallas_call x1, Pallas kernels: 7.58 us -> 3.78 us  [shards(): call(order_kernel, 'order', [whole(SMEM)] * 4, [((2 * SLOTS,), jnp.int32,...]
    reshape x2 -> x0, local copies, waits for them, and re-layouts: 3.34 us -> none  [the longest x1 3.2 us: shards(): lax.all_gather(asked, 'z', axis=1).reshape(NY * NC * NZ, NY, NZ, NC, 2)]
    all_to_all x1, starting transfers between devices: 11.2 us -> 8.08 us  [shards(): got = lax.all_to_all(picked, ('y', 'core', 'z'), 0, 0, tiled=True)]
  transfers between devices with their start and end apart: 15 -> 22, of which waited for: 10 -> 12; matrix products, arithmetic and copies ran while one was open for 3% -> 1% of each run, Pallas kernels for 11% -> 7%
where the time goes in v6:
time: 185 us; the launch traced here: 184 us
  waiting for transfers between devices  70.1 us (38%)
  starting transfers between devices  49.8 us (27%)
  Pallas kernels  36.7 us (20%)
  blocking collectives  16.8 us (9%)
  local copies, waits for them, and re-layouts  8.8 us (5%)
    all_to_all x1, waiting for transfers between devices, shards(): got = lax.all_to_all(picked, ('y', 'core', 'z'), 0, 0, tiled=True)  34.1 us
    ppermute x19, starting transfers between devices, shift_by(): lax.ppermute(value, axis, [(i, (i + shift) % size) for i in range(size)])  27 us
    ppermute x19, waiting for transfers between devices, shift_by(): lax.ppermute(value, axis, [(i, (i + shift) % size) for i in range(size)])  21.3 us
    all_gather x1, blocking collectives, shards(): asked = lax.all_gather(needed.reshape(-1), ('y', 'core'), axis=0)  16.8 us
    all_to_all x1, waiting for transfers between devices, shards(): got = lax.all_to_all(picked, ('y', 'core'), 0, 0, tiled=True)  12.7 us
    pallas_call x2, Pallas kernels, shards(): call(functools.partial(far_kernel, hop), 'far', [whole(SMEM)] * 4 + [whol...  11.8 us
    all_to_all x1, starting transfers between devices, shards(): along = lax.all_to_all(packed, 'z', 0, 0, tiled=True)  8.2 us
    all_to_all x1, starting transfers between devices, shards(): got = lax.all_to_all(picked, ('y', 'core', 'z'), 0, 0, tiled=True)  8.08 us
  transfers between devices with their start and end apart: 22, of which 12 were waited for; matrix products, arithmetic and copies ran while one was open for 1% of the time, Pallas kernels for 7%

profile of v6, /device:TPU:1, one launch (start us, length us, event | category | flops | bytes accessed | tf_op | source)
XLA Modules:
  0.0 184.0 jit_solution(15748825882574996418)
XLA Ops:
  1.7 3.3 %collective-permute-start.2 = (f32[8,128]{1,0:T(8,128)S(1)}, f32[8,128]{1,0:T(8,128)S(1)}, u32[]{:S(2)}, u32[]{:S(2)}) collective-permute-start(f32[8,128]{1,0:T(8,128)S(1)} %get-tuple-element.51.refs_0_), channel_id=1, source_target_pairs={{0,3},{1,0},{2,1},{3,2},{4,7},{5,4},{6,5},{7,6},{8,11},{9,8},{10,9... | collective-permute-start | bytes 12296 | tf_op jit(solution)/shard_map/ppermute | solution.py:370
  5.0 1.7 collective-permute-start
  6.8 1.9 %collective-permute-done.1.refs_2_ = f32[8,128]{1,0:T(8,128)S(1)} collective-permute-done((f32[8,128]{1,0:T(8,128)S(1)}, f32[8,128]{1,0:T(8,128)S(1)}, u32[]{:S(2)}, u32[]{:S(2)}) %collective-permute-start.1) | collective-permute-done | bytes 4128 | tf_op jit(solution)/shard_map/ppermute | solution.py:370
  9.9 3.0 %norm.1 = (bf16[8,4,128,128]{3,2,1,0:T(8,128)(2,1)}, bf16[1,4,128,128]{3,2,1,0:T(8,128)(2,1)}) custom-call(bf16[4,128,128]{2,1,0:T(8,128)(2,1)} %copy-done.2, f32[8,128]{1,0:T(8,128)} %copy-done.9, f32[8,128]{1,0:T(8,128)} %copy-done.26, f32[8,128]{1,0:T(8,128)} %copy-done.25, f32[8,128]{1,0:T(8,128)} %copy-done.24), custom_call_target="tpu_custom_call" | custom-call | flops 1048576 | bytes 1048576 | tf_op jit(solution)/shard_map/norm/pallas_call | solution.py:417
  12.9 8.2 %all-to-all-start = ((bf16[8,4,128,128]{3,2,1,0:T(8,128)(2,1)}), bf16[8,4,128,128]{3,2,1,0:T(8,128)(2,1)S(1)}, u32[]{:S(2)}, u32[]{:S(2)}) async-start(bf16[8,4,128,128]{3,2,1,0:T(8,128)(2,1)} %get-tuple-element.68), calls=%async_computation | async-start | bytes 2097152 | tf_op jit(solution)/shard_map/all_to_all | solution.py:423
  22.2 3.8 %order.1 = (s32[448]{0:T(512)S(1)}, s32[448]{0:T(512)S(1)}, s32[112]{0:T(128)S(1)}, s32[2]{0:T(128)S(1)}) custom-call(s32[3]{0:T(128)S(1)} %pad_add_fusion.me_ref, s32[160]{0:T(256)S(1)} %bitcast.21, s32[160]{0:T(256)S(1)} %bitcast.22, s32[1]{0:T(128)S(6)} %copy.27.count_ref), custom_call_target="tpu_custom_call" | custom-call | flops 1048576 | bytes 1048576 | tf_op jit(solution)/shard_map/order/pallas_call | solution.py:398
  28.6 16.8 %all-gather = s32[8,1,128]{2,1,0:T(1,128)S(1)} all-gather(s32[1,1,128]{2,1,0:T(1,128)S(1)} %reshape.33), channel_id=1, replica_groups=mesh['y'=4,'z'=8,'core'=2,'x'=4] {'y','core'}, dimensions={0}, use_global_device_ids=true | all-gather | bytes 4608 | tf_op jit(solution)/shard_map/all_gather | solution.py:425
  46.7 2.0 %all-to-all-done.z_ref = bf16[8,4,128,128]{3,2,1,0:T(8,128)(2,1)S(1)} async-done(((bf16[8,4,128,128]{3,2,1,0:T(8,128)(2,1)}), bf16[8,4,128,128]{3,2,1,0:T(8,128)(2,1)S(1)}, u32[]{:S(2)}, u32[]{:S(2)}) %all-to-all-start) | async-done | bytes 1048608 | tf_op jit(solution)/shard_map/all_to_all | solution.py:423
  49.7 3.2 %pick.1 = bf16[64,128,128]{2,1,0:T(8,128)(2,1)} custom-call(s32[3]{0:T(128)} %copy-done.8, s32[128]{0:T(128)} %multiply_add_fusion.idx_ref, bf16[8,4,128,128]{3,2,1,0:T(8,128)(2,1)} %copy-done.12), custom_call_target="tpu_custom_call" | custom-call | flops 1048576 | bytes 1048576 | tf_op jit(solution)/shard_map/pick/pallas_call | solution.py:428
  52.9 6.6 %all-to-all-start.1 = ((bf16[64,128,128]{2,1,0:T(8,128)(2,1)}), bf16[64,128,128]{2,1,0:T(8,128)(2,1)}, u32[]{:S(2)}, u32[]{:S(2)}) async-start(bf16[64,128,128]{2,1,0:T(8,128)(2,1)} %pick.1), calls=%async_computation.1 | async-start | bytes 4194304 | tf_op jit(solution)/shard_map/all_to_all | solution.py:434
  59.5 1.5 collective-permute-start.8
  60.9 2.4 %collective-permute-start.6 = (s32[8,128]{1,0:T(8,128)S(1)}, s32[8,128]{1,0:T(8,128)S(1)}, u32[]{:S(2)}, u32[]{:S(2)}) collective-permute-start(s32[8,128]{1,0:T(8,128)S(1)} %bitcast.30), channel_id=1, source_target_pairs={{0,16},{8,24},{16,32},{24,40},{32,48},{40,56},{48,0},{56,8},{1,17}... | collective-permute-start | bytes 12296 | tf_op jit(solution)/shard_map/ppermute | solution.py:370
  63.3 1.4 collective-permute-start.5
  64.7 1.9 %collective-permute-start.4 = (s32[8,128]{1,0:T(8,128)S(1)}, s32[8,128]{1,0:T(8,128)S(1)}, u32[]{:S(2)}, u32[]{:S(2)}) collective-permute-start(s32[8,128]{1,0:T(8,128)S(1)} %bitcast.32), channel_id=1, source_target_pairs={{0,24},{8,32},{16,40},{24,48},{32,56},{40,0},{48,8},{56,16},{1,25}... | collective-permute-start | bytes 12296 | tf_op jit(solution)/shard_map/ppermute | solution.py:370
  66.6 2.3 %collective-permute-start.3 = (s32[8,128]{1,0:T(8,128)S(1)}, s32[8,128]{1,0:T(8,128)S(1)}, u32[]{:S(2)}, u32[]{:S(2)}) collective-permute-start(s32[8,128]{1,0:T(8,128)S(1)} %bitcast.33), channel_id=1, source_target_pairs={{0,32},{8,40},{16,48},{24,56},{32,0},{40,8},{48,16},{56,24},{1,33}... | collective-permute-start | bytes 12296 | tf_op jit(solution)/shard_map/ppermute | solution.py:370
  68.9 4.0 %own.2.part_ref = f32[4,128,128]{2,1,0:T(8,128)} custom-call(s32[448]{0:T(512)} %copy-done.4, s32[448]{0:T(512)} %copy-done.5, s32[112]{0:T(128)} %copy-done.6, s32[2]{0:T(128)} %copy-done.7, bf16[160,128,128]{2,1,0:T(8,128)(2,1)} %tiles_ref.7, bf16[1,4,128,128]{3,2,1,0:T(8,128)(2,1)} %get-tuple-element.65.own_ref.refs_13_, f32[2,64,1024]{2,1,0:T(8,128)} %bitcast.23), custom_call_target="tpu_custom_call" | custom-call | flops 671088640 | bytes 4194304 | tf_op jit(solution)/shard_map/own/pallas_call | solution.py:437
  73.0 12.7 %all-to-all-done.1.got_ref = bf16[64,128,128]{2,1,0:T(8,128)(2,1)} async-done(((bf16[64,128,128]{2,1,0:T(8,128)(2,1)}), bf16[64,128,128]{2,1,0:T(8,128)(2,1)}, u32[]{:S(2)}, u32[]{:S(2)}) %all-to-all-start.1) | async-done | bytes 2097184 | tf_op jit(solution)/shard_map/all_to_all | solution.py:434
  85.8 5.9 %far.2 = (f32[4,128,128]{2,1,0:T(8,128)}, f32[8,128]{1,0:T(8,128)}) custom-call(s32[448]{0:T(512)} %copy-done.4, s32[448]{0:T(512)} %copy-done.5, s32[112]{0:T(128)} %copy-done.6, s32[2]{0:T(128)} %copy-done.7, bf16[160,128,128]{2,1,0:T(8,128)(2,1)} %tiles_ref.7, bf16[64,128,128]{2,1,0:T(8,128)(2,1)} %all-to-all-done.1.got_ref, f32[4,128,128]{2,1,0:T(8,128)} %own.2.part_ref), custom_call_target="tpu_custom_call" | custom-call | flops 671088640 | bytes 8388608 | tf_op jit(solution)/shard_map/far/pallas_call | solution.py:456
  91.7 2.7 %collective-permute-start.12 = (f32[8,128]{1,0:T(8,128)}, f32[8,128]{1,0:T(8,128)S(1)}, u32[]{:S(2)}, u32[]{:S(2)}) collective-permute-start(f32[8,128]{1,0:T(8,128)} %get-tuple-element.82.refs_9_), channel_id=1, source_target_pairs={{0,3},{1,0},{2,1},{3,2},{4,7},{5,4},{6,5},{7,6},{8,11},{9,8},{10,9... | collective-permute-start | bytes 12296 | tf_op jit(solution)/shard_map/ppermute | solution.py:370
  95.6 2.6 %collective-permute-done.11.refs_11_ = f32[8,128]{1,0:T(8,128)S(1)} collective-permute-done((f32[8,128]{1,0:T(8,128)}, f32[8,128]{1,0:T(8,128)S(1)}, u32[]{:S(2)}, u32[]{:S(2)}) %collective-permute-start.11) | collective-permute-done | bytes 4128 | tf_op jit(solution)/shard_map/ppermute | solution.py:370
  99.1 4.1 %send.1 = (bf16[64,128,128]{2,1,0:T(8,128)(2,1)}, bf16[2,4,128,128]{3,2,1,0:T(8,128)(2,1)}) custom-call(s32[3]{0:T(128)} %copy-done.8, s32[8,128]{1,0:T(8,128)} %bitcast.34, s32[8,128]{1,0:T(8,128)} %copy-done.20, s32[8,128]{1,0:T(8,128)} %copy-done.19, s32[8,128]{1,0:T(8,128)} %copy-done.18, s32[8,128]{1,0:T(8,128)} %copy-done.17, s32[8,128]{1,0:T(8,128)} %copy-done.16, ...), custom_call_target="tpu_custom_call" | custom-call | flops 1048576 | bytes 1048576 | tf_op jit(solution)/shard_map/send/pallas_call | solution.py:409
  103.2 8.1 %all-to-all-start.2 = ((bf16[64,128,128]{2,1,0:T(8,128)(2,1)}), bf16[64,128,128]{2,1,0:T(8,128)(2,1)}, u32[]{:S(2)}, u32[]{:S(2)}) async-start(bf16[64,128,128]{2,1,0:T(8,128)(2,1)} %get-tuple-element.85), calls=%async_computation.2 | async-start | bytes 4194304 | tf_op jit(solution)/shard_map/all_to_all | solution.py:415
  111.3 3.0 %collective-permute-start.15 = (bf16[2,4,128,128]{3,2,1,0:T(8,128)(2,1)}, bf16[2,4,128,128]{3,2,1,0:T(8,128)(2,1)}, u32[]{:S(2)}, u32[]{:S(2)}) collective-permute-start(bf16[2,4,128,128]{3,2,1,0:T(8,128)(2,1)} %get-tuple-element.83.refs_0_.own_ref), channel_id=1, source_target_pairs={{0,3},{1,0},{2,1},{3,2},{4,7},{5,4},{6,5},{7,6},{8,11},{9,8},{10,9... | collective-permute-start | bytes 786440 | tf_op jit(solution)/shard_map/ppermute | solution.py:370
  115.9 4.0 %own.3.part_ref = f32[4,128,128]{2,1,0:T(8,128)} custom-call(s32[448]{0:T(512)} %copy-done.4, s32[448]{0:T(512)} %copy-done.5, s32[112]{0:T(128)} %copy-done.6, s32[2]{0:T(128)} %copy-done.7, bf16[160,128,128]{2,1,0:T(8,128)(2,1)} %tiles_ref.7, bf16[2,4,128,128]{3,2,1,0:T(8,128)(2,1)} %get-tuple-element.83.refs_0_.own_ref, f32[2,64,1024]{2,1,0:T(8,128)} %bitcast.24), custom_call_target="tpu_custom_call" | custom-call | flops 671088640 | bytes 4194304 | tf_op jit(solution)/shard_map/own/pallas_call | solution.py:437
  119.9 5.3 %collective-permute-done.15.refs_3_ = bf16[2,4,128,128]{3,2,1,0:T(8,128)(2,1)} collective-permute-done((bf16[2,4,128,128]{3,2,1,0:T(8,128)(2,1)}, bf16[2,4,128,128]{3,2,1,0:T(8,128)(2,1)}, u32[]{:S(2)}, u32[]{:S(2)}) %collective-permute-start.15) | collective-permute-done | bytes 262176 | tf_op jit(solution)/shard_map/ppermute | solution.py:370
  125.2 2.2 %collective-permute-done.13.refs_1_ = bf16[2,4,128,128]{3,2,1,0:T(8,128)(2,1)} collective-permute-done((bf16[2,4,128,128]{3,2,1,0:T(8,128)(2,1)}, bf16[2,4,128,128]{3,2,1,0:T(8,128)(2,1)}, u32[]{:S(2)}, u32[]{:S(2)}) %collective-permute-start.13) | collective-permute-done | bytes 262176 | tf_op jit(solution)/shard_map/ppermute | solution.py:370
  127.4 1.6 early.1.early_ref
  129.0 34.1 %all-to-all-done.2.got_ref = bf16[64,128,128]{2,1,0:T(8,128)(2,1)} async-done(((bf16[64,128,128]{2,1,0:T(8,128)(2,1)}), bf16[64,128,128]{2,1,0:T(8,128)(2,1)}, u32[]{:S(2)}, u32[]{:S(2)}) %all-to-all-start.2) | async-done | bytes 2097184 | tf_op jit(solution)/shard_map/all_to_all | solution.py:415
  163.1 5.9 %far.3.refs_0_ = bf16[544,128]{1,0:T(8,128)(2,1)} custom-call(s32[448]{0:T(512)} %copy-done.4, s32[448]{0:T(512)} %copy-done.5, s32[112]{0:T(128)} %copy-done.6, s32[2]{0:T(128)} %copy-done.7, bf16[160,128,128]{2,1,0:T(8,128)(2,1)} %tiles_ref.7, bf16[64,128,128]{2,1,0:T(8,128)(2,1)} %all-to-all-done.2.got_ref, f32[4,128,128]{2,1,0:T(8,128)} %own.3.part_ref), custom_call_target="tpu_custom_call" | custom-call | flops 671088640 | bytes 8388608 | tf_op jit(solution)/shard_map/far/pallas_call | solution.py:456
  169.0 3.0 %collective-permute-start.18 = (bf16[544,128]{1,0:T(8,128)(2,1)}, bf16[544,128]{1,0:T(8,128)(2,1)S(1)}, u32[]{:S(2)}, u32[]{:S(2)}) collective-permute-start(bf16[544,128]{1,0:T(8,128)(2,1)} %far.3.refs_0_), channel_id=1, source_target_pairs={{0,3},{1,0},{2,1},{3,2},{4,7},{5,4},{6,5},{7,6},{8,11},{9,8},{10,9... | collective-permute-start | bytes 417800 | tf_op jit(solution)/shard_map/ppermute | solution.py:370
  173.3 2.5 %collective-permute-done.18.refs_3_ = bf16[544,128]{1,0:T(8,128)(2,1)S(1)} collective-permute-done((bf16[544,128]{1,0:T(8,128)(2,1)}, bf16[544,128]{1,0:T(8,128)(2,1)S(1)}, u32[]{:S(2)}, u32[]{:S(2)}) %collective-permute-start.18) | collective-permute-done | bytes 139296 | tf_op jit(solution)/shard_map/ppermute | solution.py:370
  175.9 6.0 %collective-permute-done.17.refs_2_ = bf16[544,128]{1,0:T(8,128)(2,1)S(1)} collective-permute-done((bf16[544,128]{1,0:T(8,128)(2,1)}, bf16[544,128]{1,0:T(8,128)(2,1)S(1)}, u32[]{:S(2)}, u32[]{:S(2)}) %collective-permute-start.17) | collective-permute-done | bytes 139296 | tf_op jit(solution)/shard_map/ppermute | solution.py:370
  (99 shorter events, 15.4 us)
Async XLA Ops:
  0.0 115.6 %copy-start = (bf16[3,256,256]{2,1,0:T(8,128)(2,1)S(1)}, bf16[3,256,256]{2,1,0:T(8,128)(2,1)}, u32[]{:S(2)}) copy-start(bf16[3,256,256]{2,1,0:T(8,128)(2,1)} %param.15) | copy-start | bytes 1179652
  0.0 22.2 %copy-start.10 = (s32[1,160]{1,0:T(1,128)S(1)}, s32[1,160]{1,0:T(1,128)}, u32[]{:S(2)}) copy-start(s32[1,160]{1,0:T(1,128)} %param.10) | copy-start | bytes 1924
  1.0 21.2 %copy-start.11 = (s32[1,160]{1,0:T(1,128)S(1)}, s32[1,160]{1,0:T(1,128)}, u32[]{:S(2)}) copy-start(s32[1,160]{1,0:T(1,128)} %param.11) | copy-start | bytes 1924
  1.0 27.4 %copy-start.27 = (s32[1,64,2]{1,2,0:T(2,128)S(1)}, s32[1,64,2]{1,2,0:T(2,128)}, u32[]{:S(2)}) copy-start(s32[1,64,2]{1,2,0:T(2,128)} %param.13) | copy-start | bytes 1540
  1.7 5.0 %collective-permute-start.2 = (f32[8,128]{1,0:T(8,128)S(1)}, f32[8,128]{1,0:T(8,128)S(1)}, u32[]{:S(2)}, u32[]{:S(2)}) collective-permute-start(f32[8,128]{1,0:T(8,128)S(1)} %get-tuple-element.51.refs_0_), channel_id=1, source_target_pairs={{0,3},{1,0},{2,1},{3,2},{4,7},{5,4},{6,5},{7,6},{8,11},{9,8},{10,9... | collective-permute-start | bytes 12296 | tf_op jit(solution)/shard_map/ppermute | solution.py:370
  5.0 3.7 %collective-permute-start.1 = (f32[8,128]{1,0:T(8,128)S(1)}, f32[8,128]{1,0:T(8,128)S(1)}, u32[]{:S(2)}, u32[]{:S(2)}) collective-permute-start(f32[8,128]{1,0:T(8,128)S(1)} %get-tuple-element.51.refs_0_), channel_id=1, source_target_pairs={{0,1},{1,2},{2,3},{3,0},{4,5},{5,6},{6,7},{7,4},{8,9},{9,10},{10,1... | collective-permute-start | bytes 12296 | tf_op jit(solution)/shard_map/ppermute | solution.py:370
  5.0 4.0 %collective-permute-start = (f32[8,128]{1,0:T(8,128)S(1)}, f32[8,128]{1,0:T(8,128)S(1)}, u32[]{:S(2)}, u32[]{:S(2)}) collective-permute-start(f32[8,128]{1,0:T(8,128)S(1)} %get-tuple-element.51.refs_0_), channel_id=1, source_target_pairs={{0,2},{1,3},{2,0},{3,1},{4,6},{5,7},{6,4},{7,5},{8,10},{9,11},{10,... | collective-permute-start | bytes 12296 | tf_op jit(solution)/shard_map/ppermute | solution.py:370
  12.9 35.8 %all-to-all-start = ((bf16[8,4,128,128]{3,2,1,0:T(8,128)(2,1)}), bf16[8,4,128,128]{3,2,1,0:T(8,128)(2,1)S(1)}, u32[]{:S(2)}, u32[]{:S(2)}) async-start(bf16[8,4,128,128]{3,2,1,0:T(8,128)(2,1)} %get-tuple-element.68), calls=%async_computation | async-start | bytes 2097152 | tf_op jit(solution)/shard_map/all_to_all | solution.py:423
  22.2 26.5 %copy-start.8 = (s32[3]{0:T(128)}, s32[3]{0:T(128)S(1)}, u32[]{:S(2)}) copy-start(s32[3]{0:T(128)S(1)} %pad_add_fusion.me_ref) | copy-start | bytes 40
  45.4 21.2 %copy-start.13 = (s32[8,1,128]{2,1,0:T(1,128)}, s32[8,1,128]{2,1,0:T(1,128)S(1)}, u32[]{:S(2)}) copy-start(s32[8,1,128]{2,1,0:T(1,128)S(1)} %all-gather) | copy-start | bytes 12292
  52.9 32.9 %all-to-all-start.1 = ((bf16[64,128,128]{2,1,0:T(8,128)(2,1)}), bf16[64,128,128]{2,1,0:T(8,128)(2,1)}, u32[]{:S(2)}, u32[]{:S(2)}) async-start(bf16[64,128,128]{2,1,0:T(8,128)(2,1)} %pick.1), calls=%async_computation.1 | async-start | bytes 4194304 | tf_op jit(solution)/shard_map/all_to_all | solution.py:434
  59.5 5.2 %collective-permute-start.9 = (s32[8,128]{1,0:T(8,128)S(1)}, s32[8,128]{1,0:T(8,128)S(1)}, u32[]{:S(2)}, u32[]{:S(2)}) collective-permute-start(s32[8,128]{1,0:T(8,128)S(1)} %bitcast.27), channel_id=1, source_target_pairs={{0,56},{8,0},{16,8},{24,16},{32,24},{40,32},{48,40},{56,48},{1,57}... | collective-permute-start | bytes 12296 | tf_op jit(solution)/shard_map/ppermute | solution.py:370
  59.5 7.1 %collective-permute-start.8 = (s32[8,128]{1,0:T(8,128)S(1)}, s32[8,128]{1,0:T(8,128)S(1)}, u32[]{:S(2)}, u32[]{:S(2)}) collective-permute-start(s32[8,128]{1,0:T(8,128)S(1)} %bitcast.28), channel_id=1, source_target_pairs={{0,8},{8,16},{16,24},{24,32},{32,40},{40,48},{48,56},{56,0},{1,9},... | collective-permute-start | bytes 12296 | tf_op jit(solution)/shard_map/ppermute | solution.py:370
  60.9 11.9 %collective-permute-start.7 = (s32[8,128]{1,0:T(8,128)S(1)}, s32[8,128]{1,0:T(8,128)S(1)}, u32[]{:S(2)}, u32[]{:S(2)}) collective-permute-start(s32[8,128]{1,0:T(8,128)S(1)} %bitcast.29), channel_id=1, source_target_pairs={{0,48},{8,56},{16,0},{24,8},{32,16},{40,24},{48,32},{56,40},{1,49}... | collective-permute-start | bytes 12296 | tf_op jit(solution)/shard_map/ppermute | solution.py:370
  60.9 11.9 %collective-permute-start.6 = (s32[8,128]{1,0:T(8,128)S(1)}, s32[8,128]{1,0:T(8,128)S(1)}, u32[]{:S(2)}, u32[]{:S(2)}) collective-permute-start(s32[8,128]{1,0:T(8,128)S(1)} %bitcast.30), channel_id=1, source_target_pairs={{0,16},{8,24},{16,32},{24,40},{32,48},{40,56},{48,0},{56,8},{1,17}... | collective-permute-start | bytes 12296 | tf_op jit(solution)/shard_map/ppermute | solution.py:370
  63.3 9.6 %collective-permute-start.5 = (s32[8,128]{1,0:T(8,128)S(1)}, s32[8,128]{1,0:T(8,128)S(1)}, u32[]{:S(2)}, u32[]{:S(2)}) collective-permute-start(s32[8,128]{1,0:T(8,128)S(1)} %bitcast.31), channel_id=1, source_target_pairs={{0,40},{8,48},{16,56},{24,0},{32,8},{40,16},{48,24},{56,32},{1,41}... | collective-permute-start | bytes 12296 | tf_op jit(solution)/shard_map/ppermute | solution.py:370
  64.7 8.3 %collective-permute-start.4 = (s32[8,128]{1,0:T(8,128)S(1)}, s32[8,128]{1,0:T(8,128)S(1)}, u32[]{:S(2)}, u32[]{:S(2)}) collective-permute-start(s32[8,128]{1,0:T(8,128)S(1)} %bitcast.32), channel_id=1, source_target_pairs={{0,24},{8,32},{16,40},{24,48},{32,56},{40,0},{48,8},{56,16},{1,25}... | collective-permute-start | bytes 12296 | tf_op jit(solution)/shard_map/ppermute | solution.py:370
  66.6 6.5 %collective-permute-start.3 = (s32[8,128]{1,0:T(8,128)S(1)}, s32[8,128]{1,0:T(8,128)S(1)}, u32[]{:S(2)}, u32[]{:S(2)}) collective-permute-start(s32[8,128]{1,0:T(8,128)S(1)} %bitcast.33), channel_id=1, source_target_pairs={{0,32},{8,40},{16,48},{24,56},{32,0},{40,8},{48,16},{56,24},{1,33}... | collective-permute-start | bytes 12296 | tf_op jit(solution)/shard_map/ppermute | solution.py:370
  72.9 18.8 %copy-start.16 = (s32[8,128]{1,0:T(8,128)}, s32[8,128]{1,0:T(8,128)S(1)}, u32[]{:S(2)}) copy-start(s32[8,128]{1,0:T(8,128)S(1)} %collective-permute-done.7.refs_5_) | copy-start | bytes 12292
  72.9 18.8 %copy-start.17 = (s32[8,128]{1,0:T(8,128)}, s32[8,128]{1,0:T(8,128)S(1)}, u32[]{:S(2)}) copy-start(s32[8,128]{1,0:T(8,128)S(1)} %collective-permute-done.6.refs_4_) | copy-start | bytes 12292
  72.9 18.7 %copy-start.18 = (s32[8,128]{1,0:T(8,128)}, s32[8,128]{1,0:T(8,128)S(1)}, u32[]{:S(2)}) copy-start(s32[8,128]{1,0:T(8,128)S(1)} %collective-permute-done.5.refs_3_) | copy-start | bytes 12292
  72.9 18.7 %copy-start.19 = (s32[8,128]{1,0:T(8,128)}, s32[8,128]{1,0:T(8,128)S(1)}, u32[]{:S(2)}) copy-start(s32[8,128]{1,0:T(8,128)S(1)} %collective-permute-done.4.refs_2_) | copy-start | bytes 12292
  91.7 3.9 %collective-permute-start.12 = (f32[8,128]{1,0:T(8,128)}, f32[8,128]{1,0:T(8,128)S(1)}, u32[]{:S(2)}, u32[]{:S(2)}) collective-permute-start(f32[8,128]{1,0:T(8,128)} %get-tuple-element.82.refs_9_), channel_id=1, source_target_pairs={{0,3},{1,0},{2,1},{3,2},{4,7},{5,4},{6,5},{7,6},{8,11},{9,8},{10,9... | collective-permute-start | bytes 12296 | tf_op jit(solution)/shard_map/ppermute | solution.py:370
  94.3 3.9 %collective-permute-start.11 = (f32[8,128]{1,0:T(8,128)}, f32[8,128]{1,0:T(8,128)S(1)}, u32[]{:S(2)}, u32[]{:S(2)}) collective-permute-start(f32[8,128]{1,0:T(8,128)} %get-tuple-element.82.refs_9_), channel_id=1, source_target_pairs={{0,1},{1,2},{2,3},{3,0},{4,5},{5,6},{6,7},{7,4},{8,9},{9,10},{10,1... | collective-permute-start | bytes 12296 | tf_op jit(solution)/shard_map/ppermute | solution.py:370
  94.3 4.2 %collective-permute-start.10 = (f32[8,128]{1,0:T(8,128)}, f32[8,128]{1,0:T(8,128)S(1)}, u32[]{:S(2)}, u32[]{:S(2)}) collective-permute-start(f32[8,128]{1,0:T(8,128)} %get-tuple-element.82.refs_9_), channel_id=1, source_target_pairs={{0,2},{1,3},{2,0},{3,1},{4,6},{5,7},{6,4},{7,5},{8,10},{9,11},{10,... | collective-permute-start | bytes 12296 | tf_op jit(solution)/shard_map/ppermute | solution.py:370
  103.2 59.9 %all-to-all-start.2 = ((bf16[64,128,128]{2,1,0:T(8,128)(2,1)}), bf16[64,128,128]{2,1,0:T(8,128)(2,1)}, u32[]{:S(2)}, u32[]{:S(2)}) async-start(bf16[64,128,128]{2,1,0:T(8,128)(2,1)} %get-tuple-element.85), calls=%async_computation.2 | async-start | bytes 4194304 | tf_op jit(solution)/shard_map/all_to_all | solution.py:415
  111.3 13.9 %collective-permute-start.15 = (bf16[2,4,128,128]{3,2,1,0:T(8,128)(2,1)}, bf16[2,4,128,128]{3,2,1,0:T(8,128)(2,1)}, u32[]{:S(2)}, u32[]{:S(2)}) collective-permute-start(bf16[2,4,128,128]{3,2,1,0:T(8,128)(2,1)} %get-tuple-element.83.refs_0_.own_ref), channel_id=1, source_target_pairs={{0,3},{1,0},{2,1},{3,2},{4,7},{5,4},{6,5},{7,6},{8,11},{9,8},{10,9... | collective-permute-start | bytes 786440 | tf_op jit(solution)/shard_map/ppermute | solution.py:370
  114.3 10.9 %collective-permute-start.14 = (bf16[2,4,128,128]{3,2,1,0:T(8,128)(2,1)}, bf16[2,4,128,128]{3,2,1,0:T(8,128)(2,1)}, u32[]{:S(2)}, u32[]{:S(2)}) collective-permute-start(bf16[2,4,128,128]{3,2,1,0:T(8,128)(2,1)} %get-tuple-element.83.refs_0_.own_ref), channel_id=1, source_target_pairs={{0,1},{1,2},{2,3},{3,0},{4,5},{5,6},{6,7},{7,4},{8,9},{9,10},{10,1... | collective-permute-start | bytes 786440 | tf_op jit(solution)/shard_map/ppermute | solution.py:370
  114.3 13.1 %collective-permute-start.13 = (bf16[2,4,128,128]{3,2,1,0:T(8,128)(2,1)}, bf16[2,4,128,128]{3,2,1,0:T(8,128)(2,1)}, u32[]{:S(2)}, u32[]{:S(2)}) collective-permute-start(bf16[2,4,128,128]{3,2,1,0:T(8,128)(2,1)} %get-tuple-element.83.refs_0_.own_ref), channel_id=1, source_target_pairs={{0,2},{1,3},{2,0},{3,1},{4,6},{5,7},{6,4},{7,5},{8,10},{9,11},{10,... | collective-permute-start | bytes 786440 | tf_op jit(solution)/shard_map/ppermute | solution.py:370
  169.0 6.8 %collective-permute-start.18 = (bf16[544,128]{1,0:T(8,128)(2,1)}, bf16[544,128]{1,0:T(8,128)(2,1)S(1)}, u32[]{:S(2)}, u32[]{:S(2)}) collective-permute-start(bf16[544,128]{1,0:T(8,128)(2,1)} %far.3.refs_0_), channel_id=1, source_target_pairs={{0,3},{1,0},{2,1},{3,2},{4,7},{5,4},{6,5},{7,6},{8,11},{9,8},{10,9... | collective-permute-start | bytes 417800 | tf_op jit(solution)/shard_map/ppermute | solution.py:370
  172.1 9.8 %collective-permute-start.17 = (bf16[544,128]{1,0:T(8,128)(2,1)}, bf16[544,128]{1,0:T(8,128)(2,1)S(1)}, u32[]{:S(2)}, u32[]{:S(2)}) collective-permute-start(bf16[544,128]{1,0:T(8,128)(2,1)} %far.3.refs_0_), channel_id=1, source_target_pairs={{0,1},{1,2},{2,3},{3,0},{4,5},{5,6},{6,7},{7,4},{8,9},{9,10},{10,1... | collective-permute-start | bytes 417800 | tf_op jit(solution)/shard_map/ppermute | solution.py:370
  172.1 9.8 %collective-permute-start.16 = (bf16[544,128]{1,0:T(8,128)(2,1)}, bf16[544,128]{1,0:T(8,128)(2,1)S(1)}, u32[]{:S(2)}, u32[]{:S(2)}) collective-permute-start(bf16[544,128]{1,0:T(8,128)(2,1)} %far.3.refs_0_), channel_id=1, source_target_pairs={{0,2},{1,3},{2,0},{3,1},{4,6},{5,7},{6,4},{7,5},{8,10},{9,11},{10,... | collective-permute-start | bytes 417800 | tf_op jit(solution)/shard_map/ppermute | solution.py:370
  (18 other events, 53.7 us)

commit v7 on v6

--- a/solution.py
+++ b/solution.py
@@ -26,7 +26,7 @@
 DEPTH = 4
 FULL = 63 << 20
 MOST = 65_000_000
-TIGHT = 66_200_000
+NORM = 24 << 20
 ROOM = 63_600_000
 EPS = 1e-06
 bf16 = jnp.bfloat16
@@ -106,11 +106,12 @@
     for p in range(PAIRS):
         v = (raw_ref[p].astype(f32) * pair_scale(columns, p)).astype(bf16)
         buf[p] = v
-        own_ref[0, p] = v
     for z in range(NZ):
         copy = pltpu.make_async_copy(buf, out_ref.at[z], sem.at[z])
         copy.start()
         copies.append(copy)
+    copies.append(pltpu.make_async_copy(buf, own_ref.at[0], sem.at[NZ]))
+    copies[-1].start()
     for copy in copies:
         copy.wait()
 
@@ -175,7 +176,23 @@
     write_slabs(me_ref, slab_of, out_ref, buf, sem)
 
 
-def order_kernel(me_ref, rows_ref, srcs_ref, count_ref, tile_ref, slab_ref, into_ref, groups_ref, fill, begin):
+class Part:
+    def __init__(self, ref, start):
+        self.ref, self.start = ref, start
+
+    def __getitem__(self, i):
+        return self.ref[self.start + i]
+
+    def __setitem__(self, i, value):
+        self.ref[self.start + i] = value
+
+
+def parts_of(ref):
+    return [Part(ref, start) for start in (0, 2 * SLOTS, 4 * SLOTS, 4 * SLOTS + 2 * MAXG)]
+
+
+def order_kernel(me_ref, rows_ref, srcs_ref, count_ref, lists_ref, fill, begin):
+    tile_ref, slab_ref, into_ref, groups_ref = parts_of(lists_ref)
     count = count_ref[0]
     empty = (me_ref[0] * NC + me_ref[2]) * NZ + me_ref[1]
 
@@ -271,8 +288,8 @@
     )
 
 
-def own_kernel(hop, tile_ref, slab_ref, into_ref, groups_ref, tiles_ref, own_ref, noise_ref, part_ref, acc, src, noise, ring, sem, load):
-    begin, run = add_groups(0, tile_ref, slab_ref, into_ref, groups_ref, tiles_ref, src, acc, ring, sem)
+def own_kernel(hop, lists_ref, tiles_ref, own_ref, noise_ref, part_ref, acc, src, noise, ring, sem, load):
+    begin, run = add_groups(0, *parts_of(lists_ref), tiles_ref, src, acc, ring, sem)
     for step in range(DEPTH):
         begin(step)
     noise_copy = pltpu.make_async_copy(noise_ref.at[hop], noise, load)
@@ -286,16 +303,20 @@
         part_ref[p] = stacked_pair(noise, p).T + fold(acc, p)
 
 
-def far_kernel(hop, tile_ref, slab_ref, into_ref, groups_ref, tiles_ref, got_ref, part_ref, *rest):
+def far_kernel(hop, lists_ref, tiles_ref, got_ref, part_ref, *rest):
     last = hop == HOPS - 1
     if last:
-        out_ref, acc, ring, sem = rest
+        out_ref, acc, src, load, ring, sem = rest
     else:
-        out_ref, sq_ref, acc, ring, sem = rest
-    begin, run = add_groups(1, tile_ref, slab_ref, into_ref, groups_ref, tiles_ref, got_ref, acc, ring, sem)
-    for step in range(DEPTH):
+        out_ref, sq_ref, acc, src, load, ring, sem = rest
+    begin, run = add_groups(1, *parts_of(lists_ref), tiles_ref, src, acc, ring, sem)
+    begin(0)
+    got_copy = pltpu.make_async_copy(got_ref, src, load)
+    got_copy.start()
+    for step in range(1, DEPTH):
         begin(step)
     acc[...] = jnp.zeros_like(acc)
+    got_copy.wait()
     run()
     pairs = []
     for p in range(PAIRS):
@@ -397,7 +418,7 @@
     )
     lists = call(
         order_kernel, "order", [whole(SMEM)] * 4,
-        [((2 * SLOTS,), jnp.int32, SMEM), ((2 * SLOTS,), jnp.int32, SMEM), ((2 * MAXG,), jnp.int32, SMEM), ((2,), jnp.int32, SMEM)],
+        [((4 * SLOTS + 2 * MAXG + 16,), jnp.int32, SMEM)],
         [SMEM((2 * BUCKETS,), jnp.int32), SMEM((2 * BUCKETS,), jnp.int32)],
     )(me, rows, srcs, count)
     owned = None
@@ -416,15 +437,15 @@
         else:
             packed, owned = call(
                 norm_kernel, "norm", [whole()] * (1 + NX),
-                [((NZ, PAIRS, BLK, BLK), bf16, HBM), ((1, PAIRS, BLK, BLK), bf16, VMEM)],
-                [VMEM((PAIRS, BLK, BLK), bf16), DMA((NZ,))],
-                limit=TIGHT,
+                [((NZ, PAIRS, BLK, BLK), bf16, HBM), ((1, PAIRS, BLK, BLK), bf16, HBM)],
+                [VMEM((PAIRS, BLK, BLK), bf16), DMA((NZ + 1,))],
+                limit=NORM,
             )(packed, *totals)
             along = lax.all_to_all(packed, "z", 0, 0, tiled=True)
             needed, owned = lax.optimization_barrier((needed, owned))
             asked = lax.all_gather(needed.reshape(-1), ("y", "core"), axis=0)
             table = slot_table(asked.reshape(NY * NC, NY, NZ, NC, 2), (me[0], 0, me[2]), jnp.arange(NZ, dtype=jnp.int32) * BPD)
-            at, table, asked, *lists = lax.optimization_barrier((me, table, asked, *lists))
+            at, table, asked, lists = lax.optimization_barrier((me, table, asked, lists))
             picked = call(
                 pick_kernel, "pick", [whole(SMEM)] * 2 + [whole()], wide,
                 [VMEM((NZ * BPD, BLK, BLK), bf16), VMEM((N_ROW, BLK, BLK), bf16), DMA((NY * NC,))],
@@ -435,11 +456,11 @@
             tables = [asked] + [shift_by(asked, "z", shift) for shift in ZSHIFTS[1:]]
         ring = [VMEM((DEPTH, STEP * GROUP, BLK, BLK), bf16), DMA((DEPTH, STEP * GROUP))]
         part = call(
-            functools.partial(own_kernel, hop), "own", [whole(SMEM)] * 4 + [whole(HBM), whole(), whole(HBM)],
+            functools.partial(own_kernel, hop), "own", [whole(SMEM)] + [whole(HBM), whole(), whole(HBM)],
             [((PAIRS, BLK, BLK), f32, VMEM)],
             [VMEM((BUCKETS, BLK, BLK), f32), VMEM((PAIRS + 1, BLK, BLK), bf16), VMEM((WIDTH, BPD * BLK), f32)] + ring + [DMA(())],
             limit=FULL, flops=TPD * 2 * BLK**3, moved=4 << 20,
-        )(*lists, tile_vals, owned, noise)
+        )(lists, tile_vals, owned, noise)
         if not last:
             part, *tables = lax.optimization_barrier((part, *tables))
         if last:
@@ -454,10 +475,10 @@
             outs = [((PAIRS, BLK, BLK), f32, VMEM), ((BPD, BLK), f32, VMEM)]
             more = []
         result = call(
-            functools.partial(far_kernel, hop), "far", [whole(SMEM)] * 4 + [whole(HBM), whole(), whole()], outs,
-            [VMEM((BUCKETS, BLK, BLK), f32)] + ring + more,
+            functools.partial(far_kernel, hop), "far", [whole(SMEM)] + [whole(HBM), whole(HBM), whole()], outs,
+            [VMEM((BUCKETS, BLK, BLK), f32), VMEM((N_ROW, BLK, BLK), bf16), DMA(())] + ring + more,
             limit=ROOM, flops=TPD * 2 * BLK**3, moved=8 << 20,
-        )(*lists, tile_vals, got, part)
+        )(lists, tile_vals, got, part)
         if not last:
             packed, squares = result
     tails = [result] + [shift_by(result, "x", shift) for shift in SHIFTS[1:]]

time: 185 us -> 183 us (0.989)
  local copies, waits for them, and re-layouts: 8.8 us -> 6.15 us
    unnamed x58 -> x44, local copies, waits for them, and re-layouts: 7.6 us -> 4.96 us
  transfers between devices with their start and end apart: 22 -> 22, of which waited for: 12 -> 11; matrix products, arithmetic and copies ran while one was open for 1% -> 1% of each run, Pallas kernels for 7% -> 8%
where the time goes in v7:
time: 183 us; the launch traced here: 181 us
  waiting for transfers between devices  70.3 us (38%)
  starting transfers between devices  50.7 us (28%)
  Pallas kernels  35.5 us (19%)
  blocking collectives  16.8 us (9%)
  local copies, waits for them, and re-layouts  6.15 us (3%)
    all_to_all x1, waiting for transfers between devices, shards(): got = lax.all_to_all(picked, ('y', 'core', 'z'), 0, 0, tiled=True)  34.1 us
    ppermute x19, starting transfers between devices, shift_by(): lax.ppermute(value, axis, [(i, (i + shift) % size) for i in range(size)])  27.3 us
    ppermute x19, waiting for transfers between devices, shift_by(): lax.ppermute(value, axis, [(i, (i + shift) % size) for i in range(size)])  20.2 us
    all_gather x1, blocking collectives, shards(): asked = lax.all_gather(needed.reshape(-1), ('y', 'core'), axis=0)  16.8 us
    all_to_all x1, waiting for transfers between devices, shards(): got = lax.all_to_all(picked, ('y', 'core'), 0, 0, tiled=True)  12.3 us
    pallas_call x2, Pallas kernels, shards(): call(functools.partial(far_kernel, hop), 'far', [whole(SMEM)] + [whole(HB...  11.2 us
    pallas_call x2, Pallas kernels, shards(): call(functools.partial(own_kernel, hop), 'own', [whole(SMEM)] + [whole(HB...  8.92 us
    all_to_all x1, starting transfers between devices, shards(): got = lax.all_to_all(picked, ('y', 'core', 'z'), 0, 0, tiled=True)  8.61 us
  transfers between devices with their start and end apart: 22, of which 11 were waited for; matrix products, arithmetic and copies ran while one was open for 1% of the time, Pallas kernels for 8%

profile of v7, /device:TPU:1, one launch (start us, length us, event | category | flops | bytes accessed | tf_op | source)
XLA Modules:
  0.0 181.2 jit_solution(5584601393777947198)
XLA Ops:
  1.1 3.4 %collective-permute-start.2 = (f32[8,128]{1,0:T(8,128)S(1)}, f32[8,128]{1,0:T(8,128)S(1)}, u32[]{:S(2)}, u32[]{:S(2)}) collective-permute-start(f32[8,128]{1,0:T(8,128)S(1)} %get-tuple-element.44.refs_0_), channel_id=1, source_target_pairs={{0,3},{1,0},{2,1},{3,2},{4,7},{5,4},{6,5},{7,6},{8,11},{9,8},{10,9... | collective-permute-start | bytes 12296 | tf_op jit(solution)/shard_map/ppermute | solution.py:391
  4.5 1.7 collective-permute-start
  6.2 1.9 %collective-permute-done.1.refs_2_ = f32[8,128]{1,0:T(8,128)S(1)} collective-permute-done((f32[8,128]{1,0:T(8,128)S(1)}, f32[8,128]{1,0:T(8,128)S(1)}, u32[]{:S(2)}, u32[]{:S(2)}) %collective-permute-start.1) | collective-permute-done | bytes 4128 | tf_op jit(solution)/shard_map/ppermute | solution.py:391
  8.4 1.4 norm.1
  10.5 8.2 %all-to-all-start = ((bf16[8,4,128,128]{3,2,1,0:T(8,128)(2,1)}), bf16[8,4,128,128]{3,2,1,0:T(8,128)(2,1)S(1)}, u32[]{:S(2)}, u32[]{:S(2)}) async-start(bf16[8,4,128,128]{3,2,1,0:T(8,128)(2,1)} %get-tuple-element.54), calls=%async_computation | async-start | bytes 2097152 | tf_op jit(solution)/shard_map/all_to_all | solution.py:444
  19.8 3.8 %order.1.lists_ref = s32[1024]{0:T(1024)S(1)} custom-call(s32[3]{0:T(128)S(1)} %pad_add_fusion.me_ref, s32[160]{0:T(256)S(1)} %bitcast.21, s32[160]{0:T(256)S(1)} %bitcast.22, s32[1]{0:T(128)S(6)} %copy.27.count_ref), custom_call_target="tpu_custom_call" | custom-call | flops 1048576 | bytes 1048576 | tf_op jit(solution)/shard_map/order/pallas_call | solution.py:419
  24.4 16.8 %all-gather = s32[8,1,128]{2,1,0:T(1,128)S(1)} all-gather(s32[1,1,128]{2,1,0:T(1,128)S(1)} %reshape.33), channel_id=1, replica_groups=mesh['y'=4,'z'=8,'core'=2,'x'=4] {'y','core'}, dimensions={0}, use_global_device_ids=true | all-gather | bytes 4608 | tf_op jit(solution)/shard_map/all_gather | solution.py:446
  42.5 3.7 %all-to-all-done.z_ref = bf16[8,4,128,128]{3,2,1,0:T(8,128)(2,1)S(1)} async-done(((bf16[8,4,128,128]{3,2,1,0:T(8,128)(2,1)}), bf16[8,4,128,128]{3,2,1,0:T(8,128)(2,1)S(1)}, u32[]{:S(2)}, u32[]{:S(2)}) %all-to-all-start) | async-done | bytes 1048608 | tf_op jit(solution)/shard_map/all_to_all | solution.py:444
  47.3 3.1 %pick.1 = bf16[64,128,128]{2,1,0:T(8,128)(2,1)} custom-call(s32[3]{0:T(128)} %copy-done.5, s32[128]{0:T(128)} %multiply_add_fusion.idx_ref, bf16[8,4,128,128]{3,2,1,0:T(8,128)(2,1)} %copy-done.8), custom_call_target="tpu_custom_call" | custom-call | flops 1048576 | bytes 1048576 | tf_op jit(solution)/shard_map/pick/pallas_call | solution.py:449
  50.4 6.6 %all-to-all-start.1 = ((bf16[64,128,128]{2,1,0:T(8,128)(2,1)}), bf16[64,128,128]{2,1,0:T(8,128)(2,1)}, u32[]{:S(2)}, u32[]{:S(2)}) async-start(bf16[64,128,128]{2,1,0:T(8,128)(2,1)} %pick.1), calls=%async_computation.1 | async-start | bytes 4194304 | tf_op jit(solution)/shard_map/all_to_all | solution.py:455
  57.0 1.5 collective-permute-start.8
  58.5 2.4 %collective-permute-start.6 = (s32[8,128]{1,0:T(8,128)S(1)}, s32[8,128]{1,0:T(8,128)S(1)}, u32[]{:S(2)}, u32[]{:S(2)}) collective-permute-start(s32[8,128]{1,0:T(8,128)S(1)} %bitcast.30), channel_id=1, source_target_pairs={{0,16},{8,24},{16,32},{24,40},{32,48},{40,56},{48,0},{56,8},{1,17}... | collective-permute-start | bytes 12296 | tf_op jit(solution)/shard_map/ppermute | solution.py:391
  60.8 1.4 collective-permute-start.5
  62.2 1.9 %collective-permute-start.4 = (s32[8,128]{1,0:T(8,128)S(1)}, s32[8,128]{1,0:T(8,128)S(1)}, u32[]{:S(2)}, u32[]{:S(2)}) collective-permute-start(s32[8,128]{1,0:T(8,128)S(1)} %bitcast.32), channel_id=1, source_target_pairs={{0,24},{8,32},{16,40},{24,48},{32,56},{40,0},{48,8},{56,16},{1,25}... | collective-permute-start | bytes 12296 | tf_op jit(solution)/shard_map/ppermute | solution.py:391
  64.1 2.3 %collective-permute-start.3 = (s32[8,128]{1,0:T(8,128)S(1)}, s32[8,128]{1,0:T(8,128)S(1)}, u32[]{:S(2)}, u32[]{:S(2)}) collective-permute-start(s32[8,128]{1,0:T(8,128)S(1)} %bitcast.33), channel_id=1, source_target_pairs={{0,32},{8,40},{16,48},{24,56},{32,0},{40,8},{48,16},{56,24},{1,33}... | collective-permute-start | bytes 12296 | tf_op jit(solution)/shard_map/ppermute | solution.py:391
  66.4 4.4 %own.2.part_ref = f32[4,128,128]{2,1,0:T(8,128)} custom-call(s32[1024]{0:T(1024)} %copy-done.4, bf16[160,128,128]{2,1,0:T(8,128)(2,1)} %tiles_ref.7, bf16[1,4,128,128]{3,2,1,0:T(8,128)(2,1)} %copy-done.2, f32[2,64,1024]{2,1,0:T(8,128)} %bitcast.23), custom_call_target="tpu_custom_call" | custom-call | flops 671088640 | bytes 4194304 | tf_op jit(solution)/shard_map/own/pallas_call | solution.py:458
  71.0 12.3 %all-to-all-done.1.got_ref = bf16[64,128,128]{2,1,0:T(8,128)(2,1)} async-done(((bf16[64,128,128]{2,1,0:T(8,128)(2,1)}), bf16[64,128,128]{2,1,0:T(8,128)(2,1)}, u32[]{:S(2)}, u32[]{:S(2)}) %all-to-all-start.1) | async-done | bytes 2097184 | tf_op jit(solution)/shard_map/all_to_all | solution.py:455
  83.3 5.6 %far.2 = (f32[4,128,128]{2,1,0:T(8,128)}, f32[8,128]{1,0:T(8,128)}) custom-call(s32[1024]{0:T(1024)} %copy-done.4, bf16[160,128,128]{2,1,0:T(8,128)(2,1)} %tiles_ref.7, bf16[64,128,128]{2,1,0:T(8,128)(2,1)} %all-to-all-done.1.got_ref, f32[4,128,128]{2,1,0:T(8,128)} %own.2.part_ref), custom_call_target="tpu_custom_call" | custom-call | flops 671088640 | bytes 8388608 | tf_op jit(solution)/shard_map/far/pallas_call | solution.py:477
  88.9 2.9 %collective-permute-start.12 = (f32[8,128]{1,0:T(8,128)}, f32[8,128]{1,0:T(8,128)S(1)}, u32[]{:S(2)}, u32[]{:S(2)}) collective-permute-start(f32[8,128]{1,0:T(8,128)} %get-tuple-element.68.refs_9_), channel_id=1, source_target_pairs={{0,3},{1,0},{2,1},{3,2},{4,7},{5,4},{6,5},{7,6},{8,11},{9,8},{10,9... | collective-permute-start | bytes 12296 | tf_op jit(solution)/shard_map/ppermute | solution.py:391
  93.2 2.6 %collective-permute-done.11.refs_11_ = f32[8,128]{1,0:T(8,128)S(1)} collective-permute-done((f32[8,128]{1,0:T(8,128)}, f32[8,128]{1,0:T(8,128)S(1)}, u32[]{:S(2)}, u32[]{:S(2)}) %collective-permute-start.11) | collective-permute-done | bytes 4128 | tf_op jit(solution)/shard_map/ppermute | solution.py:391
  96.6 4.1 %send.1 = (bf16[64,128,128]{2,1,0:T(8,128)(2,1)}, bf16[2,4,128,128]{3,2,1,0:T(8,128)(2,1)}) custom-call(s32[3]{0:T(128)} %copy-done.5, s32[8,128]{1,0:T(8,128)} %bitcast.34, s32[8,128]{1,0:T(8,128)} %copy-done.16, s32[8,128]{1,0:T(8,128)} %copy-done.15, s32[8,128]{1,0:T(8,128)} %copy-done.14, s32[8,128]{1,0:T(8,128)} %copy-done.13, s32[8,128]{1,0:T(8,128)} %copy-done.12, ...), custom_call_target="tpu_custom_call" | custom-call | flops 1048576 | bytes 1048576 | tf_op jit(solution)/shard_map/send/pallas_call | solution.py:430
  100.8 8.6 %all-to-all-start.2 = ((bf16[64,128,128]{2,1,0:T(8,128)(2,1)}), bf16[64,128,128]{2,1,0:T(8,128)(2,1)}, u32[]{:S(2)}, u32[]{:S(2)}) async-start(bf16[64,128,128]{2,1,0:T(8,128)(2,1)} %get-tuple-element.71), calls=%async_computation.2 | async-start | bytes 4194304 | tf_op jit(solution)/shard_map/all_to_all | solution.py:436
  109.4 3.0 %collective-permute-start.15 = (bf16[2,4,128,128]{3,2,1,0:T(8,128)(2,1)}, bf16[2,4,128,128]{3,2,1,0:T(8,128)(2,1)}, u32[]{:S(2)}, u32[]{:S(2)}) collective-permute-start(bf16[2,4,128,128]{3,2,1,0:T(8,128)(2,1)} %get-tuple-element.69.refs_0_.own_ref), channel_id=1, source_target_pairs={{0,3},{1,0},{2,1},{3,2},{4,7},{5,4},{6,5},{7,6},{8,11},{9,8},{10,9... | collective-permute-start | bytes 786440 | tf_op jit(solution)/shard_map/ppermute | solution.py:391
  114.0 4.5 %own.3.part_ref = f32[4,128,128]{2,1,0:T(8,128)} custom-call(s32[1024]{0:T(1024)} %copy-done.4, bf16[160,128,128]{2,1,0:T(8,128)(2,1)} %tiles_ref.7, bf16[2,4,128,128]{3,2,1,0:T(8,128)(2,1)} %get-tuple-element.69.refs_0_.own_ref, f32[2,64,1024]{2,1,0:T(8,128)} %bitcast.24), custom_call_target="tpu_custom_call" | custom-call | flops 671088640 | bytes 4194304 | tf_op jit(solution)/shard_map/own/pallas_call | solution.py:458
  118.5 4.8 %collective-permute-done.15.refs_3_ = bf16[2,4,128,128]{3,2,1,0:T(8,128)(2,1)} collective-permute-done((bf16[2,4,128,128]{3,2,1,0:T(8,128)(2,1)}, bf16[2,4,128,128]{3,2,1,0:T(8,128)(2,1)}, u32[]{:S(2)}, u32[]{:S(2)}) %collective-permute-start.15) | collective-permute-done | bytes 262176 | tf_op jit(solution)/shard_map/ppermute | solution.py:391
  123.3 2.2 %collective-permute-done.13.refs_1_ = bf16[2,4,128,128]{3,2,1,0:T(8,128)(2,1)} collective-permute-done((bf16[2,4,128,128]{3,2,1,0:T(8,128)(2,1)}, bf16[2,4,128,128]{3,2,1,0:T(8,128)(2,1)}, u32[]{:S(2)}, u32[]{:S(2)}) %collective-permute-start.13) | collective-permute-done | bytes 262176 | tf_op jit(solution)/shard_map/ppermute | solution.py:391
  125.5 1.6 early.1.early_ref
  127.1 34.1 %all-to-all-done.2.got_ref = bf16[64,128,128]{2,1,0:T(8,128)(2,1)} async-done(((bf16[64,128,128]{2,1,0:T(8,128)(2,1)}), bf16[64,128,128]{2,1,0:T(8,128)(2,1)}, u32[]{:S(2)}, u32[]{:S(2)}) %all-to-all-start.2) | async-done | bytes 2097184 | tf_op jit(solution)/shard_map/all_to_all | solution.py:436
  161.2 5.6 %far.3.refs_0_ = bf16[544,128]{1,0:T(8,128)(2,1)} custom-call(s32[1024]{0:T(1024)} %copy-done.4, bf16[160,128,128]{2,1,0:T(8,128)(2,1)} %tiles_ref.7, bf16[64,128,128]{2,1,0:T(8,128)(2,1)} %all-to-all-done.2.got_ref, f32[4,128,128]{2,1,0:T(8,128)} %own.3.part_ref), custom_call_target="tpu_custom_call" | custom-call | flops 671088640 | bytes 8388608 | tf_op jit(solution)/shard_map/far/pallas_call | solution.py:477
  166.8 3.0 %collective-permute-start.18 = (bf16[544,128]{1,0:T(8,128)(2,1)}, bf16[544,128]{1,0:T(8,128)(2,1)S(1)}, u32[]{:S(2)}, u32[]{:S(2)}) collective-permute-start(bf16[544,128]{1,0:T(8,128)(2,1)} %far.3.refs_0_), channel_id=1, source_target_pairs={{0,3},{1,0},{2,1},{3,2},{4,7},{5,4},{6,5},{7,6},{8,11},{9,8},{10,9... | collective-permute-start | bytes 417800 | tf_op jit(solution)/shard_map/ppermute | solution.py:391
  171.1 2.0 %collective-permute-done.18.refs_3_ = bf16[544,128]{1,0:T(8,128)(2,1)S(1)} collective-permute-done((bf16[544,128]{1,0:T(8,128)(2,1)}, bf16[544,128]{1,0:T(8,128)(2,1)S(1)}, u32[]{:S(2)}, u32[]{:S(2)}) %collective-permute-start.18) | collective-permute-done | bytes 139296 | tf_op jit(solution)/shard_map/ppermute | solution.py:391
  173.1 6.0 %collective-permute-done.17.refs_2_ = bf16[544,128]{1,0:T(8,128)(2,1)S(1)} collective-permute-done((bf16[544,128]{1,0:T(8,128)(2,1)}, bf16[544,128]{1,0:T(8,128)(2,1)S(1)}, u32[]{:S(2)}, u32[]{:S(2)}) %collective-permute-start.17) | collective-permute-done | bytes 139296 | tf_op jit(solution)/shard_map/ppermute | solution.py:391
  (85 shorter events, 12.6 us)
Async XLA Ops:
  0.0 113.7 %copy-start = (bf16[3,256,256]{2,1,0:T(8,128)(2,1)S(1)}, bf16[3,256,256]{2,1,0:T(8,128)(2,1)}, u32[]{:S(2)}) copy-start(bf16[3,256,256]{2,1,0:T(8,128)(2,1)} %param.15) | copy-start | bytes 1179652
  0.0 19.8 %copy-start.6 = (s32[1,160]{1,0:T(1,128)S(1)}, s32[1,160]{1,0:T(1,128)}, u32[]{:S(2)}) copy-start(s32[1,160]{1,0:T(1,128)} %param.10) | copy-start | bytes 1924
  1.0 18.8 %copy-start.7 = (s32[1,160]{1,0:T(1,128)S(1)}, s32[1,160]{1,0:T(1,128)}, u32[]{:S(2)}) copy-start(s32[1,160]{1,0:T(1,128)} %param.11) | copy-start | bytes 1924
  1.0 23.2 %copy-start.20 = (s32[1,64,2]{1,2,0:T(2,128)S(1)}, s32[1,64,2]{1,2,0:T(2,128)}, u32[]{:S(2)}) copy-start(s32[1,64,2]{1,2,0:T(2,128)} %param.13) | copy-start | bytes 1540
  1.1 5.1 %collective-permute-start.2 = (f32[8,128]{1,0:T(8,128)S(1)}, f32[8,128]{1,0:T(8,128)S(1)}, u32[]{:S(2)}, u32[]{:S(2)}) collective-permute-start(f32[8,128]{1,0:T(8,128)S(1)} %get-tuple-element.44.refs_0_), channel_id=1, source_target_pairs={{0,3},{1,0},{2,1},{3,2},{4,7},{5,4},{6,5},{7,6},{8,11},{9,8},{10,9... | collective-permute-start | bytes 12296 | tf_op jit(solution)/shard_map/ppermute | solution.py:391
  4.5 3.7 %collective-permute-start.1 = (f32[8,128]{1,0:T(8,128)S(1)}, f32[8,128]{1,0:T(8,128)S(1)}, u32[]{:S(2)}, u32[]{:S(2)}) collective-permute-start(f32[8,128]{1,0:T(8,128)S(1)} %get-tuple-element.44.refs_0_), channel_id=1, source_target_pairs={{0,1},{1,2},{2,3},{3,0},{4,5},{5,6},{6,7},{7,4},{8,9},{9,10},{10,1... | collective-permute-start | bytes 12296 | tf_op jit(solution)/shard_map/ppermute | solution.py:391
  4.5 4.0 %collective-permute-start = (f32[8,128]{1,0:T(8,128)S(1)}, f32[8,128]{1,0:T(8,128)S(1)}, u32[]{:S(2)}, u32[]{:S(2)}) collective-permute-start(f32[8,128]{1,0:T(8,128)S(1)} %get-tuple-element.44.refs_0_), channel_id=1, source_target_pairs={{0,2},{1,3},{2,0},{3,1},{4,6},{5,7},{6,4},{7,5},{8,10},{9,11},{10,... | collective-permute-start | bytes 12296 | tf_op jit(solution)/shard_map/ppermute | solution.py:391
  10.5 35.8 %all-to-all-start = ((bf16[8,4,128,128]{3,2,1,0:T(8,128)(2,1)}), bf16[8,4,128,128]{3,2,1,0:T(8,128)(2,1)S(1)}, u32[]{:S(2)}, u32[]{:S(2)}) async-start(bf16[8,4,128,128]{3,2,1,0:T(8,128)(2,1)} %get-tuple-element.54), calls=%async_computation | async-start | bytes 2097152 | tf_op jit(solution)/shard_map/all_to_all | solution.py:444
  19.8 26.5 %copy-start.5 = (s32[3]{0:T(128)}, s32[3]{0:T(128)S(1)}, u32[]{:S(2)}) copy-start(s32[3]{0:T(128)S(1)} %pad_add_fusion.me_ref) | copy-start | bytes 40
  41.2 22.9 %copy-start.9 = (s32[8,1,128]{2,1,0:T(1,128)}, s32[8,1,128]{2,1,0:T(1,128)S(1)}, u32[]{:S(2)}) copy-start(s32[8,1,128]{2,1,0:T(1,128)S(1)} %all-gather) | copy-start | bytes 12292
  50.4 32.9 %all-to-all-start.1 = ((bf16[64,128,128]{2,1,0:T(8,128)(2,1)}), bf16[64,128,128]{2,1,0:T(8,128)(2,1)}, u32[]{:S(2)}, u32[]{:S(2)}) async-start(bf16[64,128,128]{2,1,0:T(8,128)(2,1)} %pick.1), calls=%async_computation.1 | async-start | bytes 4194304 | tf_op jit(solution)/shard_map/all_to_all | solution.py:455
  57.0 5.2 %collective-permute-start.9 = (s32[8,128]{1,0:T(8,128)S(1)}, s32[8,128]{1,0:T(8,128)S(1)}, u32[]{:S(2)}, u32[]{:S(2)}) collective-permute-start(s32[8,128]{1,0:T(8,128)S(1)} %bitcast.27), channel_id=1, source_target_pairs={{0,56},{8,0},{16,8},{24,16},{32,24},{40,32},{48,40},{56,48},{1,57}... | collective-permute-start | bytes 12296 | tf_op jit(solution)/shard_map/ppermute | solution.py:391
  57.0 7.1 %collective-permute-start.8 = (s32[8,128]{1,0:T(8,128)S(1)}, s32[8,128]{1,0:T(8,128)S(1)}, u32[]{:S(2)}, u32[]{:S(2)}) collective-permute-start(s32[8,128]{1,0:T(8,128)S(1)} %bitcast.28), channel_id=1, source_target_pairs={{0,8},{8,16},{16,24},{24,32},{32,40},{40,48},{48,56},{56,0},{1,9},... | collective-permute-start | bytes 12296 | tf_op jit(solution)/shard_map/ppermute | solution.py:391
  58.5 12.4 %collective-permute-start.7 = (s32[8,128]{1,0:T(8,128)S(1)}, s32[8,128]{1,0:T(8,128)S(1)}, u32[]{:S(2)}, u32[]{:S(2)}) collective-permute-start(s32[8,128]{1,0:T(8,128)S(1)} %bitcast.29), channel_id=1, source_target_pairs={{0,48},{8,56},{16,0},{24,8},{32,16},{40,24},{48,32},{56,40},{1,49}... | collective-permute-start | bytes 12296 | tf_op jit(solution)/shard_map/ppermute | solution.py:391
  58.5 12.4 %collective-permute-start.6 = (s32[8,128]{1,0:T(8,128)S(1)}, s32[8,128]{1,0:T(8,128)S(1)}, u32[]{:S(2)}, u32[]{:S(2)}) collective-permute-start(s32[8,128]{1,0:T(8,128)S(1)} %bitcast.30), channel_id=1, source_target_pairs={{0,16},{8,24},{16,32},{24,40},{32,48},{40,56},{48,0},{56,8},{1,17}... | collective-permute-start | bytes 12296 | tf_op jit(solution)/shard_map/ppermute | solution.py:391
  60.8 10.1 %collective-permute-start.5 = (s32[8,128]{1,0:T(8,128)S(1)}, s32[8,128]{1,0:T(8,128)S(1)}, u32[]{:S(2)}, u32[]{:S(2)}) collective-permute-start(s32[8,128]{1,0:T(8,128)S(1)} %bitcast.31), channel_id=1, source_target_pairs={{0,40},{8,48},{16,56},{24,0},{32,8},{40,16},{48,24},{56,32},{1,41}... | collective-permute-start | bytes 12296 | tf_op jit(solution)/shard_map/ppermute | solution.py:391
  62.2 8.7 %collective-permute-start.4 = (s32[8,128]{1,0:T(8,128)S(1)}, s32[8,128]{1,0:T(8,128)S(1)}, u32[]{:S(2)}, u32[]{:S(2)}) collective-permute-start(s32[8,128]{1,0:T(8,128)S(1)} %bitcast.32), channel_id=1, source_target_pairs={{0,24},{8,32},{16,40},{24,48},{32,56},{40,0},{48,8},{56,16},{1,25}... | collective-permute-start | bytes 12296 | tf_op jit(solution)/shard_map/ppermute | solution.py:391
  64.1 6.9 %collective-permute-start.3 = (s32[8,128]{1,0:T(8,128)S(1)}, s32[8,128]{1,0:T(8,128)S(1)}, u32[]{:S(2)}, u32[]{:S(2)}) collective-permute-start(s32[8,128]{1,0:T(8,128)S(1)} %bitcast.33), channel_id=1, source_target_pairs={{0,32},{8,40},{16,48},{24,56},{32,0},{40,8},{48,16},{56,24},{1,33}... | collective-permute-start | bytes 12296 | tf_op jit(solution)/shard_map/ppermute | solution.py:391
  70.9 18.0 %copy-start.12 = (s32[8,128]{1,0:T(8,128)}, s32[8,128]{1,0:T(8,128)S(1)}, u32[]{:S(2)}) copy-start(s32[8,128]{1,0:T(8,128)S(1)} %collective-permute-done.7.refs_5_) | copy-start | bytes 12292
  70.9 18.0 %copy-start.13 = (s32[8,128]{1,0:T(8,128)}, s32[8,128]{1,0:T(8,128)S(1)}, u32[]{:S(2)}) copy-start(s32[8,128]{1,0:T(8,128)S(1)} %collective-permute-done.6.refs_4_) | copy-start | bytes 12292
  70.9 18.0 %copy-start.14 = (s32[8,128]{1,0:T(8,128)}, s32[8,128]{1,0:T(8,128)S(1)}, u32[]{:S(2)}) copy-start(s32[8,128]{1,0:T(8,128)S(1)} %collective-permute-done.5.refs_3_) | copy-start | bytes 12292
  70.9 18.0 %copy-start.15 = (s32[8,128]{1,0:T(8,128)}, s32[8,128]{1,0:T(8,128)S(1)}, u32[]{:S(2)}) copy-start(s32[8,128]{1,0:T(8,128)S(1)} %collective-permute-done.4.refs_2_) | copy-start | bytes 12292
  88.9 4.2 %collective-permute-start.12 = (f32[8,128]{1,0:T(8,128)}, f32[8,128]{1,0:T(8,128)S(1)}, u32[]{:S(2)}, u32[]{:S(2)}) collective-permute-start(f32[8,128]{1,0:T(8,128)} %get-tuple-element.68.refs_9_), channel_id=1, source_target_pairs={{0,3},{1,0},{2,1},{3,2},{4,7},{5,4},{6,5},{7,6},{8,11},{9,8},{10,9... | collective-permute-start | bytes 12296 | tf_op jit(solution)/shard_map/ppermute | solution.py:391
  91.9 3.9 %collective-permute-start.11 = (f32[8,128]{1,0:T(8,128)}, f32[8,128]{1,0:T(8,128)S(1)}, u32[]{:S(2)}, u32[]{:S(2)}) collective-permute-start(f32[8,128]{1,0:T(8,128)} %get-tuple-element.68.refs_9_), channel_id=1, source_target_pairs={{0,1},{1,2},{2,3},{3,0},{4,5},{5,6},{6,7},{7,4},{8,9},{9,10},{10,1... | collective-permute-start | bytes 12296 | tf_op jit(solution)/shard_map/ppermute | solution.py:391
  91.9 4.2 %collective-permute-start.10 = (f32[8,128]{1,0:T(8,128)}, f32[8,128]{1,0:T(8,128)S(1)}, u32[]{:S(2)}, u32[]{:S(2)}) collective-permute-start(f32[8,128]{1,0:T(8,128)} %get-tuple-element.68.refs_9_), channel_id=1, source_target_pairs={{0,2},{1,3},{2,0},{3,1},{4,6},{5,7},{6,4},{7,5},{8,10},{9,11},{10,... | collective-permute-start | bytes 12296 | tf_op jit(solution)/shard_map/ppermute | solution.py:391
  100.8 60.4 %all-to-all-start.2 = ((bf16[64,128,128]{2,1,0:T(8,128)(2,1)}), bf16[64,128,128]{2,1,0:T(8,128)(2,1)}, u32[]{:S(2)}, u32[]{:S(2)}) async-start(bf16[64,128,128]{2,1,0:T(8,128)(2,1)} %get-tuple-element.71), calls=%async_computation.2 | async-start | bytes 4194304 | tf_op jit(solution)/shard_map/all_to_all | solution.py:436
  109.4 13.9 %collective-permute-start.15 = (bf16[2,4,128,128]{3,2,1,0:T(8,128)(2,1)}, bf16[2,4,128,128]{3,2,1,0:T(8,128)(2,1)}, u32[]{:S(2)}, u32[]{:S(2)}) collective-permute-start(bf16[2,4,128,128]{3,2,1,0:T(8,128)(2,1)} %get-tuple-element.69.refs_0_.own_ref), channel_id=1, source_target_pairs={{0,3},{1,0},{2,1},{3,2},{4,7},{5,4},{6,5},{7,6},{8,11},{9,8},{10,9... | collective-permute-start | bytes 786440 | tf_op jit(solution)/shard_map/ppermute | solution.py:391
  112.4 10.9 %collective-permute-start.14 = (bf16[2,4,128,128]{3,2,1,0:T(8,128)(2,1)}, bf16[2,4,128,128]{3,2,1,0:T(8,128)(2,1)}, u32[]{:S(2)}, u32[]{:S(2)}) collective-permute-start(bf16[2,4,128,128]{3,2,1,0:T(8,128)(2,1)} %get-tuple-element.69.refs_0_.own_ref), channel_id=1, source_target_pairs={{0,1},{1,2},{2,3},{3,0},{4,5},{5,6},{6,7},{7,4},{8,9},{9,10},{10,1... | collective-permute-start | bytes 786440 | tf_op jit(solution)/shard_map/ppermute | solution.py:391
  112.4 13.1 %collective-permute-start.13 = (bf16[2,4,128,128]{3,2,1,0:T(8,128)(2,1)}, bf16[2,4,128,128]{3,2,1,0:T(8,128)(2,1)}, u32[]{:S(2)}, u32[]{:S(2)}) collective-permute-start(bf16[2,4,128,128]{3,2,1,0:T(8,128)(2,1)} %get-tuple-element.69.refs_0_.own_ref), channel_id=1, source_target_pairs={{0,2},{1,3},{2,0},{3,1},{4,6},{5,7},{6,4},{7,5},{8,10},{9,11},{10,... | collective-permute-start | bytes 786440 | tf_op jit(solution)/shard_map/ppermute | solution.py:391
  166.8 6.3 %collective-permute-start.18 = (bf16[544,128]{1,0:T(8,128)(2,1)}, bf16[544,128]{1,0:T(8,128)(2,1)S(1)}, u32[]{:S(2)}, u32[]{:S(2)}) collective-permute-start(bf16[544,128]{1,0:T(8,128)(2,1)} %far.3.refs_0_), channel_id=1, source_target_pairs={{0,3},{1,0},{2,1},{3,2},{4,7},{5,4},{6,5},{7,6},{8,11},{9,8},{10,9... | collective-permute-start | bytes 417800 | tf_op jit(solution)/shard_map/ppermute | solution.py:391
  169.9 9.3 %collective-permute-start.17 = (bf16[544,128]{1,0:T(8,128)(2,1)}, bf16[544,128]{1,0:T(8,128)(2,1)S(1)}, u32[]{:S(2)}, u32[]{:S(2)}) collective-permute-start(bf16[544,128]{1,0:T(8,128)(2,1)} %far.3.refs_0_), channel_id=1, source_target_pairs={{0,1},{1,2},{2,3},{3,0},{4,5},{5,6},{6,7},{7,4},{8,9},{9,10},{10,1... | collective-permute-start | bytes 417800 | tf_op jit(solution)/shard_map/ppermute | solution.py:391
  169.9 9.3 %collective-permute-start.16 = (bf16[544,128]{1,0:T(8,128)(2,1)}, bf16[544,128]{1,0:T(8,128)(2,1)S(1)}, u32[]{:S(2)}, u32[]{:S(2)}) collective-permute-start(bf16[544,128]{1,0:T(8,128)(2,1)} %far.3.refs_0_), channel_id=1, source_target_pairs={{0,2},{1,3},{2,0},{3,1},{4,6},{5,7},{6,4},{7,5},{8,10},{9,11},{10,... | collective-permute-start | bytes 417800 | tf_op jit(solution)/shard_map/ppermute | solution.py:391
  (11 other events, 41.6 us)

commit v8 on v7

--- a/solution.py
+++ b/solution.py
@@ -306,17 +306,13 @@
 def far_kernel(hop, lists_ref, tiles_ref, got_ref, part_ref, *rest):
     last = hop == HOPS - 1
     if last:
-        out_ref, acc, src, load, ring, sem = rest
+        out_ref, acc, ring, sem = rest
     else:
-        out_ref, sq_ref, acc, src, load, ring, sem = rest
-    begin, run = add_groups(1, *parts_of(lists_ref), tiles_ref, src, acc, ring, sem)
-    begin(0)
-    got_copy = pltpu.make_async_copy(got_ref, src, load)
-    got_copy.start()
-    for step in range(1, DEPTH):
+        out_ref, sq_ref, acc, ring, sem = rest
+    begin, run = add_groups(1, *parts_of(lists_ref), tiles_ref, got_ref, acc, ring, sem)
+    for step in range(DEPTH):
         begin(step)
     acc[...] = jnp.zeros_like(acc)
-    got_copy.wait()
     run()
     pairs = []
     for p in range(PAIRS):
@@ -430,7 +426,7 @@
             picked, owned = call(
                 send_kernel, "send", [whole(SMEM)] * (1 + NZ) + [whole()] * (2 + NX), wide + [((2, PAIRS, BLK, BLK), bf16, VMEM)],
                 [VMEM((BPD, BLK, BLK), bf16), VMEM((N_ROW, BLK, BLK), bf16), DMA((NY * NC,))],
-                limit=MOST,
+                limit=NORM,
             )(me, *tables, packed, *totals, owned)
             spread = [owned] + [shift_by(owned, "x", shift) for shift in SHIFTS[1:]]
             got = lax.all_to_all(picked, ("y", "core", "z"), 0, 0, tiled=True)
@@ -449,7 +445,7 @@
             picked = call(
                 pick_kernel, "pick", [whole(SMEM)] * 2 + [whole()], wide,
                 [VMEM((NZ * BPD, BLK, BLK), bf16), VMEM((N_ROW, BLK, BLK), bf16), DMA((NY * NC,))],
-                limit=MOST,
+                limit=NORM,
             )(at, table, along)
             picked, asked = lax.optimization_barrier((picked, asked))
             got = lax.all_to_all(picked, ("y", "core"), 0, 0, tiled=True)
@@ -475,8 +471,8 @@
             outs = [((PAIRS, BLK, BLK), f32, VMEM), ((BPD, BLK), f32, VMEM)]
             more = []
         result = call(
-            functools.partial(far_kernel, hop), "far", [whole(SMEM)] + [whole(HBM), whole(HBM), whole()], outs,
-            [VMEM((BUCKETS, BLK, BLK), f32), VMEM((N_ROW, BLK, BLK), bf16), DMA(())] + ring + more,
+            functools.partial(far_kernel, hop), "far", [whole(SMEM)] + [whole(HBM), whole(), whole()], outs,
+            [VMEM((BUCKETS, BLK, BLK), f32)] + ring + more,
             limit=ROOM, flops=TPD * 2 * BLK**3, moved=8 << 20,
         )(lists, tile_vals, got, part)
         if not last:

time: 183 us -> 183 us (level)
  blocking collectives: 16.8 us -> 12 us
  waiting for transfers between devices: 70.3 us -> 73.8 us
  Pallas kernels: 35.5 us -> 37.9 us
    all_gather x1, blocking collectives: 16.8 us -> 12 us  [shards(): asked = lax.all_gather(needed.reshape(-1), ('y', 'core'), axis=0)]
    all_to_all x1, waiting for transfers between devices: 3.75 us -> 7.53 us  [shards(): along = lax.all_to_all(packed, 'z', 0, 0, tiled=True)]
    unnamed x44 -> x24, local copies, waits for them, and re-layouts: 4.96 us -> 4.98 us
  transfers between devices with their start and end apart: 22 -> 22, of which waited for: 11 -> 11; matrix products, arithmetic and copies ran while one was open for 1% -> 1% of each run, Pallas kernels for 8% -> 9%
where the time goes in v8:
time: 183 us; the launch traced here: 181 us
  waiting for transfers between devices  73.8 us (40%)
  starting transfers between devices  49.9 us (27%)
  Pallas kernels  37.9 us (21%)
  blocking collectives  12 us (7%)
  local copies, waits for them, and re-layouts  6.17 us (3%)
    all_to_all x1, waiting for transfers between devices, shards(): got = lax.all_to_all(picked, ('y', 'core', 'z'), 0, 0, tiled=True)  34.1 us
    ppermute x19, starting transfers between devices, shift_by(): lax.ppermute(value, axis, [(i, (i + shift) % size) for i in range(size)])  27.2 us
    ppermute x19, waiting for transfers between devices, shift_by(): lax.ppermute(value, axis, [(i, (i + shift) % size) for i in range(size)])  20.2 us
    all_gather x1, blocking collectives, shards(): asked = lax.all_gather(needed.reshape(-1), ('y', 'core'), axis=0)  12 us
    all_to_all x1, waiting for transfers between devices, shards(): got = lax.all_to_all(picked, ('y', 'core'), 0, 0, tiled=True)  12 us
    pallas_call x2, Pallas kernels, shards(): call(functools.partial(far_kernel, hop), 'far', [whole(SMEM)] + [whole(HB...  11.9 us
    pallas_call x2, Pallas kernels, shards(): call(functools.partial(own_kernel, hop), 'own', [whole(SMEM)] + [whole(HB...  10.1 us
    all_to_all x1, starting transfers between devices, shards(): along = lax.all_to_all(packed, 'z', 0, 0, tiled=True)  8.19 us
  transfers between devices with their start and end apart: 22, of which 11 were waited for; matrix products, arithmetic and copies ran while one was open for 1% of the time, Pallas kernels for 9%

profile of v8, /device:TPU:1, one launch (start us, length us, event | category | flops | bytes accessed | tf_op | source)
XLA Modules:
  0.0 180.9 jit_solution(18338437520046586596)
XLA Ops:
  1.1 3.4 %collective-permute-start.2 = (f32[8,128]{1,0:T(8,128)S(1)}, f32[8,128]{1,0:T(8,128)S(1)}, u32[]{:S(2)}, u32[]{:S(2)}) collective-permute-start(f32[8,128]{1,0:T(8,128)S(1)} %get-tuple-element.44.refs_0_), channel_id=1, source_target_pairs={{0,3},{1,0},{2,1},{3,2},{4,7},{5,4},{6,5},{7,6},{8,11},{9,8},{10,9... | collective-permute-start | bytes 12296 | tf_op jit(solution)/shard_map/ppermute | solution.py:387
  4.5 1.7 collective-permute-start
  6.2 1.9 %collective-permute-done.1.refs_2_ = f32[8,128]{1,0:T(8,128)S(1)} collective-permute-done((f32[8,128]{1,0:T(8,128)S(1)}, f32[8,128]{1,0:T(8,128)S(1)}, u32[]{:S(2)}, u32[]{:S(2)}) %collective-permute-start.1) | collective-permute-done | bytes 4128 | tf_op jit(solution)/shard_map/ppermute | solution.py:387
  8.4 1.4 norm.1
  10.5 8.2 %all-to-all-start = ((bf16[8,4,128,128]{3,2,1,0:T(8,128)(2,1)}), bf16[8,4,128,128]{3,2,1,0:T(8,128)(2,1)S(1)}, u32[]{:S(2)}, u32[]{:S(2)}) async-start(bf16[8,4,128,128]{3,2,1,0:T(8,128)(2,1)} %get-tuple-element.54), calls=%async_computation | async-start | bytes 2097152 | tf_op jit(solution)/shard_map/all_to_all | solution.py:440
  19.8 5.4 %order.1.lists_ref = s32[1024]{0:T(1024)S(1)} custom-call(s32[3]{0:T(128)S(1)} %pad_add_fusion.me_ref, s32[160]{0:T(256)S(1)} %bitcast.29, s32[160]{0:T(256)S(1)} %bitcast.30, s32[1]{0:T(128)S(6)} %copy.27.count_ref), custom_call_target="tpu_custom_call" | custom-call | flops 1048576 | bytes 1048576 | tf_op jit(solution)/shard_map/order/pallas_call | solution.py:415
  26.0 12.0 %all-gather = s32[8,1,128]{2,1,0:T(1,128)S(1)} all-gather(s32[1,1,128]{2,1,0:T(1,128)S(1)} %reshape.33), channel_id=1, replica_groups=mesh['y'=4,'z'=8,'core'=2,'x'=4] {'y','core'}, dimensions={0}, use_global_device_ids=true | all-gather | bytes 4608 | tf_op jit(solution)/shard_map/all_gather | solution.py:442
  38.7 7.5 %all-to-all-done.z_ref = bf16[8,4,128,128]{3,2,1,0:T(8,128)(2,1)S(1)} async-done(((bf16[8,4,128,128]{3,2,1,0:T(8,128)(2,1)}), bf16[8,4,128,128]{3,2,1,0:T(8,128)(2,1)S(1)}, u32[]{:S(2)}, u32[]{:S(2)}) %all-to-all-start) | async-done | bytes 1048608 | tf_op jit(solution)/shard_map/all_to_all | solution.py:440
  46.3 2.5 %pick.1 = bf16[64,128,128]{2,1,0:T(8,128)(2,1)} custom-call(s32[3]{0:T(128)S(1)} %pad_add_fusion.me_ref, s32[128]{0:T(128)S(1)} %multiply_add_fusion.idx_ref, bf16[8,4,128,128]{3,2,1,0:T(8,128)(2,1)S(1)} %all-to-all-done.z_ref), custom_call_target="tpu_custom_call" | custom-call | flops 1048576 | bytes 1048576 | tf_op jit(solution)/shard_map/pick/pallas_call | solution.py:445
  48.7 6.6 %all-to-all-start.1 = ((bf16[64,128,128]{2,1,0:T(8,128)(2,1)}), bf16[64,128,128]{2,1,0:T(8,128)(2,1)}, u32[]{:S(2)}, u32[]{:S(2)}) async-start(bf16[64,128,128]{2,1,0:T(8,128)(2,1)} %pick.1), calls=%async_computation.1 | async-start | bytes 4194304 | tf_op jit(solution)/shard_map/all_to_all | solution.py:451
  55.3 1.5 collective-permute-start.8
  56.8 2.4 %collective-permute-start.6 = (s32[8,128]{1,0:T(8,128)S(1)}, s32[8,128]{1,0:T(8,128)S(1)}, u32[]{:S(2)}, u32[]{:S(2)}) collective-permute-start(s32[8,128]{1,0:T(8,128)S(1)} %bitcast.24), channel_id=1, source_target_pairs={{0,16},{8,24},{16,32},{24,40},{32,48},{40,56},{48,0},{56,8},{1,17}... | collective-permute-start | bytes 12296 | tf_op jit(solution)/shard_map/ppermute | solution.py:387
  59.1 1.4 collective-permute-start.5
  60.5 1.9 %collective-permute-start.4 = (s32[8,128]{1,0:T(8,128)S(1)}, s32[8,128]{1,0:T(8,128)S(1)}, u32[]{:S(2)}, u32[]{:S(2)}) collective-permute-start(s32[8,128]{1,0:T(8,128)S(1)} %bitcast.26), channel_id=1, source_target_pairs={{0,24},{8,32},{16,40},{24,48},{32,56},{40,0},{48,8},{56,16},{1,25}... | collective-permute-start | bytes 12296 | tf_op jit(solution)/shard_map/ppermute | solution.py:387
  62.4 2.1 %collective-permute-start.3 = (s32[8,128]{1,0:T(8,128)S(1)}, s32[8,128]{1,0:T(8,128)S(1)}, u32[]{:S(2)}, u32[]{:S(2)}) collective-permute-start(s32[8,128]{1,0:T(8,128)S(1)} %bitcast.27), channel_id=1, source_target_pairs={{0,32},{8,40},{16,48},{24,56},{32,0},{40,8},{48,16},{56,24},{1,33}... | collective-permute-start | bytes 12296 | tf_op jit(solution)/shard_map/ppermute | solution.py:387
  64.5 5.0 %own.2.part_ref = f32[4,128,128]{2,1,0:T(8,128)} custom-call(s32[1024]{0:T(1024)} %copy-done.6, bf16[160,128,128]{2,1,0:T(8,128)(2,1)} %tiles_ref.7, bf16[1,4,128,128]{3,2,1,0:T(8,128)(2,1)} %copy-done.2, f32[2,64,1024]{2,1,0:T(8,128)} %bitcast.31), custom_call_target="tpu_custom_call" | custom-call | flops 671088640 | bytes 4194304 | tf_op jit(solution)/shard_map/own/pallas_call | solution.py:454
  69.6 12.0 %all-to-all-done.1.got_ref = bf16[64,128,128]{2,1,0:T(8,128)(2,1)} async-done(((bf16[64,128,128]{2,1,0:T(8,128)(2,1)}), bf16[64,128,128]{2,1,0:T(8,128)(2,1)}, u32[]{:S(2)}, u32[]{:S(2)}) %all-to-all-start.1) | async-done | bytes 2097184 | tf_op jit(solution)/shard_map/all_to_all | solution.py:451
  81.6 5.9 %far.2 = (f32[4,128,128]{2,1,0:T(8,128)}, f32[8,128]{1,0:T(8,128)}) custom-call(s32[1024]{0:T(1024)} %copy-done.6, bf16[160,128,128]{2,1,0:T(8,128)(2,1)} %tiles_ref.7, bf16[64,128,128]{2,1,0:T(8,128)(2,1)} %all-to-all-done.1.got_ref, f32[4,128,128]{2,1,0:T(8,128)} %own.2.part_ref), custom_call_target="tpu_custom_call" | custom-call | flops 671088640 | bytes 8388608 | tf_op jit(solution)/shard_map/far/pallas_call | solution.py:473
  87.5 2.9 %collective-permute-start.12 = (f32[8,128]{1,0:T(8,128)}, f32[8,128]{1,0:T(8,128)S(1)}, u32[]{:S(2)}, u32[]{:S(2)}) collective-permute-start(f32[8,128]{1,0:T(8,128)} %get-tuple-element.68.refs_9_), channel_id=1, source_target_pairs={{0,3},{1,0},{2,1},{3,2},{4,7},{5,4},{6,5},{7,6},{8,11},{9,8},{10,9... | collective-permute-start | bytes 12296 | tf_op jit(solution)/shard_map/ppermute | solution.py:387
  91.7 2.6 %collective-permute-done.11.refs_11_ = f32[8,128]{1,0:T(8,128)S(1)} collective-permute-done((f32[8,128]{1,0:T(8,128)}, f32[8,128]{1,0:T(8,128)S(1)}, u32[]{:S(2)}, u32[]{:S(2)}) %collective-permute-start.11) | collective-permute-done | bytes 4128 | tf_op jit(solution)/shard_map/ppermute | solution.py:387
  96.3 3.8 %send.1 = (bf16[64,128,128]{2,1,0:T(8,128)(2,1)}, bf16[2,4,128,128]{3,2,1,0:T(8,128)(2,1)}) custom-call(s32[3]{0:T(128)S(1)} %pad_add_fusion.me_ref, s32[8,128]{1,0:T(8,128)S(1)} %bitcast.28, s32[8,128]{1,0:T(8,128)S(1)} %collective-permute-done.3.refs_1_, s32[8,128]{1,0:T(8,128)S(1)} %collective-permute-done.4.refs_2_, ...), custom_call_target="tpu_custom_call" | custom-call | flops 1048576 | bytes 1048576 | tf_op jit(solution)/shard_map/send/pallas_call | solution.py:426
  100.1 8.0 %all-to-all-start.2 = ((bf16[64,128,128]{2,1,0:T(8,128)(2,1)}), bf16[64,128,128]{2,1,0:T(8,128)(2,1)}, u32[]{:S(2)}, u32[]{:S(2)}) async-start(bf16[64,128,128]{2,1,0:T(8,128)(2,1)} %get-tuple-element.71), calls=%async_computation.2 | async-start | bytes 4194304 | tf_op jit(solution)/shard_map/all_to_all | solution.py:432
  108.1 3.0 %collective-permute-start.15 = (bf16[2,4,128,128]{3,2,1,0:T(8,128)(2,1)}, bf16[2,4,128,128]{3,2,1,0:T(8,128)(2,1)}, u32[]{:S(2)}, u32[]{:S(2)}) collective-permute-start(bf16[2,4,128,128]{3,2,1,0:T(8,128)(2,1)} %get-tuple-element.69.refs_0_.own_ref), channel_id=1, source_target_pairs={{0,3},{1,0},{2,1},{3,2},{4,7},{5,4},{6,5},{7,6},{8,11},{9,8},{10,9... | collective-permute-start | bytes 786440 | tf_op jit(solution)/shard_map/ppermute | solution.py:387
  112.7 5.0 %own.3.part_ref = f32[4,128,128]{2,1,0:T(8,128)} custom-call(s32[1024]{0:T(1024)} %copy-done.6, bf16[160,128,128]{2,1,0:T(8,128)(2,1)} %tiles_ref.7, bf16[2,4,128,128]{3,2,1,0:T(8,128)(2,1)} %get-tuple-element.69.refs_0_.own_ref, f32[2,64,1024]{2,1,0:T(8,128)} %bitcast.32), custom_call_target="tpu_custom_call" | custom-call | flops 671088640 | bytes 4194304 | tf_op jit(solution)/shard_map/own/pallas_call | solution.py:454
  117.7 4.3 %collective-permute-done.15.refs_3_ = bf16[2,4,128,128]{3,2,1,0:T(8,128)(2,1)} collective-permute-done((bf16[2,4,128,128]{3,2,1,0:T(8,128)(2,1)}, bf16[2,4,128,128]{3,2,1,0:T(8,128)(2,1)}, u32[]{:S(2)}, u32[]{:S(2)}) %collective-permute-start.15) | collective-permute-done | bytes 262176 | tf_op jit(solution)/shard_map/ppermute | solution.py:387
  122.0 2.2 %collective-permute-done.13.refs_1_ = bf16[2,4,128,128]{3,2,1,0:T(8,128)(2,1)} collective-permute-done((bf16[2,4,128,128]{3,2,1,0:T(8,128)(2,1)}, bf16[2,4,128,128]{3,2,1,0:T(8,128)(2,1)}, u32[]{:S(2)}, u32[]{:S(2)}) %collective-permute-start.13) | collective-permute-done | bytes 262176 | tf_op jit(solution)/shard_map/ppermute | solution.py:387
  124.2 1.6 early.1.early_ref
  125.9 34.1 %all-to-all-done.2.got_ref = bf16[64,128,128]{2,1,0:T(8,128)(2,1)} async-done(((bf16[64,128,128]{2,1,0:T(8,128)(2,1)}), bf16[64,128,128]{2,1,0:T(8,128)(2,1)}, u32[]{:S(2)}, u32[]{:S(2)}) %all-to-all-start.2) | async-done | bytes 2097184 | tf_op jit(solution)/shard_map/all_to_all | solution.py:432
  159.9 6.0 %far.3.refs_0_ = bf16[544,128]{1,0:T(8,128)(2,1)} custom-call(s32[1024]{0:T(1024)} %copy-done.6, bf16[160,128,128]{2,1,0:T(8,128)(2,1)} %tiles_ref.7, bf16[64,128,128]{2,1,0:T(8,128)(2,1)} %all-to-all-done.2.got_ref, f32[4,128,128]{2,1,0:T(8,128)} %own.3.part_ref), custom_call_target="tpu_custom_call" | custom-call | flops 671088640 | bytes 8388608 | tf_op jit(solution)/shard_map/far/pallas_call | solution.py:473
  165.9 3.0 %collective-permute-start.18 = (bf16[544,128]{1,0:T(8,128)(2,1)}, bf16[544,128]{1,0:T(8,128)(2,1)S(1)}, u32[]{:S(2)}, u32[]{:S(2)}) collective-permute-start(bf16[544,128]{1,0:T(8,128)(2,1)} %far.3.refs_0_), channel_id=1, source_target_pairs={{0,3},{1,0},{2,1},{3,2},{4,7},{5,4},{6,5},{7,6},{8,11},{9,8},{10,9... | collective-permute-start | bytes 417800 | tf_op jit(solution)/shard_map/ppermute | solution.py:387
  170.2 2.5 %collective-permute-done.18.refs_3_ = bf16[544,128]{1,0:T(8,128)(2,1)S(1)} collective-permute-done((bf16[544,128]{1,0:T(8,128)(2,1)}, bf16[544,128]{1,0:T(8,128)(2,1)S(1)}, u32[]{:S(2)}, u32[]{:S(2)}) %collective-permute-start.18) | collective-permute-done | bytes 139296 | tf_op jit(solution)/shard_map/ppermute | solution.py:387
  172.7 6.1 %collective-permute-done.17.refs_2_ = bf16[544,128]{1,0:T(8,128)(2,1)S(1)} collective-permute-done((bf16[544,128]{1,0:T(8,128)(2,1)}, bf16[544,128]{1,0:T(8,128)(2,1)S(1)}, u32[]{:S(2)}, u32[]{:S(2)}) %collective-permute-start.17) | collective-permute-done | bytes 139296 | tf_op jit(solution)/shard_map/ppermute | solution.py:387
  (65 shorter events, 12.1 us)
Async XLA Ops:
  0.0 112.4 %copy-start = (bf16[3,256,256]{2,1,0:T(8,128)(2,1)S(1)}, bf16[3,256,256]{2,1,0:T(8,128)(2,1)}, u32[]{:S(2)}) copy-start(bf16[3,256,256]{2,1,0:T(8,128)(2,1)} %param.15) | copy-start | bytes 1179652
  0.0 19.8 %copy-start.8 = (s32[1,160]{1,0:T(1,128)S(1)}, s32[1,160]{1,0:T(1,128)}, u32[]{:S(2)}) copy-start(s32[1,160]{1,0:T(1,128)} %param.10) | copy-start | bytes 1924
  0.0 1.0 copy-start.5
  1.0 18.8 %copy-start.9 = (s32[1,160]{1,0:T(1,128)S(1)}, s32[1,160]{1,0:T(1,128)}, u32[]{:S(2)}) copy-start(s32[1,160]{1,0:T(1,128)} %param.11) | copy-start | bytes 1924
  1.0 24.8 %copy-start.10 = (s32[1,64,2]{1,2,0:T(2,128)S(1)}, s32[1,64,2]{1,2,0:T(2,128)}, u32[]{:S(2)}) copy-start(s32[1,64,2]{1,2,0:T(2,128)} %param.13) | copy-start | bytes 1540
  1.1 5.1 %collective-permute-start.2 = (f32[8,128]{1,0:T(8,128)S(1)}, f32[8,128]{1,0:T(8,128)S(1)}, u32[]{:S(2)}, u32[]{:S(2)}) collective-permute-start(f32[8,128]{1,0:T(8,128)S(1)} %get-tuple-element.44.refs_0_), channel_id=1, source_target_pairs={{0,3},{1,0},{2,1},{3,2},{4,7},{5,4},{6,5},{7,6},{8,11},{9,8},{10,9... | collective-permute-start | bytes 12296 | tf_op jit(solution)/shard_map/ppermute | solution.py:387
  4.5 3.7 %collective-permute-start.1 = (f32[8,128]{1,0:T(8,128)S(1)}, f32[8,128]{1,0:T(8,128)S(1)}, u32[]{:S(2)}, u32[]{:S(2)}) collective-permute-start(f32[8,128]{1,0:T(8,128)S(1)} %get-tuple-element.44.refs_0_), channel_id=1, source_target_pairs={{0,1},{1,2},{2,3},{3,0},{4,5},{5,6},{6,7},{7,4},{8,9},{9,10},{10,1... | collective-permute-start | bytes 12296 | tf_op jit(solution)/shard_map/ppermute | solution.py:387
  4.5 4.0 %collective-permute-start = (f32[8,128]{1,0:T(8,128)S(1)}, f32[8,128]{1,0:T(8,128)S(1)}, u32[]{:S(2)}, u32[]{:S(2)}) collective-permute-start(f32[8,128]{1,0:T(8,128)S(1)} %get-tuple-element.44.refs_0_), channel_id=1, source_target_pairs={{0,2},{1,3},{2,0},{3,1},{4,6},{5,7},{6,4},{7,5},{8,10},{9,11},{10,... | collective-permute-start | bytes 12296 | tf_op jit(solution)/shard_map/ppermute | solution.py:387
  9.8 0.7 copy-start.2
  10.5 35.8 %all-to-all-start = ((bf16[8,4,128,128]{3,2,1,0:T(8,128)(2,1)}), bf16[8,4,128,128]{3,2,1,0:T(8,128)(2,1)S(1)}, u32[]{:S(2)}, u32[]{:S(2)}) async-start(bf16[8,4,128,128]{3,2,1,0:T(8,128)(2,1)} %get-tuple-element.54), calls=%async_computation | async-start | bytes 2097152 | tf_op jit(solution)/shard_map/all_to_all | solution.py:440
  48.7 32.9 %all-to-all-start.1 = ((bf16[64,128,128]{2,1,0:T(8,128)(2,1)}), bf16[64,128,128]{2,1,0:T(8,128)(2,1)}, u32[]{:S(2)}, u32[]{:S(2)}) async-start(bf16[64,128,128]{2,1,0:T(8,128)(2,1)} %pick.1), calls=%async_computation.1 | async-start | bytes 4194304 | tf_op jit(solution)/shard_map/all_to_all | solution.py:451
  55.3 5.2 %collective-permute-start.9 = (s32[8,128]{1,0:T(8,128)S(1)}, s32[8,128]{1,0:T(8,128)S(1)}, u32[]{:S(2)}, u32[]{:S(2)}) collective-permute-start(s32[8,128]{1,0:T(8,128)S(1)} %bitcast.21), channel_id=1, source_target_pairs={{0,56},{8,0},{16,8},{24,16},{32,24},{40,32},{48,40},{56,48},{1,57}... | collective-permute-start | bytes 12296 | tf_op jit(solution)/shard_map/ppermute | solution.py:387
  55.3 7.1 %collective-permute-start.8 = (s32[8,128]{1,0:T(8,128)S(1)}, s32[8,128]{1,0:T(8,128)S(1)}, u32[]{:S(2)}, u32[]{:S(2)}) collective-permute-start(s32[8,128]{1,0:T(8,128)S(1)} %bitcast.22), channel_id=1, source_target_pairs={{0,8},{8,16},{16,24},{24,32},{32,40},{40,48},{48,56},{56,0},{1,9},... | collective-permute-start | bytes 12296 | tf_op jit(solution)/shard_map/ppermute | solution.py:387
  56.8 12.8 %collective-permute-start.7 = (s32[8,128]{1,0:T(8,128)S(1)}, s32[8,128]{1,0:T(8,128)S(1)}, u32[]{:S(2)}, u32[]{:S(2)}) collective-permute-start(s32[8,128]{1,0:T(8,128)S(1)} %bitcast.23), channel_id=1, source_target_pairs={{0,48},{8,56},{16,0},{24,8},{32,16},{40,24},{48,32},{56,40},{1,49}... | collective-permute-start | bytes 12296 | tf_op jit(solution)/shard_map/ppermute | solution.py:387
  56.8 12.8 %collective-permute-start.6 = (s32[8,128]{1,0:T(8,128)S(1)}, s32[8,128]{1,0:T(8,128)S(1)}, u32[]{:S(2)}, u32[]{:S(2)}) collective-permute-start(s32[8,128]{1,0:T(8,128)S(1)} %bitcast.24), channel_id=1, source_target_pairs={{0,16},{8,24},{16,32},{24,40},{32,48},{40,56},{48,0},{56,8},{1,17}... | collective-permute-start | bytes 12296 | tf_op jit(solution)/shard_map/ppermute | solution.py:387
  59.1 10.5 %collective-permute-start.5 = (s32[8,128]{1,0:T(8,128)S(1)}, s32[8,128]{1,0:T(8,128)S(1)}, u32[]{:S(2)}, u32[]{:S(2)}) collective-permute-start(s32[8,128]{1,0:T(8,128)S(1)} %bitcast.25), channel_id=1, source_target_pairs={{0,40},{8,48},{16,56},{24,0},{32,8},{40,16},{48,24},{56,32},{1,41}... | collective-permute-start | bytes 12296 | tf_op jit(solution)/shard_map/ppermute | solution.py:387
  60.5 9.1 %collective-permute-start.4 = (s32[8,128]{1,0:T(8,128)S(1)}, s32[8,128]{1,0:T(8,128)S(1)}, u32[]{:S(2)}, u32[]{:S(2)}) collective-permute-start(s32[8,128]{1,0:T(8,128)S(1)} %bitcast.26), channel_id=1, source_target_pairs={{0,24},{8,32},{16,40},{24,48},{32,56},{40,0},{48,8},{56,16},{1,25}... | collective-permute-start | bytes 12296 | tf_op jit(solution)/shard_map/ppermute | solution.py:387
  62.4 7.2 %collective-permute-start.3 = (s32[8,128]{1,0:T(8,128)S(1)}, s32[8,128]{1,0:T(8,128)S(1)}, u32[]{:S(2)}, u32[]{:S(2)}) collective-permute-start(s32[8,128]{1,0:T(8,128)S(1)} %bitcast.27), channel_id=1, source_target_pairs={{0,32},{8,40},{16,48},{24,56},{32,0},{40,8},{48,16},{56,24},{1,33}... | collective-permute-start | bytes 12296 | tf_op jit(solution)/shard_map/ppermute | solution.py:387
  69.6 25.1 %copy-start.3 = (bf16[1,4,128,128]{3,2,1,0:T(8,128)(2,1)S(1)}, bf16[1,4,128,128]{3,2,1,0:T(8,128)(2,1)}, u32[]{:S(2)}) copy-start(bf16[1,4,128,128]{3,2,1,0:T(8,128)(2,1)} %copy-done.2) | copy-start | bytes 393220
  87.5 4.2 %collective-permute-start.12 = (f32[8,128]{1,0:T(8,128)}, f32[8,128]{1,0:T(8,128)S(1)}, u32[]{:S(2)}, u32[]{:S(2)}) collective-permute-start(f32[8,128]{1,0:T(8,128)} %get-tuple-element.68.refs_9_), channel_id=1, source_target_pairs={{0,3},{1,0},{2,1},{3,2},{4,7},{5,4},{6,5},{7,6},{8,11},{9,8},{10,9... | collective-permute-start | bytes 12296 | tf_op jit(solution)/shard_map/ppermute | solution.py:387
  90.5 3.9 %collective-permute-start.11 = (f32[8,128]{1,0:T(8,128)}, f32[8,128]{1,0:T(8,128)S(1)}, u32[]{:S(2)}, u32[]{:S(2)}) collective-permute-start(f32[8,128]{1,0:T(8,128)} %get-tuple-element.68.refs_9_), channel_id=1, source_target_pairs={{0,1},{1,2},{2,3},{3,0},{4,5},{5,6},{6,7},{7,4},{8,9},{9,10},{10,1... | collective-permute-start | bytes 12296 | tf_op jit(solution)/shard_map/ppermute | solution.py:387
  90.5 4.2 %collective-permute-start.10 = (f32[8,128]{1,0:T(8,128)}, f32[8,128]{1,0:T(8,128)S(1)}, u32[]{:S(2)}, u32[]{:S(2)}) collective-permute-start(f32[8,128]{1,0:T(8,128)} %get-tuple-element.68.refs_9_), channel_id=1, source_target_pairs={{0,2},{1,3},{2,0},{3,1},{4,6},{5,7},{6,4},{7,5},{8,10},{9,11},{10,... | collective-permute-start | bytes 12296 | tf_op jit(solution)/shard_map/ppermute | solution.py:387
  94.6 1.0 copy-start.4
  95.6 0.7 copy-start.7
  100.1 59.8 %all-to-all-start.2 = ((bf16[64,128,128]{2,1,0:T(8,128)(2,1)}), bf16[64,128,128]{2,1,0:T(8,128)(2,1)}, u32[]{:S(2)}, u32[]{:S(2)}) async-start(bf16[64,128,128]{2,1,0:T(8,128)(2,1)} %get-tuple-element.71), calls=%async_computation.2 | async-start | bytes 4194304 | tf_op jit(solution)/shard_map/all_to_all | solution.py:432
  108.1 13.9 %collective-permute-start.15 = (bf16[2,4,128,128]{3,2,1,0:T(8,128)(2,1)}, bf16[2,4,128,128]{3,2,1,0:T(8,128)(2,1)}, u32[]{:S(2)}, u32[]{:S(2)}) collective-permute-start(bf16[2,4,128,128]{3,2,1,0:T(8,128)(2,1)} %get-tuple-element.69.refs_0_.own_ref), channel_id=1, source_target_pairs={{0,3},{1,0},{2,1},{3,2},{4,7},{5,4},{6,5},{7,6},{8,11},{9,8},{10,9... | collective-permute-start | bytes 786440 | tf_op jit(solution)/shard_map/ppermute | solution.py:387
  111.2 10.9 %collective-permute-start.14 = (bf16[2,4,128,128]{3,2,1,0:T(8,128)(2,1)}, bf16[2,4,128,128]{3,2,1,0:T(8,128)(2,1)}, u32[]{:S(2)}, u32[]{:S(2)}) collective-permute-start(bf16[2,4,128,128]{3,2,1,0:T(8,128)(2,1)} %get-tuple-element.69.refs_0_.own_ref), channel_id=1, source_target_pairs={{0,1},{1,2},{2,3},{3,0},{4,5},{5,6},{6,7},{7,4},{8,9},{9,10},{10,1... | collective-permute-start | bytes 786440 | tf_op jit(solution)/shard_map/ppermute | solution.py:387
  111.2 13.1 %collective-permute-start.13 = (bf16[2,4,128,128]{3,2,1,0:T(8,128)(2,1)}, bf16[2,4,128,128]{3,2,1,0:T(8,128)(2,1)}, u32[]{:S(2)}, u32[]{:S(2)}) collective-permute-start(bf16[2,4,128,128]{3,2,1,0:T(8,128)(2,1)} %get-tuple-element.69.refs_0_.own_ref), channel_id=1, source_target_pairs={{0,2},{1,3},{2,0},{3,1},{4,6},{5,7},{6,4},{7,5},{8,10},{9,11},{10,... | collective-permute-start | bytes 786440 | tf_op jit(solution)/shard_map/ppermute | solution.py:387
  165.9 6.8 %collective-permute-start.18 = (bf16[544,128]{1,0:T(8,128)(2,1)}, bf16[544,128]{1,0:T(8,128)(2,1)S(1)}, u32[]{:S(2)}, u32[]{:S(2)}) collective-permute-start(bf16[544,128]{1,0:T(8,128)(2,1)} %far.3.refs_0_), channel_id=1, source_target_pairs={{0,3},{1,0},{2,1},{3,2},{4,7},{5,4},{6,5},{7,6},{8,11},{9,8},{10,9... | collective-permute-start | bytes 417800 | tf_op jit(solution)/shard_map/ppermute | solution.py:387
  168.9 9.9 %collective-permute-start.17 = (bf16[544,128]{1,0:T(8,128)(2,1)}, bf16[544,128]{1,0:T(8,128)(2,1)S(1)}, u32[]{:S(2)}, u32[]{:S(2)}) collective-permute-start(bf16[544,128]{1,0:T(8,128)(2,1)} %far.3.refs_0_), channel_id=1, source_target_pairs={{0,1},{1,2},{2,3},{3,0},{4,5},{5,6},{6,7},{7,4},{8,9},{9,10},{10,1... | collective-permute-start | bytes 417800 | tf_op jit(solution)/shard_map/ppermute | solution.py:387
  168.9 9.9 %collective-permute-start.16 = (bf16[544,128]{1,0:T(8,128)(2,1)}, bf16[544,128]{1,0:T(8,128)(2,1)S(1)}, u32[]{:S(2)}, u32[]{:S(2)}) collective-permute-start(bf16[544,128]{1,0:T(8,128)(2,1)} %far.3.refs_0_), channel_id=1, source_target_pairs={{0,2},{1,3},{2,0},{3,1},{4,6},{5,7},{6,4},{7,5},{8,10},{9,11},{10,... | collective-permute-start | bytes 417800 | tf_op jit(solution)/shard_map/ppermute | solution.py:387
  178.8 0.9 copy-start.1
  (1 other events, 0.6 us)
